TPU v7x, 128 devices: a whole 4x4x4 slice. The times are simulated.
128 devices in a mesh: head: 2 (over core), seq: 64 (over x, z, y).
Axes of the slice: x: 4, y: 4, z: 4, core: 2. Of those that a mesh axis runs over, the one named last changes fastest.
Arguments:
- queries: bfloat16 [32768, 5120], P(('seq', 'head')), may hold values from -8 to 8
- key_states: bfloat16 [32768, 5120], P(('seq', 'head')), may hold values from -8 to 8
- value_states: bfloat16 [32768, 5120], P(('seq', 'head')), may hold values from -6 to 6
- cluster_perm: int32 [40, 32768], P('head', 'seq'), may hold values from 0 to 32767, as said below
- block_mask: int32 [40, 256, 256], P('head', 'seq'), may hold values from 0 to 1, as said below
Outputs:
- attention_out: bfloat16 [32768, 5120], P(('seq', 'head'))
Inputs may be any that keep to these rules, and one draw needn't show every extreme that they name: `cluster_perm`: for each head, positions k * 512 to (k + 1) * 512 - 1 list the tokens k * 512 to (k + 1) * 512 - 1, each once. `block_mask`: for each head and each aligned run of 4 query blocks, the key blocks used by some query block of the run number exactly 4. For such a run and the 20 heads g * 20 to (g + 1) * 20 - 1, the (head, key block) pairs so used that lie in one aligned run of 4 key blocks number at most 2, and exactly 2 in some run. Every query block uses 1 to 4 key blocks, and some query block of every run uses 4, for every head.
All inputs are finite; a program needn't handle non-finite values.
Results may differ from a plain program's by a relative error of at most 0.0049.
Values may be sent and summed in bfloat16 or wider, within the bound.
No kernel may reach another device: no remote copies, remote signals or barrier semaphores. Data moves between devices by JAX's collectives and lax.ppermute only.
A program may use at most 128 MiB of HBM per device.

v0:
```python
import math

import jax
import jax.numpy as jnp
from jax import lax
from jax.sharding import PartitionSpec as P

HEAD_DIM = 128
BLOCK = 128


def shards(queries, key_states, value_states, cluster_perm, block_mask):
    group_heads = cluster_perm.shape[0]
    shard_rows = cluster_perm.shape[1]
    shard_blocks = shard_rows // BLOCK
    seq_count = lax.axis_size("seq")
    block_total = block_mask.shape[2]
    pick_count = max(1, block_total // 64)
    capacity = max(
        1, min(shard_blocks, (group_heads * pick_count * 8 + 5 * seq_count - 1) // (5 * seq_count))
    )
    pair_count = group_heads * shard_blocks
    slot_total = seq_count * capacity
    score_scale = 1.0 / math.sqrt(HEAD_DIM)
    query_rows, key_rows, value_rows = (
        lax.all_to_all(queries, "head", split_axis=1, concat_axis=0, tiled=True),
        lax.all_to_all(key_states, "head", split_axis=1, concat_axis=0, tiled=True),
        lax.all_to_all(value_states, "head", split_axis=1, concat_axis=0, tiled=True),
    )
    local_perm = cluster_perm - lax.axis_index("seq") * shard_rows
    row_ids = jnp.arange(shard_rows, dtype=jnp.int32)
    order_table = (local_perm[:, :, None] == row_ids[None, None, :]).astype(jnp.bfloat16)
    stacked = jnp.concatenate(
        [
            query_rows.reshape(shard_rows, group_heads, HEAD_DIM),
            key_rows.reshape(shard_rows, group_heads, HEAD_DIM),
            value_rows.reshape(shard_rows, group_heads, HEAD_DIM),
        ],
        axis=2,
    )
    sorted_all = jnp.einsum(
        "hit,thd->hid", order_table, stacked, preferred_element_type=jnp.float32
    ).astype(jnp.bfloat16)
    query_sorted = sorted_all[:, :, :HEAD_DIM]
    key_sorted = sorted_all[:, :, HEAD_DIM : 2 * HEAD_DIM]
    value_sorted = sorted_all[:, :, 2 * HEAD_DIM :]
    needed = jnp.max(block_mask, axis=1)
    by_owner = needed.reshape(group_heads, seq_count, shard_blocks)
    requested = lax.all_to_all(by_owner, "seq", split_axis=1, concat_axis=1, tiled=True)

    def slot_ranks(bit_table):
        flat_bits = bit_table.transpose(1, 0, 2).reshape(seq_count, pair_count)
        return (flat_bits, jnp.cumsum(flat_bits, axis=1) - flat_bits)

    asked_bits, asked_rank = slot_ranks(requested)
    cap_ids = jnp.arange(capacity, dtype=jnp.int32)
    matches = (asked_bits[:, :, None] == 1) & (asked_rank[:, :, None] == cap_ids[None, None, :])
    send_table = matches.transpose(0, 2, 1).astype(jnp.bfloat16)
    block_width = BLOCK * HEAD_DIM
    kv_pairs = jnp.concatenate(
        [
            key_sorted.reshape(pair_count, block_width),
            value_sorted.reshape(pair_count, block_width),
        ],
        axis=1,
    )
    kv_send = jnp.einsum(
        "scp,pw->scw", send_table, kv_pairs, preferred_element_type=jnp.float32
    ).astype(jnp.bfloat16)
    key_send = kv_send[:, :, :block_width].reshape(seq_count, capacity, BLOCK, HEAD_DIM)
    value_send = kv_send[:, :, block_width:].reshape(seq_count, capacity, BLOCK, HEAD_DIM)
    own_bits, own_rank = slot_ranks(by_owner)
    prefix = jnp.cumsum(needed, axis=1) - needed
    chosen = (needed[:, :, None] == 1) & (
        prefix[:, :, None] == jnp.arange(pick_count, dtype=jnp.int32)[None, None, :]
    )
    picked = jnp.sum(
        jnp.where(chosen, jnp.arange(block_total, dtype=jnp.int32)[None, :, None], 0), axis=1
    )
    owner_idx = picked // shard_blocks
    pair_idx = (
        jnp.arange(group_heads, dtype=jnp.int32)[:, None] * shard_blocks + picked % shard_blocks
    )
    slot_idx = jnp.take(own_rank.reshape(-1), owner_idx * pair_count + pair_idx)
    position = owner_idx * capacity + slot_idx
    live_bits = jnp.take_along_axis(block_mask, picked[:, None, :], axis=2)
    query_blocks = query_sorted.reshape(group_heads, shard_blocks, BLOCK, HEAD_DIM)
    usable = live_bits == 1
    score_form = "qid,pjd->qipj"
    mix_form = "qipj,pjd->qid"
    slot_ids = jnp.arange(slot_total, dtype=jnp.int32)

    def select_blocks(got_flat, slot_head):
        pick_table = (slot_head[..., None] == slot_ids).astype(jnp.bfloat16)
        chosen_rows = jnp.einsum(
            "...s,sw->...w", pick_table, got_flat, preferred_element_type=jnp.float32
        ).astype(jnp.bfloat16)
        return chosen_rows.reshape(slot_head.shape + (BLOCK, HEAD_DIM))

    def head_scores(query_head, key_got, slot_head, usable_head):
        key_sel = select_blocks(key_got, slot_head)
        scores = (
            jnp.einsum(score_form, query_head, key_sel, preferred_element_type=jnp.float32)
            * score_scale
        )
        return jnp.where(usable_head[:, None, :, None], scores, -jnp.inf)

    def head_mix(weights, value_got, slot_head):
        value_sel = select_blocks(value_got, slot_head)
        return jnp.einsum(mix_form, weights, value_sel, preferred_element_type=jnp.float32).astype(
            jnp.bfloat16
        )

    flat_shape = (slot_total, block_width)
    key_got, value_got = (
        lax.all_to_all(key_send, "seq", split_axis=0, concat_axis=0, tiled=True),
        lax.all_to_all(value_send, "seq", split_axis=0, concat_axis=0, tiled=True),
    )
    key_got = key_got.reshape(flat_shape)
    value_got = value_got.reshape(flat_shape)

    def full_pass(operands):
        query_head, slot_head, usable_head = operands
        scores = head_scores(query_head, key_got, slot_head, usable_head)
        row_top = jnp.max(scores, axis=(2, 3), keepdims=True)
        exponent = jnp.exp(scores - row_top)
        row_total = jnp.sum(exponent, axis=(2, 3), keepdims=True)
        weights = (exponent / row_total).astype(jnp.bfloat16)
        return head_mix(weights, value_got, slot_head)

    attended = lax.map(full_pass, (query_blocks, position, usable))
    attended_flat = attended.reshape(group_heads, shard_rows, HEAD_DIM)
    restored = jnp.einsum(
        "hit,hid->thd", order_table, attended_flat, preferred_element_type=jnp.float32
    ).astype(jnp.bfloat16)
    out_rows = restored.reshape(shard_rows, group_heads * HEAD_DIM)
    return lax.all_to_all(out_rows, "head", split_axis=0, concat_axis=1, tiled=True)


def solution(mesh):
    placed = (
        P(("seq", "head"), None),
        P(("seq", "head"), None),
        P(("seq", "head"), None),
        P("head", "seq"),
        P("head", "seq", None),
    )
    return jax.shard_map(
        shards, mesh=mesh, in_specs=placed, out_specs=P(("seq", "head"), None), check_vma=False
    )
```

profile of v0, /device:TPU:103, one launch (start us, length us, event | category | flops | bytes accessed | tf_op | source)
XLA Modules:
  0.0 414.0 jit_solution(14078010110601934045)
XLA Ops:
  0.0 4.4 %copy.79 = bf16[256,5120]{0,1:T(8,128)(2,1)} copy(bf16[256,5120]{1,0:T(8,128)(2,1)} %param.7) | data formatting | bytes 5242880 | tf_op args[0]
  4.4 4.7 %all-to-all-start = ((bf16[256,2,2560]{0,2,1:T(8,128)(2,1)}), bf16[256,2,2560]{0,2,1:T(8,128)(2,1)S(1)}, u32[]{:S(2)}, u32[]{:S(2)}) async-start(bf16[256,2,2560]{0,2,1:T(8,128)(2,1)} %bitcast.157), calls=%async_computation | async-start | bytes 5242880 | tf_op jit(solution)/shard_map/all_to_all | solution.py:26
  9.9 4.4 %copy.81 = bf16[256,5120]{0,1:T(8,128)(2,1)} copy(bf16[256,5120]{1,0:T(8,128)(2,1)} %param.8) | data formatting | bytes 5242880 | tf_op args[1]
  14.3 5.0 %all-to-all-start.1 = ((bf16[256,2,2560]{0,2,1:T(8,128)(2,1)}), bf16[256,2,2560]{0,2,1:T(8,128)(2,1)}, u32[]{:S(2)}, u32[]{:S(2)}) async-start(bf16[256,2,2560]{0,2,1:T(8,128)(2,1)} %bitcast.155), calls=%async_computation.1 | async-start | bytes 5242880 | tf_op jit(solution)/shard_map/all_to_all | solution.py:27
  19.3 17.3 %copy.80 = bf16[2,256,2560]{1,0,2:T(2,128)(2,1)} copy(bf16[2,256,2560]{1,2,0:T(8,128)(2,1)S(1)} %bitcast.153) | data formatting | bytes 5242880 | tf_op jit(solution)/shard_map/all_to_all | solution.py:26
  36.6 4.2 %reshape.273 = bf16[512,20,128]{0,2,1:T(8,128)(2,1)S(1)} reshape(bf16[2,256,2560]{1,0,2:T(2,128)(2,1)} %copy.80) | data formatting | bytes 5242880 | tf_op jit(solution)/shard_map/reshape | solution.py:35
  43.3 4.4 %copy.83 = bf16[256,5120]{0,1:T(8,128)(2,1)} copy(bf16[256,5120]{1,0:T(8,128)(2,1)} %param.9) | data formatting | bytes 5242880 | tf_op args[2]
  51.6 7.0 %copy.82 = bf16[2,256,2560]{1,0,2:T(2,128)(2,1)} copy(bf16[2,256,2560]{1,2,0:T(8,128)(2,1)} %bitcast.6) | data formatting | bytes 5242880 | tf_op jit(solution)/shard_map/all_to_all | solution.py:27
  58.5 5.3 %reshape.274 = bf16[512,20,128]{0,2,1:T(8,128)(2,1)} reshape(bf16[2,256,2560]{1,0,2:T(2,128)(2,1)} %copy.82) | data formatting | bytes 5242880 | tf_op jit(solution)/shard_map/reshape | solution.py:36
  63.9 4.4 %copy.86 = bf16[512,20,128]{2,0,1:T(8,128)(2,1)} copy(bf16[512,20,128]{0,2,1:T(8,128)(2,1)} %reshape.274) | data formatting | bytes 5242880 | tf_op jit(solution)/shard_map/reshape | solution.py:36
  68.3 10.2 %all-to-all-start.3 = ((s32[20,64,4]{0,2,1:T(4,128)}), s32[20,64,4]{0,2,1:T(4,128)S(1)}, u32[]{:S(2)}, u32[]{:S(2)}) async-start(s32[20,64,4]{0,2,1:T(4,128)} %bitcast.10), calls=%async_computation.3 | async-start | bytes 262144 | tf_op jit(solution)/shard_map/all_to_all | solution.py:49
  78.5 17.3 %copy.84 = bf16[2,256,2560]{1,0,2:T(2,128)(2,1)} copy(bf16[2,256,2560]{1,2,0:T(8,128)(2,1)S(1)} %bitcast.154) | data formatting | bytes 5242880 | tf_op jit(solution)/shard_map/all_to_all | solution.py:28
  95.8 4.2 %reshape.275 = bf16[512,20,128]{0,2,1:T(8,128)(2,1)S(1)} reshape(bf16[2,256,2560]{1,0,2:T(2,128)(2,1)} %copy.84) | data formatting | bytes 5242880 | tf_op jit(solution)/shard_map/reshape | solution.py:37
  102.5 7.9 %fusion.30 = bf16[20,512,384]{2,1,0:T(8,128)(2,1)S(1)} fusion(bf16[512,20,128]{2,0,1:T(8,128)(2,1)} %copy.87, bf16[512,20,128]{2,0,1:T(8,128)(2,1)} %copy.86, bf16[512,20,128]{2,0,1:T(8,128)(2,1)} %copy.85, s32[20,512]{1,0:T(8,128)S(1)} %broadcast_subtract_fusion), kind=kOutput, calls=%fused_computation.42 | convolution fusion | flops 4059299840 | bytes 15769600 | tf_op jit(solution)/shard_map/hit,thd->hid/dot_general | solution.py:41
  117.7 5.2 %reshape.281 = bf16[80,16384]{1,0:T(8,128)(2,1)} reshape(bf16[20,512,128]{2,1,0:T(8,128)(2,1)} %get-tuple-element.83) | data formatting | bytes 5242880 | tf_op jit(solution)/shard_map/reshape | solution.py:63
  133.3 10.6 %all-to-all-start.5 = ((bf16[64,2,128,128]{3,2,1,0:T(8,128)(2,1)}), bf16[64,2,128,128]{3,2,1,0:T(8,128)(2,1)}, u32[]{:S(2)}, u32[]{:S(2)}) async-start(bf16[64,2,128,128]{3,2,1,0:T(8,128)(2,1)} %copy.98), calls=%async_computation.5 | async-start | bytes 8388608 | tf_op jit(solution)/shard_map/all_to_all | solution.py:117
  149.7 55.8 %all-to-all-done.5 = bf16[64,2,128,128]{3,2,1,0:T(8,128)(2,1)} async-done(((bf16[64,2,128,128]{3,2,1,0:T(8,128)(2,1)}), bf16[64,2,128,128]{3,2,1,0:T(8,128)(2,1)}, u32[]{:S(2)}, u32[]{:S(2)}) %all-to-all-start.5) | async-done | bytes 4194336 | tf_op jit(solution)/shard_map/all_to_all | solution.py:117
  205.5 7.1 %all-to-all-start.4 = ((bf16[64,2,128,128]{3,2,1,0:T(8,128)(2,1)}), bf16[64,2,128,128]{3,2,1,0:T(8,128)(2,1)}, u32[]{:S(2)}, u32[]{:S(2)}) async-start(bf16[64,2,128,128]{3,2,1,0:T(8,128)(2,1)} %copy.97), calls=%async_computation.4 | async-start | bytes 8388608 | tf_op jit(solution)/shard_map/all_to_all | solution.py:116
  222.7 7.7 %copy.125 = bf16[16,8,128,128]{3,1,2,0:T(8,128)(2,1)} copy(bf16[16,8,128,128]{3,2,1,0:T(8,128)(2,1)} %bitcast.63) | data formatting | bytes 8388608
  230.3 44.0 %all-to-all-done.4 = bf16[64,2,128,128]{3,2,1,0:T(8,128)(2,1)} async-done(((bf16[64,2,128,128]{3,2,1,0:T(8,128)(2,1)}), bf16[64,2,128,128]{3,2,1,0:T(8,128)(2,1)}, u32[]{:S(2)}, u32[]{:S(2)}) %all-to-all-start.4) | async-done | bytes 4194336 | tf_op jit(solution)/shard_map/all_to_all | solution.py:116
  274.3 7.9 %copy.126 = bf16[16,8,128,128]{3,1,2,0:T(8,128)(2,1)} copy(bf16[16,8,128,128]{3,2,1,0:T(8,128)(2,1)} %bitcast.54) | data formatting | bytes 8388608
  282.2 112.7 %while.11 = (s32[]{:T(128)}, bf16[20,4,128,128]{3,2,1,0:T(8,128)(2,1)S(1)}, pred[20,4,4]{2,1,0:T(4,128)(4,1)S(1)}, bf16[20,4,128,128]{3,2,1,0:T(8,128)(2,1)}, s3...) while((s32[]{:T(128)}, ...), condition=%wide.region_9.10_spmd.clone, body=%wide.region_6.9_spmd.clone.sunk | while | flops 170065920 | bytes 29108972 | solution.py:131
  395.0 6.2 %convert_bitcast_fusion = bf16[512,20,128]{0,2,1:T(8,128)(2,1)} fusion(bf16[20,512,128]{2,1,0:T(8,128)(2,1)S(1)} %bitcast.167, s32[20,512]{1,0:T(8,128)S(1)} %copy-done.4), kind=kOutput, calls=%fused_computation.48 | convolution fusion | flops 1348730880 | bytes 5283840 | tf_op jit(solution)/shard_map/hit,hid->thd/dot_general | solution.py:133
  405.1 6.0 %all_to_all.82 = bf16[2,256,2560]{1,2,0:T(8,128)(2,1)S(1)} all-to-all(bf16[2,256,2560]{1,2,0:T(8,128)(2,1)S(1)} %copy.100), channel_id=1, replica_groups=mesh['head'=2,'seq'=64] {'head'}, dimensions={0} | all-to-all | bytes 5242880 | tf_op jit(solution)/shard_map/all_to_all | solution.py:137
  (254 shorter events, 161.5 us)
Async XLA Ops:
  4.4 4.7 %copy-start.1 = (s32[20,4,256]{2,1,0:T(4,128)S(1)}, s32[20,4,256]{2,1,0:T(4,128)}, u32[]{:S(2)}) copy-start(s32[20,4,256]{2,1,0:T(4,128)} %param.11) | copy-start | bytes 245764
  4.4 9.9 %all-to-all-start = ((bf16[256,2,2560]{0,2,1:T(8,128)(2,1)}), bf16[256,2,2560]{0,2,1:T(8,128)(2,1)S(1)}, u32[]{:S(2)}, u32[]{:S(2)}) async-start(bf16[256,2,2560]{0,2,1:T(8,128)(2,1)} %bitcast.157), calls=%async_computation | async-start | bytes 5242880 | tf_op jit(solution)/shard_map/all_to_all | solution.py:26
  14.3 33.4 %all-to-all-start.1 = ((bf16[256,2,2560]{0,2,1:T(8,128)(2,1)}), bf16[256,2,2560]{0,2,1:T(8,128)(2,1)}, u32[]{:S(2)}, u32[]{:S(2)}) async-start(bf16[256,2,2560]{0,2,1:T(8,128)(2,1)} %bitcast.155), calls=%async_computation.1 | async-start | bytes 5242880 | tf_op jit(solution)/shard_map/all_to_all | solution.py:27
  47.7 20.6 %all-to-all-start.2 = ((bf16[256,2,2560]{0,2,1:T(8,128)(2,1)}), bf16[256,2,2560]{0,2,1:T(8,128)(2,1)S(1)}, u32[]{:S(2)}, u32[]{:S(2)}) async-start(bf16[256,2,2560]{0,2,1:T(8,128)(2,1)} %bitcast.156), calls=%async_computation.2 | async-start | bytes 5242880 | tf_op jit(solution)/shard_map/all_to_all | solution.py:28
  68.3 54.6 %all-to-all-start.3 = ((s32[20,64,4]{0,2,1:T(4,128)}), s32[20,64,4]{0,2,1:T(4,128)S(1)}, u32[]{:S(2)}, u32[]{:S(2)}) async-start(s32[20,64,4]{0,2,1:T(4,128)} %bitcast.10), calls=%async_computation.3 | async-start | bytes 262144 | tf_op jit(solution)/shard_map/all_to_all | solution.py:49
  102.5 7.9 %copy-start.3 = (s32[20,512]{1,0:T(8,128)}, s32[20,512]{1,0:T(8,128)S(1)}, u32[]{:S(2)}) copy-start(s32[20,512]{1,0:T(8,128)S(1)} %broadcast_subtract_fusion) | copy-start | bytes 122884
  133.3 72.1 %all-to-all-start.5 = ((bf16[64,2,128,128]{3,2,1,0:T(8,128)(2,1)}), bf16[64,2,128,128]{3,2,1,0:T(8,128)(2,1)}, u32[]{:S(2)}, u32[]{:S(2)}) async-start(bf16[64,2,128,128]{3,2,1,0:T(8,128)(2,1)} %copy.98), calls=%async_computation.5 | async-start | bytes 8388608 | tf_op jit(solution)/shard_map/all_to_all | solution.py:117
  205.5 68.9 %all-to-all-start.4 = ((bf16[64,2,128,128]{3,2,1,0:T(8,128)(2,1)}), bf16[64,2,128,128]{3,2,1,0:T(8,128)(2,1)}, u32[]{:S(2)}, u32[]{:S(2)}) async-start(bf16[64,2,128,128]{3,2,1,0:T(8,128)(2,1)} %copy.97), calls=%async_computation.4 | async-start | bytes 8388608 | tf_op jit(solution)/shard_map/all_to_all | solution.py:116
  274.3 7.9 %copy-start.5 = (bf16[20,4,128,128]{3,2,1,0:T(8,128)(2,1)S(1)}, bf16[20,4,128,128]{3,2,1,0:T(8,128)(2,1)}, u32[]{:S(2)}) copy-start(bf16[20,4,128,128]{3,2,1,0:T(8,128)(2,1)} %custom-call.4) | copy-start | bytes 7864324
  282.2 112.7 %copy-start.4 = (s32[20,512]{1,0:T(8,128)S(1)}, s32[20,512]{1,0:T(8,128)}, u32[]{:S(2)}) copy-start(s32[20,512]{1,0:T(8,128)} %copy-done.3) | copy-start | bytes 122884
  288.0 4.4 %copy-start = (bf16[128,16384]{1,0:T(8,128)(2,1)S(1)}, bf16[128,16384]{1,0:T(8,128)(2,1)}, u32[]{:S(2)}) copy-start(bf16[128,16384]{1,0:T(8,128)(2,1)} %get-tuple-element.156) | copy-start | bytes 12582916 | tf_op jit(solution)/shard_map/while
  293.6 4.4 %copy-start = (bf16[128,16384]{1,0:T(8,128)(2,1)S(1)}, bf16[128,16384]{1,0:T(8,128)(2,1)}, u32[]{:S(2)}) copy-start(bf16[128,16384]{1,0:T(8,128)(2,1)} %get-tuple-element.156) | copy-start | bytes 12582916 | tf_op jit(solution)/shard_map/while
  299.3 4.4 %copy-start = (bf16[128,16384]{1,0:T(8,128)(2,1)S(1)}, bf16[128,16384]{1,0:T(8,128)(2,1)}, u32[]{:S(2)}) copy-start(bf16[128,16384]{1,0:T(8,128)(2,1)} %get-tuple-element.156) | copy-start | bytes 12582916 | tf_op jit(solution)/shard_map/while
  304.9 4.4 %copy-start = (bf16[128,16384]{1,0:T(8,128)(2,1)S(1)}, bf16[128,16384]{1,0:T(8,128)(2,1)}, u32[]{:S(2)}) copy-start(bf16[128,16384]{1,0:T(8,128)(2,1)} %get-tuple-element.156) | copy-start | bytes 12582916 | tf_op jit(solution)/shard_map/while
  310.5 4.4 %copy-start = (bf16[128,16384]{1,0:T(8,128)(2,1)S(1)}, bf16[128,16384]{1,0:T(8,128)(2,1)}, u32[]{:S(2)}) copy-start(bf16[128,16384]{1,0:T(8,128)(2,1)} %get-tuple-element.156) | copy-start | bytes 12582916 | tf_op jit(solution)/shard_map/while
  316.2 4.4 %copy-start = (bf16[128,16384]{1,0:T(8,128)(2,1)S(1)}, bf16[128,16384]{1,0:T(8,128)(2,1)}, u32[]{:S(2)}) copy-start(bf16[128,16384]{1,0:T(8,128)(2,1)} %get-tuple-element.156) | copy-start | bytes 12582916 | tf_op jit(solution)/shard_map/while
  327.4 4.4 %copy-start = (bf16[128,16384]{1,0:T(8,128)(2,1)S(1)}, bf16[128,16384]{1,0:T(8,128)(2,1)}, u32[]{:S(2)}) copy-start(bf16[128,16384]{1,0:T(8,128)(2,1)} %get-tuple-element.156) | copy-start | bytes 12582916 | tf_op jit(solution)/shard_map/while
  338.7 4.4 %copy-start = (bf16[128,16384]{1,0:T(8,128)(2,1)S(1)}, bf16[128,16384]{1,0:T(8,128)(2,1)}, u32[]{:S(2)}) copy-start(bf16[128,16384]{1,0:T(8,128)(2,1)} %get-tuple-element.156) | copy-start | bytes 12582916 | tf_op jit(solution)/shard_map/while
  344.3 4.4 %copy-start = (bf16[128,16384]{1,0:T(8,128)(2,1)S(1)}, bf16[128,16384]{1,0:T(8,128)(2,1)}, u32[]{:S(2)}) copy-start(bf16[128,16384]{1,0:T(8,128)(2,1)} %get-tuple-element.156) | copy-start | bytes 12582916 | tf_op jit(solution)/shard_map/while
  349.9 4.4 %copy-start = (bf16[128,16384]{1,0:T(8,128)(2,1)S(1)}, bf16[128,16384]{1,0:T(8,128)(2,1)}, u32[]{:S(2)}) copy-start(bf16[128,16384]{1,0:T(8,128)(2,1)} %get-tuple-element.156) | copy-start | bytes 12582916 | tf_op jit(solution)/shard_map/while
  361.2 4.4 %copy-start = (bf16[128,16384]{1,0:T(8,128)(2,1)S(1)}, bf16[128,16384]{1,0:T(8,128)(2,1)}, u32[]{:S(2)}) copy-start(bf16[128,16384]{1,0:T(8,128)(2,1)} %get-tuple-element.156) | copy-start | bytes 12582916 | tf_op jit(solution)/shard_map/while
  372.5 4.4 %copy-start = (bf16[128,16384]{1,0:T(8,128)(2,1)S(1)}, bf16[128,16384]{1,0:T(8,128)(2,1)}, u32[]{:S(2)}) copy-start(bf16[128,16384]{1,0:T(8,128)(2,1)} %get-tuple-element.156) | copy-start | bytes 12582916 | tf_op jit(solution)/shard_map/while
  378.1 4.4 %copy-start = (bf16[128,16384]{1,0:T(8,128)(2,1)S(1)}, bf16[128,16384]{1,0:T(8,128)(2,1)}, u32[]{:S(2)}) copy-start(bf16[128,16384]{1,0:T(8,128)(2,1)} %get-tuple-element.156) | copy-start | bytes 12582916 | tf_op jit(solution)/shard_map/while
  383.7 4.4 %copy-start = (bf16[128,16384]{1,0:T(8,128)(2,1)S(1)}, bf16[128,16384]{1,0:T(8,128)(2,1)}, u32[]{:S(2)}) copy-start(bf16[128,16384]{1,0:T(8,128)(2,1)} %get-tuple-element.156) | copy-start | bytes 12582916 | tf_op jit(solution)/shard_map/while
  (7 other events, 29.2 us)
where the time goes:
time: 422 us; the launch traced here: 414 us
  local copies, waits for them, and re-layouts  134 us (32%)
  matrix products  126 us (30%)
  waiting for transfers between devices  99.8 us (24%)
  starting transfers between devices  41.5 us (10%)
  blocking collectives  5.97 us (1%)
  other arithmetic  5.1 us (1%)
    dot_general x40, matrix products, select_blocks(): jnp.einsum('...s,sw->...w', pick_table, got_flat, preferred_element_type=...  74.8 us
    all_to_all x1, waiting for transfers between devices, shards(): lax.all_to_all(value_send, 'seq', split_axis=0, concat_axis=0, tiled=True)  55.8 us
    all_to_all x1, waiting for transfers between devices, shards(): lax.all_to_all(key_send, 'seq', split_axis=0, concat_axis=0, tiled=True)  44 us
    unnamed x20, local copies, waits for them, and re-layouts  34.1 us
    dot_general x20, matrix products, head_scores(): jnp.einsum(score_form, query_head, key_sel, preferred_element_type=jnp.fl...  24.4 us
    all_to_all x1, local copies, waits for them, and re-layouts, shards(): lax.all_to_all(value_states, 'head', split_axis=1, concat_axis=0, tiled=T...  17.3 us
    all_to_all x1, local copies, waits for them, and re-layouts, shards(): lax.all_to_all(queries, 'head', split_axis=1, concat_axis=0, tiled=True)  17.3 us
    all_to_all x1, starting transfers between devices, shards(): lax.all_to_all(value_send, 'seq', split_axis=0, concat_axis=0, tiled=True)  10.6 us
  transfers between devices with their start and end apart: 6, of which 2 were waited for; matrix products, arithmetic and copies ran while one was open for 28% of the time, Pallas kernels for 0%

commit v1 on v0

v1 whole, which is shorter than its diff:
```python
import functools
import math

import jax
import jax.numpy as jnp
from jax import lax
from jax.experimental import pallas as pl
from jax.experimental.pallas import tpu as pltpu
from jax.sharding import PartitionSpec as P

HEAD_DIM = 128
BLOCK = 128
CAPACITY = 2
PICKS = 4
HEADS_STEP = 4
MASKED = -1e30


def request_kernel(mask_ref, table_ref):
    heads, shard_blocks, blocks = mask_ref.shape
    shards = table_ref.shape[0]
    mask = mask_ref[...]
    needed = jnp.max(mask, axis=1)
    key_block = lax.broadcasted_iota(jnp.int32, (heads, blocks), 1)
    head = lax.broadcasted_iota(jnp.int32, (heads, blocks), 0)
    pair = head * shard_blocks + lax.rem(key_block, shard_blocks)
    low = jnp.min(jnp.where(needed > 0, pair, heads * shard_blocks), axis=0, keepdims=True)
    high = jnp.max(jnp.where(needed > 0, pair, -1), axis=0, keepdims=True)
    owner = lax.broadcasted_iota(jnp.int32, (shards, blocks), 1) // shard_blocks
    mine = owner == lax.broadcasted_iota(jnp.int32, (shards, blocks), 0)
    low_col = jnp.min(jnp.where(mine, low, heads * shard_blocks), axis=1, keepdims=True)
    high_col = jnp.max(jnp.where(mine, high, -1), axis=1, keepdims=True)
    low_col = jnp.minimum(low_col, heads * shard_blocks - 1)
    high_col = jnp.maximum(high_col, 0)
    lane = lax.broadcasted_iota(jnp.int32, (shards, 128), 1)
    table_ref[...] = jnp.where(lane == 0, low_col, high_col)


def plan_kernel(mask_ref, position_ref, bias_ref):
    heads, shard_blocks, blocks = mask_ref.shape
    shards = blocks // shard_blocks
    mask = mask_ref[...]
    needed = jnp.max(mask, axis=1)
    key_block = lax.broadcasted_iota(jnp.int32, (heads, blocks), 1)
    head = lax.broadcasted_iota(jnp.int32, (heads, blocks), 0)
    pair = head * shard_blocks + lax.rem(key_block, shard_blocks)
    low = jnp.min(jnp.where(needed > 0, pair, heads * shard_blocks), axis=0, keepdims=True)
    owner = lax.broadcasted_iota(jnp.int32, (shards, blocks), 1) // shard_blocks
    mine = owner == lax.broadcasted_iota(jnp.int32, (shards, blocks), 0)
    low_col = jnp.min(jnp.where(mine, low, heads * shard_blocks), axis=1, keepdims=True)
    low_own = jnp.min(jnp.where(mine, low_col, heads * shard_blocks), axis=0, keepdims=True)
    slot = (key_block // shard_blocks) * CAPACITY + (pair != low_own).astype(jnp.int32)
    upper = (
        lax.broadcasted_iota(jnp.int32, (blocks, blocks), 0)
        < lax.broadcasted_iota(jnp.int32, (blocks, blocks), 1)
    )
    prefix = jnp.dot(
        needed.astype(jnp.float32).astype(jnp.bfloat16),
        jnp.where(upper, 1.0, 0.0).astype(jnp.bfloat16),
        preferred_element_type=jnp.float32,
    )
    lane = lax.broadcasted_iota(jnp.int32, (heads, 128), 1)
    row = lax.broadcasted_iota(jnp.int32, (heads, 128), 0)
    position = jnp.zeros((heads, 128), jnp.int32)
    for j in range(PICKS):
        chosen = (needed > 0) & (prefix == float(j))
        slot_j = jnp.sum(jnp.where(chosen, slot, 0), axis=1, keepdims=True)
        position = jnp.where(lane == j, slot_j, position)
        bias = jnp.zeros((heads, 128), jnp.float32)
        for q in range(shard_blocks):
            live = jnp.max(jnp.where(chosen, mask[:, q, :], 0), axis=1, keepdims=True)
            bias = jnp.where(
                (lane == row * shard_blocks + q) & (live == 0), MASKED, bias
            )
        bias_ref[j] = bias
    position_ref[...] = position


def sort_kernel(meta, column_ref, key_own, key_far, value_own, value_far, key_out, value_out):
    del meta
    rows = column_ref.shape[1]
    half = rows // 2
    token = lax.broadcasted_iota(jnp.int32, (rows, rows), 1)
    for k in range(HEADS_STEP):
        cut = slice(k * HEAD_DIM, (k + 1) * HEAD_DIM)
        order = jnp.where(column_ref[0, :, k : k + 1] == token, 1.0, 0.0).astype(jnp.bfloat16)
        own = jnp.concatenate([key_own[:, cut], value_own[:, cut]], axis=1)
        far = jnp.concatenate([key_far[:, cut], value_far[:, cut]], axis=1)
        both = jnp.concatenate([own, far], axis=0)
        ordered = jnp.dot(order, both, preferred_element_type=jnp.float32).astype(jnp.bfloat16)
        key_out[k] = ordered[:, :HEAD_DIM]
        value_out[k] = ordered[:, HEAD_DIM:]


def scatter_kernel(request_ref, blocks_ref, send_ref, sem):
    shards = request_ref.shape[0]

    def start(d, carry):
        for j in range(CAPACITY):
            pltpu.make_async_copy(
                blocks_ref.at[request_ref[d, j]], send_ref.at[d * CAPACITY + j], sem
            ).start()
        return carry

    lax.fori_loop(0, shards, start, 0)
    pltpu.make_async_copy(send_ref, send_ref, sem).wait()


def member_kernel(perm_ref, member_ref):
    heads, rows = perm_ref.shape
    shard_blocks = rows // BLOCK
    token = lax.broadcasted_iota(jnp.int32, (rows, rows), 0)
    block = lax.broadcasted_iota(jnp.int32, (rows, 128), 0) // BLOCK
    lane = lax.broadcasted_iota(jnp.int32, (rows, 128), 1)

    def step(h, total):
        place = jnp.where(perm_ref[pl.ds(h, 1), :] == token, 1.0, 0.0).astype(jnp.bfloat16)
        target = jnp.where(lane == h * shard_blocks + block, 1.0, 0.0).astype(jnp.bfloat16)
        return total + jnp.dot(place, target, preferred_element_type=jnp.float32)

    total = lax.fori_loop(0, heads, step, jnp.zeros((rows, 128), jnp.float32))
    member_ref[...] = total.astype(jnp.bfloat16)


def score_kernel(meta, position, *refs):
    del meta, position
    query_own, query_far, member_ref, bias_ref = refs[:4]
    keys = refs[4 : 4 + PICKS]
    weight_ref = refs[4 + PICKS]
    h = pl.program_id(0)
    query = jnp.concatenate([query_own[...], query_far[...]], axis=0)
    left = jnp.concatenate([query, member_ref[...]], axis=1)
    right = []
    for j in range(PICKS):
        bias = bias_ref[j, pl.ds(h, 1), :].astype(jnp.bfloat16)
        right.append(
            jnp.concatenate([keys[j][0], jnp.broadcast_to(bias, (BLOCK, 128))], axis=1)
        )
    right = jnp.concatenate(right, axis=0)
    scores = lax.dot_general(
        left, right, (((1,), (1,)), ((), ())), preferred_element_type=jnp.float32
    )
    top = jnp.max(scores, axis=1, keepdims=True)
    exponent = jnp.exp2((scores - top) * (math.log2(math.e) / math.sqrt(HEAD_DIM)))
    total = jnp.sum(exponent, axis=1, keepdims=True)
    weight_ref[0] = (exponent * (1.0 / total)).astype(jnp.bfloat16)


def mix_kernel(meta, position, *refs):
    del meta, position
    weight_ref, out_ref = refs[0], refs[-1]
    values = refs[1:-1]
    for k in range(HEADS_STEP):
        value = jnp.concatenate([values[k * PICKS + j][0] for j in range(PICKS)], axis=0)
        mixed = jnp.dot(weight_ref[k], value, preferred_element_type=jnp.float32)
        out_ref[:, k * HEAD_DIM : (k + 1) * HEAD_DIM] = mixed.astype(jnp.bfloat16)


def place_kernel(meta, out_in, far_ref, out_ref, sem):
    del out_in
    width = far_ref.shape[1]
    start = pl.multiple_of((1 - meta[0]) * width, 128)
    copy = pltpu.make_async_copy(far_ref, out_ref.at[:, pl.ds(start, width)], sem)
    copy.start()
    copy.wait()


def shards(queries, key_states, value_states, cluster_perm, block_mask):
    heads, rows = cluster_perm.shape
    half, columns = queries.shape
    width = heads * HEAD_DIM
    shard_blocks = rows // BLOCK
    seq_count = lax.axis_size("seq")
    pairs = heads * shard_blocks
    slots = seq_count * CAPACITY
    steps = heads // HEADS_STEP
    step_width = HEADS_STEP * HEAD_DIM
    core = lax.axis_index("head")
    meta = jnp.stack([core, lax.axis_index("seq")]).astype(jnp.int32)
    vmem = pl.BlockSpec(memory_space=pltpu.VMEM)
    smem = pl.BlockSpec(memory_space=pltpu.SMEM)
    hbm = pl.BlockSpec(memory_space=pl.ANY)
    big = pltpu.CompilerParams(vmem_limit_bytes=56 << 20)

    table = pl.pallas_call(
        request_kernel,
        out_shape=jax.ShapeDtypeStruct((seq_count, 128), jnp.int32),
        in_specs=[vmem],
        out_specs=vmem,
        name="request",
    )(block_mask)
    requested = lax.all_to_all(
        table.reshape(seq_count, 1, 128), "seq", split_axis=0, concat_axis=0, tiled=True
    ).reshape(seq_count, 128)

    def swap(x):
        return lax.ppermute(x, "head", [(0, 1), (1, 0)])

    def far_half(x):
        return swap(lax.dynamic_slice(x, (0, (1 - core) * width), (half, width)))

    key_far = far_half(key_states)
    value_far = far_half(value_states)
    query_far = far_half(queries)

    local_perm = jnp.bitwise_and(
        cluster_perm - lax.axis_index("seq") * rows + core * half, rows - 1
    )
    column = local_perm.reshape(steps, HEADS_STEP, rows).transpose(0, 2, 1)

    own_spec = pl.BlockSpec((half, step_width), lambda g, meta: (0, meta[0] * steps + g))
    far_spec = pl.BlockSpec((half, step_width), lambda g, meta: (0, g))
    sorted_spec = pl.BlockSpec((HEADS_STEP, rows, HEAD_DIM), lambda g, meta: (g, 0, 0))
    key_sorted, value_sorted = pl.pallas_call(
        sort_kernel,
        out_shape=[jax.ShapeDtypeStruct((heads, rows, HEAD_DIM), jnp.bfloat16)] * 2,
        grid_spec=pltpu.PrefetchScalarGridSpec(
            num_scalar_prefetch=1,
            grid=(steps,),
            in_specs=[
                pl.BlockSpec((1, rows, HEADS_STEP), lambda g, meta: (g, 0, 0)),
                own_spec,
                far_spec,
                own_spec,
                far_spec,
            ],
            out_specs=[sorted_spec] * 2,
        ),
        compiler_params=big,
        name="sort",
    )(meta, column, key_states, key_far, value_states, value_far)

    def exchange(blocks):
        send = pl.pallas_call(
            scatter_kernel,
            out_shape=jax.ShapeDtypeStruct((slots, BLOCK, HEAD_DIM), jnp.bfloat16),
            in_specs=[smem, hbm],
            out_specs=hbm,
            scratch_shapes=[pltpu.SemaphoreType.DMA],
            name="scatter",
        )(requested, blocks.reshape(pairs, BLOCK, HEAD_DIM))
        return lax.all_to_all(send, "seq", split_axis=0, concat_axis=0, tiled=True)

    key_got = exchange(key_sorted)
    value_got = exchange(value_sorted)

    member = pl.pallas_call(
        member_kernel,
        out_shape=jax.ShapeDtypeStruct((rows, 128), jnp.bfloat16),
        in_specs=[vmem],
        out_specs=vmem,
        compiler_params=big,
        name="member",
    )(local_perm)
    position, bias = pl.pallas_call(
        plan_kernel,
        out_shape=[
            jax.ShapeDtypeStruct((heads, 128), jnp.int32),
            jax.ShapeDtypeStruct((PICKS, heads, 128), jnp.float32),
        ],
        in_specs=[vmem],
        out_specs=[vmem] * 2,
        name="plan",
    )(block_mask)

    def pick_spec(heads_step, k, j):
        return pl.BlockSpec(
            (1, BLOCK, HEAD_DIM),
            lambda g, meta, position: (position[g * heads_step + k, j], 0, 0),
        )

    weights = pl.pallas_call(
        score_kernel,
        out_shape=jax.ShapeDtypeStruct((heads, rows, PICKS * BLOCK), jnp.bfloat16),
        grid_spec=pltpu.PrefetchScalarGridSpec(
            num_scalar_prefetch=2,
            grid=(heads,),
            in_specs=[
                pl.BlockSpec((half, HEAD_DIM), lambda h, meta, position: (0, meta[0] * heads + h)),
                pl.BlockSpec((half, HEAD_DIM), lambda h, meta, position: (0, h)),
                pl.BlockSpec((rows, 128), lambda h, meta, position: (0, 0)),
                pl.BlockSpec((PICKS, heads, 128), lambda h, meta, position: (0, 0, 0)),
            ]
            + [pick_spec(1, 0, j) for j in range(PICKS)],
            out_specs=pl.BlockSpec(
                (1, rows, PICKS * BLOCK), lambda h, meta, position: (h, 0, 0)
            ),
        ),
        compiler_params=big,
        name="score",
    )(meta, position, queries, query_far, member, bias, *([key_got] * PICKS))

    def mix(part, out_columns, column_map):
        return pl.pallas_call(
            mix_kernel,
            out_shape=jax.ShapeDtypeStruct((half, out_columns), jnp.bfloat16),
            grid_spec=pltpu.PrefetchScalarGridSpec(
                num_scalar_prefetch=2,
                grid=(steps,),
                in_specs=[
                    pl.BlockSpec(
                        (HEADS_STEP, half, PICKS * BLOCK),
                        lambda g, meta, position: (g, part, 0),
                    )
                ]
                + [
                    pick_spec(HEADS_STEP, k, j)
                    for k in range(HEADS_STEP)
                    for j in range(PICKS)
                ],
                out_specs=pl.BlockSpec((half, step_width), column_map),
            ),
            compiler_params=big,
            name="mix",
        )(meta, position, weights, *([value_got] * (HEADS_STEP * PICKS)))

    out_far = swap(mix(1, width, lambda g, meta, position: (0, g)))
    out_own = mix(0, columns, lambda g, meta, position: (0, meta[0] * steps + g))
    return pl.pallas_call(
        place_kernel,
        out_shape=jax.ShapeDtypeStruct((half, columns), jnp.bfloat16),
        in_specs=[smem, hbm, hbm],
        out_specs=hbm,
        scratch_shapes=[pltpu.SemaphoreType.DMA],
        input_output_aliases={1: 0},
        name="place",
    )(meta, out_own, out_far)


def solution(mesh):
    placed = (
        P(("seq", "head"), None),
        P(("seq", "head"), None),
        P(("seq", "head"), None),
        P("head", "seq"),
        P("head", "seq", None),
    )
    return jax.shard_map(
        shards, mesh=mesh, in_specs=placed, out_specs=P(("seq", "head"), None), check_vma=False
    )
```

time: 422 us -> 427 us (1.012)
  the two profiles are of different devices: /device:TPU:103 before, /device:TPU:1 now
where the time goes in v1:
time: 427 us; the launch traced here: 421 us
  Pallas kernels  354 us (83%)
  starting transfers between devices  40.1 us (9%)
  waiting for transfers between devices  15.6 us (4%)
  local copies, waits for them, and re-layouts  10.3 us (2%)
    pallas_call x2, Pallas kernels, exchange(): pl.pallas_call(scatter_kernel, out_shape=jax.ShapeDtypeStruct((slots, BLO...  259 us
    pallas_call x1, Pallas kernels, shards(): pl.pallas_call(place_kernel, out_shape=jax.ShapeDtypeStruct((half, column...  41.5 us
    all_to_all x2, starting transfers between devices, exchange(): return lax.all_to_all(send, 'seq', split_axis=0, concat_axis=0, tiled=True)  20.2 us
    pallas_call x1, Pallas kernels, shards(): pl.pallas_call(score_kernel, out_shape=jax.ShapeDtypeStruct((heads, rows,...  18.9 us
    all_to_all x2, waiting for transfers between devices, exchange(): return lax.all_to_all(send, 'seq', split_axis=0, concat_axis=0, tiled=True)  15.6 us
    pallas_call x2, Pallas kernels, mix(): pl.pallas_call(mix_kernel, out_shape=jax.ShapeDtypeStruct((half, out_colu...  14.5 us
    all_to_all x1, starting transfers between devices, shards(): lax.all_to_all(table.reshape(seq_count, 1, 128), 'seq', split_axis=0, con...  11.2 us
    pallas_call x1, Pallas kernels, shards(): pl.pallas_call(sort_kernel, out_shape=[jax.ShapeDtypeStruct((heads, rows,...  8.77 us
  transfers between devices with their start and end apart: 7, of which 1 were waited for; matrix products, arithmetic and copies ran while one was open for 1% of the time, Pallas kernels for 42%

profile of v1, /device:TPU:1, one launch (start us, length us, event | category | flops | bytes accessed | tf_op | source)
XLA Modules:
  0.0 420.5 jit_solution(2755070716932575726)
XLA Ops:
  0.0 2.6 constant_dynamic-slice_fusion.1
  2.6 1.4 collective-permute-start.1
  4.0 1.2 constant_dynamic-slice_fusion
  5.2 1.8 request.1
  6.9 11.2 %all-to-all-start = ((s32[64,1,128]{2,1,0:T(1,128)}), s32[64,1,128]{2,1,0:T(1,128)S(1)}, u32[]{:S(2)}, u32[]{:S(2)}) async-start(s32[64,1,128]{2,1,0:T(1,128)} %bitcast.14), calls=%async_computation | async-start | bytes 65536 | tf_op jit(solution)/shard_map/all_to_all | solution.py:192
  18.8 1.5 copy.9
  20.3 1.1 copy-done.3
  21.4 8.8 %sort.1 = (bf16[20,512,128]{2,1,0:T(8,128)(2,1)}, bf16[20,512,128]{2,1,0:T(8,128)(2,1)}) custom-call(s32[2]{0:T(128)} %pad_add_fusion.meta, s32[5,512,4]{2,1,0:T(8,128)} %bitcast.9, bf16[256,5120]{1,0:T(8,128)(2,1)} %key_own.1, bf16[256,2560]{1,0:T(8,128)(2,1)} %collective-permute-done.1.key_far, bf16[256,5120]{1,0:T(8,128)(2,1)} %value_own.1, ...), custom_call_target="tpu_custom_call" | custom-call | tf_op jit(solution)/shard_map/sort/pallas_call | solution.py:214
  30.8 129.4 %scatter.2 = bf16[128,128,128]{2,1,0:T(8,128)(2,1)} custom-call(s32[64,128]{1,0:T(8,128)} %bitcast.12, bf16[80,128,128]{2,1,0:T(8,128)(2,1)} %bitcast.11), custom_call_target="tpu_custom_call" | custom-call | tf_op jit(solution)/shard_map/scatter/pallas_call | solution.py:234
  160.2 10.1 %all-to-all-start.1 = ((bf16[128,128,128]{2,1,0:T(8,128)(2,1)}), bf16[128,128,128]{2,1,0:T(8,128)(2,1)}, u32[]{:S(2)}, u32[]{:S(2)}) async-start(bf16[128,128,128]{2,1,0:T(8,128)(2,1)} %scatter.2), calls=%async_computation.1 | async-start | bytes 8388608 | tf_op jit(solution)/shard_map/all_to_all | solution.py:242
  170.2 129.4 %scatter.3 = bf16[128,128,128]{2,1,0:T(8,128)(2,1)} custom-call(s32[64,128]{1,0:T(8,128)} %bitcast.13, bf16[80,128,128]{2,1,0:T(8,128)(2,1)} %bitcast.10), custom_call_target="tpu_custom_call" | custom-call | tf_op jit(solution)/shard_map/scatter/pallas_call | solution.py:234
  299.6 10.1 %all-to-all-start.2 = ((bf16[128,128,128]{2,1,0:T(8,128)(2,1)}), bf16[128,128,128]{2,1,0:T(8,128)(2,1)}, u32[]{:S(2)}, u32[]{:S(2)}) async-start(bf16[128,128,128]{2,1,0:T(8,128)(2,1)} %scatter.3), calls=%async_computation.2 | async-start | bytes 8388608 | tf_op jit(solution)/shard_map/all_to_all | solution.py:242
  309.7 1.1 constant_dynamic-slice_fusion.2
  310.9 1.9 collective-permute-start
  312.8 7.7 %member.1.refs_2_ = bf16[512,128]{1,0:T(8,128)(2,1)} custom-call(s32[20,512]{1,0:T(8,128)} %copy-done.5), custom_call_target="tpu_custom_call" | custom-call | tf_op jit(solution)/shard_map/member/pallas_call | solution.py:247
  320.5 2.0 plan.1
  322.5 1.1 copy-done.2
  323.6 18.9 %score.1.refs_0_ = bf16[20,512,512]{2,1,0:T(8,128)(2,1)} custom-call(s32[2]{0:T(128)} %pad_add_fusion.meta, s32[20,128]{1,0:T(8,128)} %get-tuple-element.9.position, bf16[256,5120]{1,0:T(8,128)(2,1)} %refs_0_.1, bf16[256,2560]{1,0:T(8,128)(2,1)} %copy-done.2, bf16[512,128]{1,0:T(8,128)(2,1)} %member.1.refs_2_, f32[4,20,128]{2,1,0:T(8,128)} %get-tuple-element.10.refs_3_, ...), custom_call_target="tpu_custom_call" | custom-call | tf_op jit(solution)/shard_map/score/pallas_call | solution.py:272
  342.5 15.6 %all-to-all-done.2.refs_1_.refs_2_.refs_3_.refs_4_.refs_5_.refs_6_.refs_7_.refs_8_.refs_9_.refs_10_.refs_11_.refs_12_.refs_13_.refs_14_.refs_15_.refs_16_ = bf16[128,128,128]{2,1,0:T(8,128)(2,1)} async-done(((bf16[128,128,128]{2,1,0:T(8,128)(2,1)}), bf16[128,128,128]{2,1,0:T(8,128)(2,1)}, u32[]{:S(2)}, u32[]{:S(2)}) %all-to-all-start.2) | async-done | bytes 4194336 | tf_op jit(solution)/shard_map/all_to_all | solution.py:242
  358.1 7.3 %mix.3 = bf16[256,2560]{1,0:T(8,128)(2,1)} custom-call(s32[2]{0:T(128)} %pad_add_fusion.meta, s32[20,128]{1,0:T(8,128)} %get-tuple-element.9.position, bf16[20,512,512]{2,1,0:T(8,128)(2,1)} %score.1.refs_0_, ...), custom_call_target="tpu_custom_call" | custom-call | tf_op jit(solution)/shard_map/mix/pallas_call | solution.py:294
  365.3 5.3 %collective-permute-start.3 = (bf16[256,2560]{1,0:T(8,128)(2,1)}, bf16[256,2560]{1,0:T(8,128)(2,1)S(1)}, u32[]{:S(2)}, u32[]{:S(2)}) collective-permute-start(bf16[256,2560]{1,0:T(8,128)(2,1)} %mix.3), channel_id=1, source_target_pairs={{0,64},{64,0},{1,65},{65,1},{2,66},{66,2},{3,67},{67,3},{4,68},{68... | collective-permute-start | bytes 3932168 | tf_op jit(solution)/shard_map/ppermute | solution.py:197
  370.7 7.2 %mix.2.out_in = bf16[256,5120]{1,0:T(8,128)(2,1)} custom-call(s32[2]{0:T(128)} %pad_add_fusion.meta, s32[20,128]{1,0:T(8,128)} %get-tuple-element.9.position, bf16[20,512,512]{2,1,0:T(8,128)(2,1)} %score.1.refs_0_, ...), custom_call_target="tpu_custom_call" | custom-call | tf_op jit(solution)/shard_map/mix/pallas_call | solution.py:294
  378.0 1.1 copy-done.4
  379.0 41.5 %place.1 = bf16[256,5120]{1,0:T(8,128)(2,1)} custom-call(s32[2]{0:T(128)} %pad_add_fusion.meta, bf16[256,5120]{1,0:T(8,128)(2,1)} %mix.2.out_in, bf16[256,2560]{1,0:T(8,128)(2,1)} %copy-done.4), custom_call_target="tpu_custom_call", output_to_operand_aliasing={{}: (1, {})} | custom-call | tf_op jit(solution)/shard_map/place/pallas_call | solution.py:319
  (23 shorter events, 1.3 us)
Async XLA Ops:
  0.0 4.0 copy-start
  0.0 18.2 %copy-start.7 = (s32[20,512]{1,0:T(8,128)S(1)}, s32[20,512]{1,0:T(8,128)}, u32[]{:S(2)}) copy-start(s32[20,512]{1,0:T(8,128)} %param.8) | copy-start | bytes 122884
  2.6 17.7 %collective-permute-start.1 = (bf16[256,2560]{1,0:T(8,128)(2,1)}, bf16[256,2560]{1,0:T(8,128)(2,1)}, u32[]{:S(2)}, u32[]{:S(2)}) collective-permute-start(bf16[256,2560]{1,0:T(8,128)(2,1)} %constant_dynamic-slice_fusion.1), channel_id=1, source_target_pairs={{0,64},{64,0},{1,65},{65,1},{2,66},{66,2},{3,67},{67,3},{4,68},{68... | collective-permute-start | bytes 3932168 | tf_op jit(solution)/shard_map/ppermute | solution.py:197
  5.2 15.1 %collective-permute-start.2 = (bf16[256,2560]{1,0:T(8,128)(2,1)}, bf16[256,2560]{1,0:T(8,128)(2,1)S(1)}, u32[]{:S(2)}, u32[]{:S(2)}) collective-permute-start(bf16[256,2560]{1,0:T(8,128)(2,1)} %constant_dynamic-slice_fusion), channel_id=1, source_target_pairs={{0,64},{64,0},{1,65},{65,1},{2,66},{66,2},{3,67},{67,3},{4,68},{68... | collective-permute-start | bytes 3932168 | tf_op jit(solution)/shard_map/ppermute | solution.py:197
  6.9 23.2 %all-to-all-start = ((s32[64,1,128]{2,1,0:T(1,128)}), s32[64,1,128]{2,1,0:T(1,128)S(1)}, u32[]{:S(2)}, u32[]{:S(2)}) async-start(s32[64,1,128]{2,1,0:T(1,128)} %bitcast.14), calls=%async_computation | async-start | bytes 65536 | tf_op jit(solution)/shard_map/all_to_all | solution.py:192
  18.2 12.0 %copy-start.5 = (s32[20,512]{1,0:T(8,128)}, s32[20,512]{1,0:T(8,128)S(1)}, u32[]{:S(2)}) copy-start(s32[20,512]{1,0:T(8,128)S(1)} %add_and_fusion.perm_ref) | copy-start | bytes 122884
  20.3 1.1 copy-start.3
  30.2 0.6 copy-start.6
  160.2 139.4 %all-to-all-start.1 = ((bf16[128,128,128]{2,1,0:T(8,128)(2,1)}), bf16[128,128,128]{2,1,0:T(8,128)(2,1)}, u32[]{:S(2)}, u32[]{:S(2)}) async-start(bf16[128,128,128]{2,1,0:T(8,128)(2,1)} %scatter.2), calls=%async_computation.1 | async-start | bytes 8388608 | tf_op jit(solution)/shard_map/all_to_all | solution.py:242
  299.6 10.1 %copy-start.1 = (bf16[256,5120]{1,0:T(8,128)(2,1)S(1)}, bf16[256,5120]{1,0:T(8,128)(2,1)}, u32[]{:S(2)}) copy-start(bf16[256,5120]{1,0:T(8,128)(2,1)} %refs_0_.1) | copy-start | bytes 7864324
  299.6 58.4 %all-to-all-start.2 = ((bf16[128,128,128]{2,1,0:T(8,128)(2,1)}), bf16[128,128,128]{2,1,0:T(8,128)(2,1)}, u32[]{:S(2)}, u32[]{:S(2)}) async-start(bf16[128,128,128]{2,1,0:T(8,128)(2,1)} %scatter.3), calls=%async_computation.2 | async-start | bytes 8388608 | tf_op jit(solution)/shard_map/all_to_all | solution.py:242
  310.9 11.6 %collective-permute-start = (bf16[256,2560]{1,0:T(8,128)(2,1)}, bf16[256,2560]{1,0:T(8,128)(2,1)S(1)}, u32[]{:S(2)}, u32[]{:S(2)}) collective-permute-start(bf16[256,2560]{1,0:T(8,128)(2,1)} %constant_dynamic-slice_fusion.2), channel_id=1, source_target_pairs={{0,64},{64,0},{1,65},{65,1},{2,66},{66,2},{3,67},{67,3},{4,68},{68... | collective-permute-start | bytes 3932168 | tf_op jit(solution)/shard_map/ppermute | solution.py:197
  322.5 1.1 copy-start.2
  365.3 12.6 %collective-permute-start.3 = (bf16[256,2560]{1,0:T(8,128)(2,1)}, bf16[256,2560]{1,0:T(8,128)(2,1)S(1)}, u32[]{:S(2)}, u32[]{:S(2)}) collective-permute-start(bf16[256,2560]{1,0:T(8,128)(2,1)} %mix.3), channel_id=1, source_target_pairs={{0,64},{64,0},{1,65},{65,1},{2,66},{66,2},{3,67},{67,3},{4,68},{68... | collective-permute-start | bytes 3932168 | tf_op jit(solution)/shard_map/ppermute | solution.py:197
  377.9 1.1 copy-start.4

commit v2 on v1

--- a/solution.py
+++ b/solution.py
@@ -234,9 +234,10 @@
         send = pl.pallas_call(
             scatter_kernel,
             out_shape=jax.ShapeDtypeStruct((slots, BLOCK, HEAD_DIM), jnp.bfloat16),
-            in_specs=[smem, hbm],
+            in_specs=[smem, vmem],
             out_specs=hbm,
             scratch_shapes=[pltpu.SemaphoreType.DMA],
+            compiler_params=pltpu.CompilerParams(vmem_limit_bytes=16 << 20),
             name="scatter",
         )(requested, blocks.reshape(pairs, BLOCK, HEAD_DIM))
         return lax.all_to_all(send, "seq", split_axis=0, concat_axis=0, tiled=True)
@@ -319,7 +320,7 @@
     return pl.pallas_call(
         place_kernel,
         out_shape=jax.ShapeDtypeStruct((half, columns), jnp.bfloat16),
-        in_specs=[smem, hbm, hbm],
+        in_specs=[smem, hbm, vmem],
         out_specs=hbm,
         scratch_shapes=[pltpu.SemaphoreType.DMA],
         input_output_aliases={1: 0},

time: 427 us -> 200 us (0.47)
  the two profiles are of different devices: /device:TPU:1 before, /device:TPU:103 now
where the time goes in v2:
time: 200 us; the launch traced here: 198 us
  waiting for transfers between devices  81.5 us (41%)
  Pallas kernels  70.7 us (35%)
  starting transfers between devices  29.7 us (15%)
  local copies, waits for them, and re-layouts  15.2 us (8%)
    all_to_all x2, waiting for transfers between devices, exchange(): return lax.all_to_all(send, 'seq', split_axis=0, concat_axis=0, tiled=True)  81.5 us
    pallas_call x1, Pallas kernels, shards(): pl.pallas_call(score_kernel, out_shape=jax.ShapeDtypeStruct((heads, rows,...  19 us
    all_to_all x2, starting transfers between devices, exchange(): return lax.all_to_all(send, 'seq', split_axis=0, concat_axis=0, tiled=True)  17.2 us
    pallas_call x2, Pallas kernels, exchange(): pl.pallas_call(scatter_kernel, out_shape=jax.ShapeDtypeStruct((slots, BLO...  14.6 us
    pallas_call x2, Pallas kernels, mix(): pl.pallas_call(mix_kernel, out_shape=jax.ShapeDtypeStruct((half, out_colu...  14.5 us
    all_to_all x1, starting transfers between devices, shards(): lax.all_to_all(table.reshape(seq_count, 1, 128), 'seq', split_axis=0, con...  9.8 us
    unnamed x22, local copies, waits for them, and re-layouts  8.82 us
    pallas_call x1, Pallas kernels, shards(): pl.pallas_call(sort_kernel, out_shape=[jax.ShapeDtypeStruct((heads, rows,...  8.76 us
  transfers between devices with their start and end apart: 7, of which 2 were waited for; matrix products, arithmetic and copies ran while one was open for 2% of the time, Pallas kernels for 27%

profile of v2, /device:TPU:103, one launch (start us, length us, event | category | flops | bytes accessed | tf_op | source)
XLA Modules:
  0.0 197.9 jit_solution(11667840624713912801)
XLA Ops:
  0.0 2.6 %constant_dynamic-slice_fusion.1 = bf16[256,2560]{1,0:T(8,128)(2,1)} fusion(bf16[256,5120]{1,0:T(8,128)(2,1)} %key_own.1, s32[]{:T(128)S(6)} %select_n.2), kind=kLoop, calls=%fused_computation.2 | loop fusion | bytes 2621444 | tf_op jit(solution)/shard_map/dynamic_slice | solution.py:200
  3.3 1.1 constant_dynamic-slice_fusion
  4.4 1.8 request.1
  6.2 9.8 %all-to-all-start = ((s32[64,1,128]{2,1,0:T(1,128)}), s32[64,1,128]{2,1,0:T(1,128)S(1)}, u32[]{:S(2)}, u32[]{:S(2)}) async-start(s32[64,1,128]{2,1,0:T(1,128)} %bitcast.14), calls=%async_computation | async-start | bytes 65536 | tf_op jit(solution)/shard_map/all_to_all | solution.py:192
  16.7 1.5 copy.9
  19.3 8.8 %sort.1 = (bf16[20,512,128]{2,1,0:T(8,128)(2,1)}, bf16[20,512,128]{2,1,0:T(8,128)(2,1)}) custom-call(s32[2]{0:T(128)} %pad_add_fusion.meta, s32[5,512,4]{2,1,0:T(8,128)} %bitcast.13, bf16[256,5120]{1,0:T(8,128)(2,1)} %key_own.1, bf16[256,2560]{1,0:T(8,128)(2,1)} %collective-permute-done.1.key_far, bf16[256,5120]{1,0:T(8,128)(2,1)} %value_own.1, ...), custom_call_target="tpu_custom_call" | custom-call | tf_op jit(solution)/shard_map/sort/pallas_call | solution.py:214
  28.1 1.7 copy-done.3
  29.8 7.3 %scatter.2 = bf16[128,128,128]{2,1,0:T(8,128)(2,1)S(1)} custom-call(s32[64,128]{1,0:T(8,128)S(1)} %bitcast.11, bf16[80,128,128]{2,1,0:T(8,128)(2,1)S(1)} %bitcast.10), custom_call_target="tpu_custom_call" | custom-call | tf_op jit(solution)/shard_map/scatter/pallas_call | solution.py:234
  37.1 1.9 copy-done.1
  39.1 10.1 %all-to-all-start.1 = ((bf16[128,128,128]{2,1,0:T(8,128)(2,1)}), bf16[128,128,128]{2,1,0:T(8,128)(2,1)}, u32[]{:S(2)}, u32[]{:S(2)}) async-start(bf16[128,128,128]{2,1,0:T(8,128)(2,1)} %copy-done.1), calls=%async_computation.1 | async-start | bytes 8388608 | tf_op jit(solution)/shard_map/all_to_all | solution.py:243
  49.2 7.3 %scatter.3 = bf16[128,128,128]{2,1,0:T(8,128)(2,1)S(1)} custom-call(s32[64,128]{1,0:T(8,128)S(1)} %bitcast.12, bf16[80,128,128]{2,1,0:T(8,128)(2,1)S(1)} %bitcast.9), custom_call_target="tpu_custom_call" | custom-call | tf_op jit(solution)/shard_map/scatter/pallas_call | solution.py:234
  56.5 2.0 copy-done
  58.5 52.1 %all-to-all-done.1.refs_4_.refs_5_.refs_6_.refs_7_ = bf16[128,128,128]{2,1,0:T(8,128)(2,1)} async-done(((bf16[128,128,128]{2,1,0:T(8,128)(2,1)}), bf16[128,128,128]{2,1,0:T(8,128)(2,1)}, u32[]{:S(2)}, u32[]{:S(2)}) %all-to-all-start.1) | async-done | bytes 4194336 | tf_op jit(solution)/shard_map/all_to_all | solution.py:243
  110.5 7.1 %all-to-all-start.2 = ((bf16[128,128,128]{2,1,0:T(8,128)(2,1)}), bf16[128,128,128]{2,1,0:T(8,128)(2,1)}, u32[]{:S(2)}, u32[]{:S(2)}) async-start(bf16[128,128,128]{2,1,0:T(8,128)(2,1)} %copy-done), calls=%async_computation.2 | async-start | bytes 8388608 | tf_op jit(solution)/shard_map/all_to_all | solution.py:243
  117.6 1.1 constant_dynamic-slice_fusion.2
  118.8 1.3 collective-permute-start
  120.1 7.7 %member.1.refs_2_ = bf16[512,128]{1,0:T(8,128)(2,1)} custom-call(s32[20,512]{1,0:T(8,128)} %copy-done.9), custom_call_target="tpu_custom_call" | custom-call | tf_op jit(solution)/shard_map/member/pallas_call | solution.py:248
  127.8 2.0 %plan.1 = (s32[20,128]{1,0:T(8,128)}, f32[4,20,128]{2,1,0:T(8,128)}) custom-call(s32[20,4,256]{2,1,0:T(4,128)} %mask_ref.3), custom_call_target="tpu_custom_call" | custom-call | tf_op jit(solution)/shard_map/plan/pallas_call | solution.py:256
  130.8 19.0 %score.1.refs_0_ = bf16[20,512,512]{2,1,0:T(8,128)(2,1)} custom-call(s32[2]{0:T(128)} %pad_add_fusion.meta, s32[20,128]{1,0:T(8,128)} %get-tuple-element.9.position, bf16[256,5120]{1,0:T(8,128)(2,1)} %refs_0_.1, bf16[256,2560]{1,0:T(8,128)(2,1)} %copy-done.6, bf16[512,128]{1,0:T(8,128)(2,1)} %member.1.refs_2_, f32[4,20,128]{2,1,0:T(8,128)} %get-tuple-element.10.refs_3_, ...), custom_call_target="tpu_custom_call" | custom-call | tf_op jit(solution)/shard_map/score/pallas_call | solution.py:273
  149.8 29.4 %all-to-all-done.2.refs_1_.refs_2_.refs_3_.refs_4_.refs_5_.refs_6_.refs_7_.refs_8_.refs_9_.refs_10_.refs_11_.refs_12_.refs_13_.refs_14_.refs_15_.refs_16_ = bf16[128,128,128]{2,1,0:T(8,128)(2,1)} async-done(((bf16[128,128,128]{2,1,0:T(8,128)(2,1)}), bf16[128,128,128]{2,1,0:T(8,128)(2,1)}, u32[]{:S(2)}, u32[]{:S(2)}) %all-to-all-start.2) | async-done | bytes 4194336 | tf_op jit(solution)/shard_map/all_to_all | solution.py:243
  179.2 7.3 %mix.3 = bf16[256,2560]{1,0:T(8,128)(2,1)} custom-call(s32[2]{0:T(128)} %pad_add_fusion.meta, s32[20,128]{1,0:T(8,128)} %get-tuple-element.9.position, bf16[20,512,512]{2,1,0:T(8,128)(2,1)} %score.1.refs_0_, ...), custom_call_target="tpu_custom_call" | custom-call | tf_op jit(solution)/shard_map/mix/pallas_call | solution.py:295
  187.2 7.2 %mix.2.out_in = bf16[256,5120]{1,0:T(8,128)(2,1)} custom-call(s32[2]{0:T(128)} %pad_add_fusion.meta, s32[20,128]{1,0:T(8,128)} %get-tuple-element.9.position, bf16[20,512,512]{2,1,0:T(8,128)(2,1)} %score.1.refs_0_, ...), custom_call_target="tpu_custom_call" | custom-call | tf_op jit(solution)/shard_map/mix/pallas_call | solution.py:295
  194.4 1.1 copy-done.8
  195.5 2.4 %place.1 = bf16[256,5120]{1,0:T(8,128)(2,1)} custom-call(s32[2]{0:T(128)} %pad_add_fusion.meta, bf16[256,5120]{1,0:T(8,128)(2,1)} %mix.2.out_in, bf16[256,2560]{1,0:T(8,128)(2,1)} %copy-done.8), custom_call_target="tpu_custom_call", output_to_operand_aliasing={{}: (1, {})} | custom-call | tf_op jit(solution)/shard_map/place/pallas_call | solution.py:320
  (29 shorter events, 4.2 us)
Async XLA Ops:
  0.0 3.3 %copy-start.4 = (bf16[256,5120]{1,0:T(8,128)(2,1)S(1)}, bf16[256,5120]{1,0:T(8,128)(2,1)}, u32[]{:S(2)}) copy-start(bf16[256,5120]{1,0:T(8,128)(2,1)} %value_own.1) | copy-start | bytes 7864324
  0.0 16.0 %copy-start.10 = (s32[20,512]{1,0:T(8,128)S(1)}, s32[20,512]{1,0:T(8,128)}, u32[]{:S(2)}) copy-start(s32[20,512]{1,0:T(8,128)} %param.8) | copy-start | bytes 122884
  2.6 15.6 %collective-permute-start.1 = (bf16[256,2560]{1,0:T(8,128)(2,1)}, bf16[256,2560]{1,0:T(8,128)(2,1)}, u32[]{:S(2)}, u32[]{:S(2)}) collective-permute-start(bf16[256,2560]{1,0:T(8,128)(2,1)} %constant_dynamic-slice_fusion.1), channel_id=1, source_target_pairs={{0,64},{64,0},{1,65},{65,1},{2,66},{66,2},{3,67},{67,3},{4,68},{68... | collective-permute-start | bytes 3932168 | tf_op jit(solution)/shard_map/ppermute | solution.py:197
  4.4 13.8 %collective-permute-start.2 = (bf16[256,2560]{1,0:T(8,128)(2,1)}, bf16[256,2560]{1,0:T(8,128)(2,1)S(1)}, u32[]{:S(2)}, u32[]{:S(2)}) collective-permute-start(bf16[256,2560]{1,0:T(8,128)(2,1)} %constant_dynamic-slice_fusion), channel_id=1, source_target_pairs={{0,64},{64,0},{1,65},{65,1},{2,66},{66,2},{3,67},{67,3},{4,68},{68... | collective-permute-start | bytes 3932168 | tf_op jit(solution)/shard_map/ppermute | solution.py:197
  6.2 21.9 %all-to-all-start = ((s32[64,1,128]{2,1,0:T(1,128)}), s32[64,1,128]{2,1,0:T(1,128)S(1)}, u32[]{:S(2)}, u32[]{:S(2)}) async-start(s32[64,1,128]{2,1,0:T(1,128)} %bitcast.14), calls=%async_computation | async-start | bytes 65536 | tf_op jit(solution)/shard_map/all_to_all | solution.py:192
  16.0 12.0 %copy-start.9 = (s32[20,512]{1,0:T(8,128)}, s32[20,512]{1,0:T(8,128)S(1)}, u32[]{:S(2)}) copy-start(s32[20,512]{1,0:T(8,128)S(1)} %add_and_fusion.perm_ref) | copy-start | bytes 122884
  18.2 1.1 copy-start.7
  28.1 1.7 copy-start.3
  37.1 1.9 copy-start.1
  39.1 10.1 %copy-start.2 = (bf16[20,512,128]{2,1,0:T(8,128)(2,1)S(1)}, bf16[20,512,128]{2,1,0:T(8,128)(2,1)}, u32[]{:S(2)}) copy-start(bf16[20,512,128]{2,1,0:T(8,128)(2,1)} %get-tuple-element.12) | copy-start | bytes 7864324
  39.1 71.5 %all-to-all-start.1 = ((bf16[128,128,128]{2,1,0:T(8,128)(2,1)}), bf16[128,128,128]{2,1,0:T(8,128)(2,1)}, u32[]{:S(2)}, u32[]{:S(2)}) async-start(bf16[128,128,128]{2,1,0:T(8,128)(2,1)} %copy-done.1), calls=%async_computation.1 | async-start | bytes 8388608 | tf_op jit(solution)/shard_map/all_to_all | solution.py:243
  56.5 2.0 copy-start
  58.5 59.2 %copy-start.5 = (bf16[256,5120]{1,0:T(8,128)(2,1)S(1)}, bf16[256,5120]{1,0:T(8,128)(2,1)}, u32[]{:S(2)}) copy-start(bf16[256,5120]{1,0:T(8,128)(2,1)} %refs_0_.1) | copy-start | bytes 7864324
  110.5 68.7 %all-to-all-start.2 = ((bf16[128,128,128]{2,1,0:T(8,128)(2,1)}), bf16[128,128,128]{2,1,0:T(8,128)(2,1)}, u32[]{:S(2)}, u32[]{:S(2)}) async-start(bf16[128,128,128]{2,1,0:T(8,128)(2,1)} %copy-done), calls=%async_computation.2 | async-start | bytes 8388608 | tf_op jit(solution)/shard_map/all_to_all | solution.py:243
  118.8 11.0 %collective-permute-start = (bf16[256,2560]{1,0:T(8,128)(2,1)}, bf16[256,2560]{1,0:T(8,128)(2,1)S(1)}, u32[]{:S(2)}, u32[]{:S(2)}) collective-permute-start(bf16[256,2560]{1,0:T(8,128)(2,1)} %constant_dynamic-slice_fusion.2), channel_id=1, source_target_pairs={{0,64},{64,0},{1,65},{65,1},{2,66},{66,2},{3,67},{67,3},{4,68},{68... | collective-permute-start | bytes 3932168 | tf_op jit(solution)/shard_map/ppermute | solution.py:197
  129.8 1.1 copy-start.6
  186.5 8.0 %collective-permute-start.3 = (bf16[256,2560]{1,0:T(8,128)(2,1)}, bf16[256,2560]{1,0:T(8,128)(2,1)S(1)}, u32[]{:S(2)}, u32[]{:S(2)}) collective-permute-start(bf16[256,2560]{1,0:T(8,128)(2,1)} %mix.3), channel_id=1, source_target_pairs={{0,64},{64,0},{1,65},{65,1},{2,66},{66,2},{3,67},{67,3},{4,68},{68... | collective-permute-start | bytes 3932168 | tf_op jit(solution)/shard_map/ppermute | solution.py:197
  194.4 1.1 copy-start.8

commit v3 on v0

v3 whole, which is shorter than its diff:
```python
import math

import jax
import jax.numpy as jnp
from jax import lax
from jax.experimental import pallas as pl
from jax.experimental.pallas import tpu as pltpu
from jax.sharding import PartitionSpec as P

HEAD_DIM = 128
BLOCK = 128
CAPACITY = 2
PICKS = 4
HEADS_STEP = 4
MASKED = -1e30


def slot_lows(needed, shard_blocks):
    heads, blocks = needed.shape
    shards = blocks // shard_blocks
    key_block = lax.broadcasted_iota(jnp.int32, (heads, blocks), 1)
    head = lax.broadcasted_iota(jnp.int32, (heads, blocks), 0)
    pair = head * shard_blocks + lax.rem(key_block, shard_blocks)
    low = jnp.min(jnp.where(needed > 0, pair, heads * shard_blocks), axis=0, keepdims=True)
    owner = lax.broadcasted_iota(jnp.int32, (shards, blocks), 1) // shard_blocks
    mine = owner == lax.broadcasted_iota(jnp.int32, (shards, blocks), 0)
    low_col = jnp.min(jnp.where(mine, low, heads * shard_blocks), axis=1, keepdims=True)
    return pair, mine, low_col


def request_kernel(mask_ref, table_ref):
    heads, shard_blocks, _ = mask_ref.shape
    needed = jnp.max(mask_ref[...], axis=1)
    pair, mine, low_col = slot_lows(needed, shard_blocks)
    high = jnp.max(jnp.where(needed > 0, pair, -1), axis=0, keepdims=True)
    high_col = jnp.max(jnp.where(mine, high, -1), axis=1, keepdims=True)
    low_col = jnp.minimum(low_col, heads * shard_blocks - 1)
    high_col = jnp.maximum(high_col, 0)
    lane = lax.broadcasted_iota(jnp.int32, table_ref.shape, 1)
    table_ref[...] = jnp.where(lane == 0, low_col, high_col)


def local_tokens(perm, rows):
    return jnp.bitwise_and(perm + lax.axis_index("head") * (rows // 2), rows - 1)


def sort_kernel(perm_ref, key_own, key_far, value_own, value_far, out_ref, perm_pad, buf, sem):
    heads, rows = perm_ref.shape
    steps, _, half, step_width = buf.shape
    shard_blocks = rows // BLOCK
    base = lax.axis_index("head") * (heads * HEAD_DIM)

    def copies(g):
        cut = pl.ds(pl.multiple_of(base + g * step_width, 128), step_width)
        return [
            pltpu.make_async_copy(ref.at[:, cut], buf.at[g, n], sem.at[g, n])
            for n, ref in enumerate((key_own, value_own, key_far, value_far))
        ]

    for g in range(steps):
        for copy in copies(g):
            copy.start()
    perm_pad[0:heads, :] = local_tokens(perm_ref[...], rows)
    column = jnp.transpose(perm_pad[...])
    token = lax.broadcasted_iota(jnp.int32, (rows, rows), 1)
    for g in range(steps):
        for copy in copies(g):
            copy.wait()
        for k in range(HEADS_STEP):
            h = g * HEADS_STEP + k
            cut = slice(k * HEAD_DIM, (k + 1) * HEAD_DIM)
            order = jnp.where(column[:, h : h + 1] == token, 1.0, 0.0).astype(jnp.bfloat16)
            own = jnp.concatenate([buf[g, 0, :, cut], buf[g, 1, :, cut]], axis=1)
            far = jnp.concatenate([buf[g, 2, :, cut], buf[g, 3, :, cut]], axis=1)
            both = jnp.concatenate([own, far], axis=0)
            ordered = jnp.dot(order, both, preferred_element_type=jnp.float32)
            ordered = ordered.astype(jnp.bfloat16)
            for b in range(shard_blocks):
                block = ordered[b * BLOCK : (b + 1) * BLOCK]
                out_ref[h * shard_blocks + b, 0:BLOCK] = block[:, :HEAD_DIM]
                out_ref[h * shard_blocks + b, BLOCK : 2 * BLOCK] = block[:, HEAD_DIM:]


def scatter_kernel(request_ref, blocks_ref, send_ref, sem):
    shards = request_ref.shape[0]

    def start(d, carry):
        for j in range(CAPACITY):
            pltpu.make_async_copy(
                blocks_ref.at[request_ref[d, j]], send_ref.at[d * CAPACITY + j], sem
            ).start()
        return carry

    lax.fori_loop(0, shards, start, 0, unroll=4)
    pltpu.make_async_copy(send_ref, send_ref, sem).wait()


def prepare_kernel(
    perm_ref, mask_ref, query_own, query_far, query_ref, member_ref, position_ref, bias_ref, sem
):
    heads, rows = perm_ref.shape
    _, shard_blocks, blocks = mask_ref.shape
    half = rows // 2
    width = heads * HEAD_DIM
    cut = pl.ds(pl.multiple_of(lax.axis_index("head") * width, 128), width)
    copies = [
        pltpu.make_async_copy(query_own.at[:, cut], query_ref.at[0:half, :], sem.at[0]),
        pltpu.make_async_copy(query_far.at[:, cut], query_ref.at[half:rows, :], sem.at[1]),
    ]
    for copy in copies:
        copy.start()

    token = lax.broadcasted_iota(jnp.int32, (rows, rows), 0)
    block = lax.broadcasted_iota(jnp.int32, (rows, 128), 0) // BLOCK
    lane = lax.broadcasted_iota(jnp.int32, (rows, 128), 1)

    def step(h, total):
        local = local_tokens(perm_ref[pl.ds(h, 1), :], rows)
        place = jnp.where(local == token, 1.0, 0.0).astype(jnp.bfloat16)
        target = jnp.where(lane == h * shard_blocks + block, 1.0, 0.0).astype(jnp.bfloat16)
        return total + jnp.dot(place, target, preferred_element_type=jnp.float32)

    total = lax.fori_loop(0, heads, step, jnp.zeros((rows, 128), jnp.float32))
    member_ref[...] = total.astype(jnp.bfloat16)

    mask = mask_ref[...]
    needed = jnp.max(mask, axis=1)
    pair, mine, low_col = slot_lows(needed, shard_blocks)
    low_own = jnp.min(jnp.where(mine, low_col, heads * shard_blocks), axis=0, keepdims=True)
    key_block = lax.broadcasted_iota(jnp.int32, (heads, blocks), 1)
    slot = (key_block // shard_blocks) * CAPACITY + (pair != low_own).astype(jnp.int32)
    upper = (
        lax.broadcasted_iota(jnp.int32, (blocks, blocks), 0)
        < lax.broadcasted_iota(jnp.int32, (blocks, blocks), 1)
    )
    prefix = jnp.dot(
        needed.astype(jnp.float32).astype(jnp.bfloat16),
        jnp.where(upper, 1.0, 0.0).astype(jnp.bfloat16),
        preferred_element_type=jnp.float32,
    )
    lane = lax.broadcasted_iota(jnp.int32, (heads, 128), 1)
    row = lax.broadcasted_iota(jnp.int32, (heads, 128), 0)
    position = jnp.zeros((heads, 128), jnp.int32)
    for j in range(PICKS):
        chosen = (needed > 0) & (prefix == float(j))
        slot_j = jnp.sum(jnp.where(chosen, slot, 0), axis=1, keepdims=True)
        position = jnp.where(lane == j, slot_j, position)
        bias = jnp.zeros((heads, 128), jnp.float32)
        for q in range(shard_blocks):
            live = jnp.max(jnp.where(chosen, mask[:, q, :], 0), axis=1, keepdims=True)
            bias = jnp.where((lane == row * shard_blocks + q) & (live == 0), MASKED, bias)
        bias_ref[j] = bias
    position_ref[...] = position
    for copy in copies:
        copy.wait()


def attend(h, query, member, bias_ref, blocks_ref):
    left = jnp.concatenate([query, member], axis=1)
    keys, values = [], []
    for j in range(PICKS):
        bias = bias_ref[j, pl.ds(h, 1), :].astype(jnp.bfloat16)
        bias = jnp.broadcast_to(bias, (BLOCK, 128))
        keys.append(jnp.concatenate([blocks_ref[h * PICKS + j, 0:BLOCK], bias], axis=1))
        values.append(blocks_ref[h * PICKS + j, BLOCK : 2 * BLOCK])
    keys = jnp.concatenate(keys, axis=0)
    values = jnp.concatenate(values, axis=0)
    scores = lax.dot_general(
        left, keys, (((1,), (1,)), ((), ())), preferred_element_type=jnp.float32
    )
    top = jnp.max(scores, axis=1, keepdims=True)
    exponent = jnp.exp2((scores - top) * (math.log2(math.e) / math.sqrt(HEAD_DIM)))
    total = jnp.sum(exponent, axis=1, keepdims=True)
    weights = (exponent * (1.0 / total)).astype(jnp.bfloat16)
    return jnp.dot(weights, values, preferred_element_type=jnp.float32).astype(jnp.bfloat16)


def far_kernel(
    position_ref, query_ref, member_ref, bias_ref, got_ref, out_ref, blocks_ref, sem
):
    heads = position_ref.shape[0]
    half = out_ref.shape[0]

    def start(h, carry):
        for j in range(PICKS):
            pltpu.make_async_copy(
                got_ref.at[position_ref[h, j]], blocks_ref.at[h * PICKS + j], sem.at[h]
            ).start()
        return carry

    lax.fori_loop(0, heads, start, 0, unroll=2)
    for h in range(heads):
        part = blocks_ref.at[h * PICKS : (h + 1) * PICKS]
        pltpu.make_async_copy(part, part, sem.at[h]).wait()
        cut = slice(h * HEAD_DIM, (h + 1) * HEAD_DIM)
        out_ref[:, cut] = attend(
            h, query_ref[half:, cut], member_ref[half:, :], bias_ref, blocks_ref
        )


def own_kernel(query_ref, member_ref, bias_ref, blocks_ref, out_ref, stage, sem):
    half, width = stage.shape
    heads = width // HEAD_DIM
    step_width = HEADS_STEP * HEAD_DIM
    base = lax.axis_index("head") * width

    def copy(g):
        return pltpu.make_async_copy(
            stage.at[:, g * step_width : (g + 1) * step_width],
            out_ref.at[:, pl.ds(pl.multiple_of(base + g * step_width, 128), step_width)],
            sem.at[g],
        )

    for h in range(heads):
        cut = slice(h * HEAD_DIM, (h + 1) * HEAD_DIM)
        stage[:, cut] = attend(
            h, query_ref[:half, cut], member_ref[:half, :], bias_ref, blocks_ref
        )
        if h % HEADS_STEP == HEADS_STEP - 1:
            copy(h // HEADS_STEP).start()
    for g in range(heads // HEADS_STEP):
        copy(g).wait()


def place_kernel(out_in, far_ref, out_ref, sem):
    del out_in
    width = far_ref.shape[1]
    start = pl.multiple_of((1 - lax.axis_index("head")) * width, 128)
    copy = pltpu.make_async_copy(far_ref, out_ref.at[:, pl.ds(start, width)], sem)
    copy.start()
    copy.wait()


def shards(queries, key_states, value_states, cluster_perm, block_mask):
    heads, rows = cluster_perm.shape
    half, columns = queries.shape
    width = heads * HEAD_DIM
    shard_blocks = rows // BLOCK
    seq_count = lax.axis_size("seq")
    pairs = heads * shard_blocks
    slots = seq_count * CAPACITY
    steps = heads // HEADS_STEP
    vmem = pl.BlockSpec(memory_space=pltpu.VMEM)
    smem = pl.BlockSpec(memory_space=pltpu.SMEM)
    hbm = pl.BlockSpec(memory_space=pltpu.HBM)
    limit = lambda mib: pltpu.CompilerParams(vmem_limit_bytes=mib << 20)
    held = lambda x: pltpu.with_memory_space_constraint(x, pltpu.VMEM)
    held_out = lambda shape, dtype: pltpu.VMEM(shape, dtype)
    hbm_out = lambda shape, dtype: pltpu.HBM(shape, dtype)
    dma = pltpu.SemaphoreType.DMA
    bf16 = jnp.bfloat16

    table = pl.pallas_call(
        request_kernel,
        out_shape=jax.ShapeDtypeStruct((seq_count, 128), jnp.int32),
        in_specs=[vmem],
        out_specs=vmem,
        name="request",
    )(block_mask)
    requested = lax.all_to_all(
        table.reshape(seq_count, 1, 128), "seq", split_axis=0, concat_axis=0, tiled=True
    ).reshape(seq_count, 128)

    def swap(x):
        return lax.ppermute(x, "head", [(0, 1), (1, 0)])

    key_far = swap(key_states)
    value_far = swap(value_states)

    blocks = pl.pallas_call(
        sort_kernel,
        out_shape=held_out((pairs, 2 * BLOCK, HEAD_DIM), bf16),
        in_specs=[vmem, hbm, hbm, hbm, hbm],
        out_specs=vmem,
        scratch_shapes=[
            pltpu.VMEM((128, rows), jnp.int32),
            pltpu.VMEM((steps, 4, half, HEADS_STEP * HEAD_DIM), bf16),
            dma((steps, 4)),
        ],
        compiler_params=limit(24),
        name="sort",
    )(cluster_perm, key_states, key_far, value_states, value_far)
    send = pl.pallas_call(
        scatter_kernel,
        out_shape=hbm_out((slots, 2 * BLOCK, HEAD_DIM), bf16),
        in_specs=[smem, vmem],
        out_specs=hbm,
        scratch_shapes=[dma],
        compiler_params=limit(16),
        name="scatter",
    )(requested, held(blocks))
    got = lax.all_to_all(send, "seq", split_axis=0, concat_axis=0, tiled=True)

    query, member, position, bias = pl.pallas_call(
        prepare_kernel,
        out_shape=[
            held_out((rows, width), bf16),
            jax.ShapeDtypeStruct((rows, 128), bf16),
            jax.ShapeDtypeStruct((heads, 128), jnp.int32),
            jax.ShapeDtypeStruct((PICKS, heads, 128), jnp.float32),
        ],
        in_specs=[vmem, vmem, hbm, hbm],
        out_specs=[vmem] * 4,
        scratch_shapes=[dma((2,))],
        compiler_params=limit(24),
        name="prepare",
    )(cluster_perm, block_mask, queries, swap(queries))

    out_far, picked = pl.pallas_call(
        far_kernel,
        out_shape=[
            jax.ShapeDtypeStruct((half, width), bf16),
            held_out((pairs, 2 * BLOCK, HEAD_DIM), bf16),
        ],
        in_specs=[smem, vmem, vmem, vmem, hbm],
        out_specs=[vmem, vmem],
        scratch_shapes=[dma((heads,))],
        compiler_params=limit(32),
        name="far_rows",
    )(position, held(query), member, bias, got)
    out_far = swap(out_far)
    out_own = pl.pallas_call(
        own_kernel,
        out_shape=hbm_out((half, columns), bf16),
        in_specs=[vmem] * 4,
        out_specs=hbm,
        scratch_shapes=[pltpu.VMEM((half, width), bf16), dma((steps,))],
        compiler_params=limit(32),
        name="own_rows",
    )(held(query), member, bias, held(picked))
    return pl.pallas_call(
        place_kernel,
        out_shape=hbm_out((half, columns), bf16),
        in_specs=[hbm, vmem],
        out_specs=hbm,
        scratch_shapes=[dma],
        input_output_aliases={0: 0},
        name="place",
    )(out_own, held(out_far))


def solution(mesh):
    placed = (
        P(("seq", "head"), None),
        P(("seq", "head"), None),
        P(("seq", "head"), None),
        P("head", "seq"),
        P("head", "seq", None),
    )
    return jax.shard_map(
        shards, mesh=mesh, in_specs=placed, out_specs=P(("seq", "head"), None), check_vma=False
    )
```

time: 422 us -> 192 us (0.45)
  the two profiles are of different devices: /device:TPU:103 before, /device:TPU:33 now
where the time goes in v3:
time: 192 us
  waiting for transfers between devices  110 us (57%)
  Pallas kernels  43 us (22%)
  starting transfers between devices  25.6 us (13%)
  local copies, waits for them, and re-layouts  13.2 us (7%)
    all_to_all x1, waiting for transfers between devices, shards(): got = lax.all_to_all(send, 'seq', split_axis=0, concat_axis=0, tiled=True)  105 us
    pallas_call x1, Pallas kernels, shards(): pl.pallas_call(far_kernel, out_shape=[jax.ShapeDtypeStruct((half, width),...  14 us
    unnamed x22, local copies, waits for them, and re-layouts  13.2 us
    all_to_all x1, starting transfers between devices, shards(): lax.all_to_all(table.reshape(seq_count, 1, 128), 'seq', split_axis=0, con...  10.5 us
    all_to_all x1, starting transfers between devices, shards(): got = lax.all_to_all(send, 'seq', split_axis=0, concat_axis=0, tiled=True)  10.1 us
    pallas_call x1, Pallas kernels, shards(): pl.pallas_call(own_kernel, out_shape=hbm_out((half, columns), bf16), in_s...  9.49 us
    pallas_call x1, Pallas kernels, shards(): pl.pallas_call(prepare_kernel, out_shape=[held_out((rows, width), bf16),...  7.01 us
    pallas_call x1, Pallas kernels, shards(): pl.pallas_call(sort_kernel, out_shape=held_out((pairs, 2 * BLOCK, HEAD_DI...  5.34 us
  transfers between devices with their start and end apart: 6, of which 2 were waited for; matrix products, arithmetic and copies ran while one was open for 0% of the time, Pallas kernels for 12%

profile of v3, /device:TPU:33, one launch (start us, length us, event | category | flops | bytes accessed | tf_op | source)
XLA Modules:
  0.0 191.8 jit_solution(16087410551702773378)
XLA Ops:
  0.0 0.7 collective-permute-start.1
  0.7 1.8 request.1
  2.4 10.5 %all-to-all-start = ((s32[64,1,128]{2,1,0:T(1,128)}), s32[64,1,128]{2,1,0:T(1,128)S(1)}, u32[]{:S(2)}, u32[]{:S(2)}) async-start(s32[64,1,128]{2,1,0:T(1,128)} %bitcast.5), calls=%async_computation | async-start | bytes 65536 | tf_op jit(solution)/shard_map/all_to_all | solution.py:260
  13.0 1.7 copy-done.4
  14.7 1.7 copy-done.5
  16.5 0.8 copy-done.9
  17.3 5.3 %sort.1.blocks_ref = bf16[80,256,128]{2,1,0:T(8,128)(2,1)S(1)} custom-call(s32[20,512]{1,0:T(8,128)S(1)} %copy-done.9, bf16[256,5120]{1,0:T(8,128)(2,1)S(1)} %copy-done.4, bf16[256,5120]{1,0:T(8,128)(2,1)S(1)} %collective-permute-done.1.key_far, bf16[256,5120]{1,0:T(8,128)(2,1)S(1)} %copy-done.5, bf16[256,5120]{1,0:T(8,128)(2,1)} %collective-permute-done.2.value_far), custom_call_target="tpu_custom_call" | custom-call | tf_op jit(solution)/shard_map/sort/pallas_call | solution.py:270
  22.6 2.3 %copy-done = bf16[80,256,128]{2,1,0:T(8,128)(2,1)} copy-done((bf16[80,256,128]{2,1,0:T(8,128)(2,1)}, bf16[80,256,128]{2,1,0:T(8,128)(2,1)S(1)}, u32[]{:S(2)}) %copy-start) | copy-done | bytes 5242904
  24.9 2.5 %copy-done.1 = bf16[80,256,128]{2,1,0:T(8,128)(2,1)S(1)} copy-done((bf16[80,256,128]{2,1,0:T(8,128)(2,1)S(1)}, bf16[80,256,128]{2,1,0:T(8,128)(2,1)}, u32[]{:S(2)}) %copy-start.1) | copy-done | bytes 5242904
  27.4 4.3 %scatter.1 = bf16[128,256,128]{2,1,0:T(8,128)(2,1)} custom-call(s32[64,128]{1,0:T(8,128)S(1)} %bitcast.4, bf16[80,256,128]{2,1,0:T(8,128)(2,1)S(1)} %copy-done.1), custom_call_target="tpu_custom_call" | custom-call | tf_op jit(solution)/shard_map/scatter/pallas_call | solution.py:283
  31.7 0.0 copy-start.2
  31.8 0.0 copy-start.8
  31.8 10.1 %all-to-all-start.1 = ((bf16[128,256,128]{2,1,0:T(8,128)(2,1)}), bf16[128,256,128]{2,1,0:T(8,128)(2,1)}, u32[]{:S(2)}, u32[]{:S(2)}) async-start(bf16[128,256,128]{2,1,0:T(8,128)(2,1)} %scatter.1), calls=%async_computation.1 | async-start | bytes 16777216 | tf_op jit(solution)/shard_map/all_to_all | solution.py:292
  41.9 1.9 collective-permute-start
  43.8 4.5 %collective-permute-done.query_far = bf16[256,5120]{1,0:T(8,128)(2,1)S(1)} collective-permute-done((bf16[256,5120]{1,0:T(8,128)(2,1)S(1)}, bf16[256,5120]{1,0:T(8,128)(2,1)S(1)}, u32[]{:S(2)}, u32[]{:S(2)}) %collective-permute-start) | collective-permute-done | bytes 2621472 | tf_op jit(solution)/shard_map/ppermute | solution.py:265
  48.3 1.7 copy-done.3
  50.1 7.0 %prepare.1 = (bf16[512,2560]{1,0:T(8,128)(2,1)S(1)}, bf16[512,128]{1,0:T(8,128)(2,1)S(1)}, s32[20,128]{1,0:T(8,128)S(1)}, f32[4,20,128]{2,1,0:T(8,128)S(1)}) custom-call(s32[20,512]{1,0:T(8,128)S(1)} %copy-done.10, s32[20,4,256]{2,1,0:T(4,128)S(1)} %copy-done.8, bf16[256,5120]{1,0:T(8,128)(2,1)S(1)} %copy-done.3, ...), custom_call_target="tpu_custom_call" | custom-call | tf_op jit(solution)/shard_map/prepare/pallas_call | solution.py:294
  57.1 105.2 %all-to-all-done.1.got_ref = bf16[128,256,128]{2,1,0:T(8,128)(2,1)} async-done(((bf16[128,256,128]{2,1,0:T(8,128)(2,1)}), bf16[128,256,128]{2,1,0:T(8,128)(2,1)}, u32[]{:S(2)}, u32[]{:S(2)}) %all-to-all-start.1) | async-done | bytes 8388640 | tf_op jit(solution)/shard_map/all_to_all | solution.py:292
  162.3 14.0 %far_rows.1 = (bf16[256,2560]{1,0:T(8,128)(2,1)S(1)}, bf16[80,256,128]{2,1,0:T(8,128)(2,1)S(1)}) custom-call(s32[20,128]{1,0:T(8,128)S(1)} %get-tuple-element.14.position_ref, bf16[512,2560]{1,0:T(8,128)(2,1)S(1)} %get-tuple-element.11.query_ref, bf16[512,128]{1,0:T(8,128)(2,1)S(1)} %get-tuple-element.12.member_ref, ...), custom_call_target="tpu_custom_call" | custom-call | tf_op jit(solution)/shard_map/far_rows/pallas_call | solution.py:309
  176.2 2.4 %collective-permute-start.3 = (bf16[256,2560]{1,0:T(8,128)(2,1)S(1)}, bf16[256,2560]{1,0:T(8,128)(2,1)S(1)}, u32[]{:S(2)}, u32[]{:S(2)}) collective-permute-start(bf16[256,2560]{1,0:T(8,128)(2,1)S(1)} %get-tuple-element.16), channel_id=1, source_target_pairs={{0,64},{64,0},{1,65},{65,1},{2,66},{66,2},{3,67},{67,3},{4,68},{68... | collective-permute-start | bytes 3932168 | tf_op jit(solution)/shard_map/ppermute | solution.py:265
  178.7 9.5 %own_rows.1.out_in = bf16[256,5120]{1,0:T(8,128)(2,1)} custom-call(bf16[512,2560]{1,0:T(8,128)(2,1)S(1)} %get-tuple-element.11.query_ref, bf16[512,128]{1,0:T(8,128)(2,1)S(1)} %get-tuple-element.12.member_ref, f32[4,20,128]{2,1,0:T(8,128)S(1)} %get-tuple-element.13.bias_ref, bf16[80,256,128]{2,1,0:T(8,128)(2,1)S(1)} %get-tuple-element.15.blocks_ref), custom_call_target="tpu_custom_call" | custom-call | tf_op jit(solution)/shard_map/own_rows/pallas_call | solution.py:322
  188.2 1.1 copy-done.6
  189.3 1.3 copy-done.7
  190.6 1.1 place.1
  (17 shorter events, 0.0 us)
Async XLA Ops:
  0.0 13.0 %collective-permute-start.1 = (bf16[256,5120]{1,0:T(8,128)(2,1)}, bf16[256,5120]{1,0:T(8,128)(2,1)S(1)}, u32[]{:S(2)}, u32[]{:S(2)}) collective-permute-start(bf16[256,5120]{1,0:T(8,128)(2,1)} %key_own.1), channel_id=1, source_target_pairs={{0,64},{64,0},{1,65},{65,1},{2,66},{66,2},{3,67},{67,3},{4,68},{68... | collective-permute-start | bytes 7864328 | tf_op jit(solution)/shard_map/ppermute | solution.py:265
  0.7 12.3 %collective-permute-start.2 = (bf16[256,5120]{1,0:T(8,128)(2,1)}, bf16[256,5120]{1,0:T(8,128)(2,1)}, u32[]{:S(2)}, u32[]{:S(2)}) collective-permute-start(bf16[256,5120]{1,0:T(8,128)(2,1)} %value_own.1), channel_id=1, source_target_pairs={{0,64},{64,0},{1,65},{65,1},{2,66},{66,2},{3,67},{67,3},{4,68},{68... | collective-permute-start | bytes 7864328 | tf_op jit(solution)/shard_map/ppermute | solution.py:265
  2.4 22.5 %all-to-all-start = ((s32[64,1,128]{2,1,0:T(1,128)}), s32[64,1,128]{2,1,0:T(1,128)S(1)}, u32[]{:S(2)}, u32[]{:S(2)}) async-start(s32[64,1,128]{2,1,0:T(1,128)} %bitcast.5), calls=%async_computation | async-start | bytes 65536 | tf_op jit(solution)/shard_map/all_to_all | solution.py:260
  13.0 1.7 copy-start.4
  14.7 1.7 copy-start.5
  16.5 0.8 copy-start.9
  22.6 2.3 %copy-start = (bf16[80,256,128]{2,1,0:T(8,128)(2,1)}, bf16[80,256,128]{2,1,0:T(8,128)(2,1)S(1)}, u32[]{:S(2)}) copy-start(bf16[80,256,128]{2,1,0:T(8,128)(2,1)S(1)} %sort.1.blocks_ref) | copy-start | bytes 15728644
  24.9 2.5 %copy-start.1 = (bf16[80,256,128]{2,1,0:T(8,128)(2,1)S(1)}, bf16[80,256,128]{2,1,0:T(8,128)(2,1)}, u32[]{:S(2)}) copy-start(bf16[80,256,128]{2,1,0:T(8,128)(2,1)} %copy-done) | copy-start | bytes 15728644
  31.7 10.2 %copy-start.2 = (bf16[256,5120]{1,0:T(8,128)(2,1)S(1)}, bf16[256,5120]{1,0:T(8,128)(2,1)}, u32[]{:S(2)}) copy-start(bf16[256,5120]{1,0:T(8,128)(2,1)} %query_own.1) | copy-start | bytes 7864324
  31.8 16.6 %copy-start.8 = (s32[20,4,256]{2,1,0:T(4,128)S(1)}, s32[20,4,256]{2,1,0:T(4,128)}, u32[]{:S(2)}) copy-start(s32[20,4,256]{2,1,0:T(4,128)} %mask_ref.3) | copy-start | bytes 245764
  31.8 16.6 %copy-start.10 = (s32[20,512]{1,0:T(8,128)S(1)}, s32[20,512]{1,0:T(8,128)}, u32[]{:S(2)}) copy-start(s32[20,512]{1,0:T(8,128)} %perm_ref.3) | copy-start | bytes 122884
  31.8 130.5 %all-to-all-start.1 = ((bf16[128,256,128]{2,1,0:T(8,128)(2,1)}), bf16[128,256,128]{2,1,0:T(8,128)(2,1)}, u32[]{:S(2)}, u32[]{:S(2)}) async-start(bf16[128,256,128]{2,1,0:T(8,128)(2,1)} %scatter.1), calls=%async_computation.1 | async-start | bytes 16777216 | tf_op jit(solution)/shard_map/all_to_all | solution.py:292
  41.9 6.4 %collective-permute-start = (bf16[256,5120]{1,0:T(8,128)(2,1)S(1)}, bf16[256,5120]{1,0:T(8,128)(2,1)S(1)}, u32[]{:S(2)}, u32[]{:S(2)}) collective-permute-start(bf16[256,5120]{1,0:T(8,128)(2,1)S(1)} %copy-done.2), channel_id=1, source_target_pairs={{0,64},{64,0},{1,65},{65,1},{2,66},{66,2},{3,67},{67,3},{4,68},{68... | collective-permute-start | bytes 7864328 | tf_op jit(solution)/shard_map/ppermute | solution.py:265
  48.3 1.7 copy-start.3
  176.2 11.9 %collective-permute-start.3 = (bf16[256,2560]{1,0:T(8,128)(2,1)S(1)}, bf16[256,2560]{1,0:T(8,128)(2,1)S(1)}, u32[]{:S(2)}, u32[]{:S(2)}) collective-permute-start(bf16[256,2560]{1,0:T(8,128)(2,1)S(1)} %get-tuple-element.16), channel_id=1, source_target_pairs={{0,64},{64,0},{1,65},{65,1},{2,66},{66,2},{3,67},{67,3},{4,68},{68... | collective-permute-start | bytes 3932168 | tf_op jit(solution)/shard_map/ppermute | solution.py:265
  188.2 1.1 copy-start.6
  189.3 1.3 copy-start.7

commit v4 on v3

v4 whole, which is shorter than its diff:
```python
import math

import jax
import jax.numpy as jnp
from jax import lax
from jax.experimental import pallas as pl
from jax.experimental.pallas import tpu as pltpu
from jax.sharding import PartitionSpec as P

HEAD_DIM = 128
BLOCK = 128
CAPACITY = 2
PICKS = 4
HEADS_STEP = 4
MASKED = -1e30


def slot_lows(needed, shard_blocks):
    heads, blocks = needed.shape
    shards = blocks // shard_blocks
    key_block = lax.broadcasted_iota(jnp.int32, (heads, blocks), 1)
    head = lax.broadcasted_iota(jnp.int32, (heads, blocks), 0)
    pair = head * shard_blocks + lax.rem(key_block, shard_blocks)
    low = jnp.min(jnp.where(needed > 0, pair, heads * shard_blocks), axis=0, keepdims=True)
    owner = lax.broadcasted_iota(jnp.int32, (shards, blocks), 1) // shard_blocks
    mine = owner == lax.broadcasted_iota(jnp.int32, (shards, blocks), 0)
    low_col = jnp.min(jnp.where(mine, low, heads * shard_blocks), axis=1, keepdims=True)
    return pair, mine, low_col


def request_kernel(mask_ref, table_ref):
    heads, shard_blocks, _ = mask_ref.shape
    needed = jnp.max(mask_ref[...], axis=1)
    pair, mine, low_col = slot_lows(needed, shard_blocks)
    high = jnp.max(jnp.where(needed > 0, pair, -1), axis=0, keepdims=True)
    high_col = jnp.max(jnp.where(mine, high, -1), axis=1, keepdims=True)
    low_col = jnp.minimum(low_col, heads * shard_blocks - 1)
    high_col = jnp.maximum(high_col, 0)
    lane = lax.broadcasted_iota(jnp.int32, table_ref.shape, 1)
    table_ref[...] = jnp.where(lane == 0, low_col, high_col)


def local_tokens(perm, rows):
    return jnp.bitwise_and(perm + lax.axis_index("head") * (rows // 2), rows - 1)


def plan_kernel(mask_ref, position_ref, bias_ref):
    heads, shard_blocks, blocks = mask_ref.shape
    mask = mask_ref[...]
    needed = jnp.max(mask, axis=1)
    pair, mine, low_col = slot_lows(needed, shard_blocks)
    low_own = jnp.min(jnp.where(mine, low_col, heads * shard_blocks), axis=0, keepdims=True)
    key_block = lax.broadcasted_iota(jnp.int32, (heads, blocks), 1)
    slot = (key_block // shard_blocks) * CAPACITY + (pair != low_own).astype(jnp.int32)
    upper = (
        lax.broadcasted_iota(jnp.int32, (blocks, blocks), 0)
        < lax.broadcasted_iota(jnp.int32, (blocks, blocks), 1)
    )
    prefix = jnp.dot(
        needed.astype(jnp.float32).astype(jnp.bfloat16),
        jnp.where(upper, 1.0, 0.0).astype(jnp.bfloat16),
        preferred_element_type=jnp.float32,
    )
    lane = lax.broadcasted_iota(jnp.int32, (heads, 128), 1)
    row = lax.broadcasted_iota(jnp.int32, (heads, 128), 0)
    position = jnp.zeros((heads, 128), jnp.int32)
    for j in range(PICKS):
        chosen = (needed > 0) & (prefix == float(j))
        slot_j = jnp.sum(jnp.where(chosen, slot, 0), axis=1, keepdims=True)
        position = jnp.where(lane == j, slot_j, position)
        bias = jnp.zeros((heads, 128), jnp.float32)
        for q in range(shard_blocks):
            live = jnp.max(jnp.where(chosen, mask[:, q, :], 0), axis=1, keepdims=True)
            bias = jnp.where((lane == row * shard_blocks + q) & (live == 0), MASKED, bias)
        bias_ref[j] = bias
    position_ref[...] = position


def sort_kernel(
    request_ref, perm_ref, key_own, key_far, value_own, value_far,
    send_ref, member_ref, perm_pad, member_pad, buf, out_ref, sem, send_sem,
):
    heads, rows = perm_ref.shape
    steps, _, half, step_width = buf.shape
    shard_blocks = rows // BLOCK
    base = lax.axis_index("head") * (heads * HEAD_DIM)

    def copies(g):
        cut = pl.ds(pl.multiple_of(base + g * step_width, 128), step_width)
        return [
            pltpu.make_async_copy(ref.at[:, cut], buf.at[g, n], sem.at[g, n])
            for n, ref in enumerate((key_own, value_own, key_far, value_far))
        ]

    for g in range(steps):
        for copy in copies(g):
            copy.start()
    perm_pad[0:heads, :] = local_tokens(perm_ref[...], rows)
    column = jnp.transpose(perm_pad[...])
    token = lax.broadcasted_iota(jnp.int32, (rows, rows), 1)
    member_pad[heads * shard_blocks :, :] = jnp.zeros(
        (member_pad.shape[0] - heads * shard_blocks, rows), jnp.float32
    )
    for g in range(steps):
        for copy in copies(g):
            copy.wait()
        for k in range(HEADS_STEP):
            h = g * HEADS_STEP + k
            cut = slice(k * HEAD_DIM, (k + 1) * HEAD_DIM)
            order = jnp.where(column[:, h : h + 1] == token, 1.0, 0.0)
            own = jnp.concatenate([buf[g, 0, :, cut], buf[g, 1, :, cut]], axis=1)
            far = jnp.concatenate([buf[g, 2, :, cut], buf[g, 3, :, cut]], axis=1)
            both = jnp.concatenate([own, far], axis=0)
            ordered = jnp.dot(
                order.astype(jnp.bfloat16), both, preferred_element_type=jnp.float32
            ).astype(jnp.bfloat16)
            for b in range(shard_blocks):
                part = slice(b * BLOCK, (b + 1) * BLOCK)
                row = h * shard_blocks + b
                member_pad[row : row + 1, :] = jnp.sum(order[part], axis=0, keepdims=True)
                out_ref[row, 0:BLOCK] = ordered[part, :HEAD_DIM]
                out_ref[row, BLOCK : 2 * BLOCK] = ordered[part, HEAD_DIM:]

    def start(d, carry):
        for j in range(CAPACITY):
            pltpu.make_async_copy(
                out_ref.at[request_ref[d, j]], send_ref.at[d * CAPACITY + j], send_sem
            ).start()
        return carry

    lax.fori_loop(0, request_ref.shape[0], start, 0, unroll=8)
    member_ref[...] = jnp.transpose(member_pad[...]).astype(jnp.bfloat16)
    pltpu.make_async_copy(send_ref, send_ref, send_sem).wait()


def score(h, query, member, bias_ref, blocks_ref):
    left = jnp.concatenate([query, member], axis=1)
    keys = []
    for j in range(PICKS):
        bias = jnp.broadcast_to(bias_ref[j, h : h + 1, :].astype(jnp.bfloat16), (BLOCK, 128))
        keys.append(jnp.concatenate([blocks_ref[h * PICKS + j, 0:BLOCK], bias], axis=1))
    return lax.dot_general(
        left,
        jnp.concatenate(keys, axis=0),
        (((1,), (1,)), ((), ())),
        preferred_element_type=jnp.float32,
    )


def mix(h, scores, blocks_ref):
    top = jnp.max(scores, axis=1, keepdims=True)
    exponent = jnp.exp2((scores - top) * (math.log2(math.e) / math.sqrt(HEAD_DIM)))
    total = jnp.sum(exponent, axis=1, keepdims=True)
    weights = (exponent * (1.0 / total)).astype(jnp.bfloat16)
    values = jnp.concatenate(
        [blocks_ref[h * PICKS + j, BLOCK : 2 * BLOCK] for j in range(PICKS)], axis=0
    )
    return jnp.dot(weights, values, preferred_element_type=jnp.float32).astype(jnp.bfloat16)


def attend(heads, ready, query_ref, member, bias_ref, blocks_ref, finish):
    def score_of(h):
        ready(h)
        cut = slice(h * HEAD_DIM, (h + 1) * HEAD_DIM)
        return score(h, query_ref[:, cut], member, bias_ref, blocks_ref)

    following = score_of(0)
    for h in range(heads):
        scores = following
        if h + 1 < heads:
            following = score_of(h + 1)
        finish(h, mix(h, scores, blocks_ref))


def query_copy(query_hbm, query_ref, sem):
    width = query_ref.shape[1]
    cut = pl.ds(pl.multiple_of(lax.axis_index("head") * width, 128), width)
    return pltpu.make_async_copy(query_hbm.at[:, cut], query_ref, sem)


def far_kernel(
    position_ref, member_ref, bias_ref, query_hbm, got_ref, out_ref, blocks_ref, query_ref, sem
):
    heads = position_ref.shape[0]
    half = out_ref.shape[0]
    load = query_copy(query_hbm, query_ref, sem.at[heads])
    load.start()

    def start(h, carry):
        for j in range(PICKS):
            pltpu.make_async_copy(
                got_ref.at[position_ref[h, j]], blocks_ref.at[h * PICKS + j], sem.at[h]
            ).start()
        return carry

    lax.fori_loop(0, heads, start, 0, unroll=4)
    load.wait()

    def ready(h):
        part = blocks_ref.at[h * PICKS : (h + 1) * PICKS]
        pltpu.make_async_copy(part, part, sem.at[h]).wait()

    def finish(h, mixed):
        out_ref[:, h * HEAD_DIM : (h + 1) * HEAD_DIM] = mixed

    attend(heads, ready, query_ref, member_ref[half:, :], bias_ref, blocks_ref, finish)


def own_kernel(
    member_ref, bias_ref, blocks_ref, query_hbm, out_ref, query_ref, stage, sem, query_sem
):
    half, width = stage.shape
    heads = width // HEAD_DIM
    step_width = HEADS_STEP * HEAD_DIM
    base = lax.axis_index("head") * width
    load = query_copy(query_hbm, query_ref, query_sem)
    load.start()

    def copy(g):
        return pltpu.make_async_copy(
            stage.at[:, g * step_width : (g + 1) * step_width],
            out_ref.at[:, pl.ds(pl.multiple_of(base + g * step_width, 128), step_width)],
            sem.at[g],
        )

    def finish(h, mixed):
        stage[:, h * HEAD_DIM : (h + 1) * HEAD_DIM] = mixed
        if h % HEADS_STEP == HEADS_STEP - 1:
            copy(h // HEADS_STEP).start()

    load.wait()
    attend(
        heads, lambda h: None, query_ref, member_ref[:half, :], bias_ref, blocks_ref, finish
    )
    for g in range(heads // HEADS_STEP):
        copy(g).wait()


def place_kernel(out_in, far_ref, out_ref, sem):
    del out_in
    width = far_ref.shape[1]
    start = pl.multiple_of((1 - lax.axis_index("head")) * width, 128)
    copy = pltpu.make_async_copy(far_ref, out_ref.at[:, pl.ds(start, width)], sem)
    copy.start()
    copy.wait()


def shards(queries, key_states, value_states, cluster_perm, block_mask):
    heads, rows = cluster_perm.shape
    half, columns = queries.shape
    width = heads * HEAD_DIM
    shard_blocks = rows // BLOCK
    seq_count = lax.axis_size("seq")
    pairs = heads * shard_blocks
    slots = seq_count * CAPACITY
    steps = heads // HEADS_STEP
    vmem = pl.BlockSpec(memory_space=pltpu.VMEM)
    smem = pl.BlockSpec(memory_space=pltpu.SMEM)
    hbm = pl.BlockSpec(memory_space=pltpu.HBM)
    limit = lambda mib: pltpu.CompilerParams(vmem_limit_bytes=mib << 20)
    held = lambda x: pltpu.with_memory_space_constraint(x, pltpu.VMEM)
    far = lambda x: pltpu.with_memory_space_constraint(x, pltpu.HBM)
    held_out = lambda shape, dtype: pltpu.VMEM(shape, dtype)
    hbm_out = lambda shape, dtype: pltpu.HBM(shape, dtype)
    dma = pltpu.SemaphoreType.DMA
    bf16 = jnp.bfloat16

    table = pl.pallas_call(
        request_kernel,
        out_shape=jax.ShapeDtypeStruct((seq_count, 128), jnp.int32),
        in_specs=[vmem],
        out_specs=vmem,
        name="request",
    )(block_mask)
    requested = lax.all_to_all(
        table.reshape(seq_count, 1, 128), "seq", split_axis=0, concat_axis=0, tiled=True
    ).reshape(seq_count, 128)

    def swap(x):
        return lax.ppermute(x, "head", [(0, 1), (1, 0)])

    key_far = swap(key_states)
    value_far = swap(value_states)

    query_far = swap(queries)
    position, bias = pl.pallas_call(
        plan_kernel,
        out_shape=[
            jax.ShapeDtypeStruct((heads, 128), jnp.int32),
            jax.ShapeDtypeStruct((PICKS, heads, 128), jnp.float32),
        ],
        in_specs=[vmem],
        out_specs=[vmem] * 2,
        name="plan",
    )(block_mask)
    send, member = pl.pallas_call(
        sort_kernel,
        out_shape=[
            hbm_out((slots, 2 * BLOCK, HEAD_DIM), bf16),
            held_out((rows, 128), bf16),
        ],
        in_specs=[smem, vmem, hbm, hbm, hbm, hbm],
        out_specs=[hbm, vmem],
        scratch_shapes=[
            pltpu.VMEM((128, rows), jnp.int32),
            pltpu.VMEM((128, rows), jnp.float32),
            pltpu.VMEM((steps, 4, half, HEADS_STEP * HEAD_DIM), bf16),
            pltpu.VMEM((pairs, 2 * BLOCK, HEAD_DIM), bf16),
            dma((steps, 4)),
            dma,
        ],
        compiler_params=limit(32),
        name="sort",
    )(requested, cluster_perm, far(key_states), key_far, far(value_states), value_far)
    send, member, position, bias, query_far = lax.optimization_barrier(
        (send, member, position, bias, query_far)
    )
    got = lax.all_to_all(send, "seq", split_axis=0, concat_axis=0, tiled=True)

    out_far, picked = pl.pallas_call(
        far_kernel,
        out_shape=[
            held_out((half, width), bf16),
            held_out((pairs, 2 * BLOCK, HEAD_DIM), bf16),
        ],
        in_specs=[smem, vmem, vmem, hbm, hbm],
        out_specs=[vmem, vmem],
        scratch_shapes=[pltpu.VMEM((half, width), bf16), dma((heads + 1,))],
        compiler_params=limit(32),
        name="far_rows",
    )(position, held(member), bias, query_far, far(got))
    out_far = swap(out_far)
    out_own = pl.pallas_call(
        own_kernel,
        out_shape=hbm_out((half, columns), bf16),
        in_specs=[vmem, vmem, vmem, hbm],
        out_specs=hbm,
        scratch_shapes=[
            pltpu.VMEM((half, width), bf16),
            pltpu.VMEM((half, width), bf16),
            dma((steps,)),
            dma,
        ],
        compiler_params=limit(32),
        name="own_rows",
    )(held(member), bias, held(picked), far(queries))
    return pl.pallas_call(
        place_kernel,
        out_shape=hbm_out((half, columns), bf16),
        in_specs=[hbm, vmem],
        out_specs=hbm,
        scratch_shapes=[dma],
        input_output_aliases={0: 0},
        name="place",
    )(out_own, held(out_far))


def solution(mesh):
    placed = (
        P(("seq", "head"), None),
        P(("seq", "head"), None),
        P(("seq", "head"), None),
        P("head", "seq"),
        P("head", "seq", None),
    )
    return jax.shard_map(
        shards, mesh=mesh, in_specs=placed, out_specs=P(("seq", "head"), None), check_vma=False
    )
```

time: 192 us -> 164 us (0.85)
  the two profiles are of different devices: /device:TPU:33 before, /device:TPU:1 now
where the time goes in v4:
time: 164 us
  blocking collectives  106 us (65%)
  Pallas kernels  34.4 us (21%)
  starting transfers between devices  16.1 us (10%)
  waiting for transfers between devices  6.42 us (4%)
    all_to_all x1, blocking collectives, shards(): got = lax.all_to_all(send, 'seq', split_axis=0, concat_axis=0, tiled=True)  106 us
    pallas_call x1, Pallas kernels, shards(): pl.pallas_call(sort_kernel, out_shape=[hbm_out((slots, 2 * BLOCK, HEAD_DI...  11.4 us
    all_to_all x1, starting transfers between devices, shards(): lax.all_to_all(table.reshape(seq_count, 1, 128), 'seq', split_axis=0, con...  11.2 us
    pallas_call x1, Pallas kernels, shards(): pl.pallas_call(far_kernel, out_shape=[held_out((half, width), bf16), held...  11 us
    pallas_call x1, Pallas kernels, shards(): pl.pallas_call(own_kernel, out_shape=hbm_out((half, columns), bf16), in_s...  7.18 us
    all_to_all x1, waiting for transfers between devices, shards(): lax.all_to_all(table.reshape(seq_count, 1, 128), 'seq', split_axis=0, con...  6.41 us
    ppermute x4, starting transfers between devices, swap(): return lax.ppermute(x, 'head', [(0, 1), (1, 0)])  4.91 us
  transfers between devices with their start and end apart: 5, of which 1 were waited for; matrix products, arithmetic and copies ran while one was open for 0% of the time, Pallas kernels for 14%

profile of v4, /device:TPU:1, one launch (start us, length us, event | category | flops | bytes accessed | tf_op | source)
XLA Modules:
  0.0 163.8 jit_solution(105152099751491297)
XLA Ops:
  0.0 1.4 collective-permute-start
  1.4 0.0 collective-permute-start.1
  1.4 0.5 collective-permute-start.2
  1.9 1.8 %request.1 = s32[64,128]{1,0:T(8,128)} custom-call(s32[20,4,256]{2,1,0:T(4,128)} %mask_ref.3), custom_call_target="tpu_custom_call" | custom-call | tf_op jit(solution)/shard_map/request/pallas_call | solution.py:268
  3.7 11.2 %all-to-all-start = ((s32[64,1,128]{2,1,0:T(1,128)}), s32[64,1,128]{2,1,0:T(1,128)S(1)}, u32[]{:S(2)}, u32[]{:S(2)}) async-start(s32[64,1,128]{2,1,0:T(1,128)} %bitcast.5), calls=%async_computation | async-start | bytes 65536 | tf_op jit(solution)/shard_map/all_to_all | solution.py:275
  14.9 2.0 %plan.1 = (s32[20,128]{1,0:T(8,128)}, f32[4,20,128]{2,1,0:T(8,128)}) custom-call(s32[20,4,256]{2,1,0:T(4,128)} %mask_ref.3), custom_call_target="tpu_custom_call" | custom-call | tf_op jit(solution)/shard_map/plan/pallas_call | solution.py:286
  16.9 6.4 %all-to-all-done = s32[64,1,128]{2,1,0:T(1,128)S(1)} async-done(((s32[64,1,128]{2,1,0:T(1,128)}), s32[64,1,128]{2,1,0:T(1,128)S(1)}, u32[]{:S(2)}, u32[]{:S(2)}) %all-to-all-start) | async-done | bytes 32800 | tf_op jit(solution)/shard_map/all_to_all | solution.py:275
  23.3 0.0 collective-permute-done.key_far
  23.3 0.0 collective-permute-done.1.value_far
  23.3 0.0 copy-start.1
  23.3 0.8 copy-done.1
  24.1 11.4 %sort.1 = (bf16[128,256,128]{2,1,0:T(8,128)(2,1)}, bf16[512,128]{1,0:T(8,128)(2,1)S(1)}) custom-call(s32[64,128]{1,0:T(8,128)S(1)} %bitcast.4, s32[20,512]{1,0:T(8,128)S(1)} %copy-done.1, bf16[256,5120]{1,0:T(8,128)(2,1)} %key_own.1, bf16[256,5120]{1,0:T(8,128)(2,1)S(1)} %collective-permute-done.key_far, bf16[256,5120]{1,0:T(8,128)(2,1)} %value_own.1, ...), custom_call_target="tpu_custom_call" | custom-call | tf_op jit(solution)/shard_map/sort/pallas_call | solution.py:296
  35.5 0.0 collective-permute-done.2.query_hbm
  35.5 0.0 copy-start
  35.5 0.0 copy-start.2
  35.5 105.8 %all_to_all.10.got_ref = bf16[128,256,128]{2,1,0:T(8,128)(2,1)} all-to-all(bf16[128,256,128]{2,1,0:T(8,128)(2,1)} %get-tuple-element.24), channel_id=1, replica_groups=mesh['head'=2,'seq'=64] {'seq'}, dimensions={0} | all-to-all | bytes 16777216 | tf_op jit(solution)/shard_map/all_to_all | solution.py:318
  141.4 0.0 copy-done
  141.4 0.0 copy-done.2
  141.4 11.0 %far_rows.1 = (bf16[256,2560]{1,0:T(8,128)(2,1)S(1)}, bf16[80,256,128]{2,1,0:T(8,128)(2,1)S(1)}) custom-call(s32[20,128]{1,0:T(8,128)S(1)} %copy-done.2, bf16[512,128]{1,0:T(8,128)(2,1)S(1)} %get-tuple-element.20.member_ref, f32[4,20,128]{2,1,0:T(8,128)S(1)} %copy-done, bf16[256,5120]{1,0:T(8,128)(2,1)} %collective-permute-done.2.query_hbm, ...), custom_call_target="tpu_custom_call" | custom-call | tf_op jit(solution)/shard_map/far_rows/pallas_call | solution.py:320
  152.4 3.0 %collective-permute-start.3 = (bf16[256,2560]{1,0:T(8,128)(2,1)S(1)}, bf16[256,2560]{1,0:T(8,128)(2,1)S(1)}, u32[]{:S(2)}, u32[]{:S(2)}) collective-permute-start(bf16[256,2560]{1,0:T(8,128)(2,1)S(1)} %get-tuple-element.26), channel_id=1, source_target_pairs={{0,64},{64,0},{1,65},{65,1},{2,66},{66,2},{3,67},{67,3},{4,68},{68... | collective-permute-start | bytes 3932168 | tf_op jit(solution)/shard_map/ppermute | solution.py:280
  155.4 7.2 %own_rows.1.out_in = bf16[256,5120]{1,0:T(8,128)(2,1)} custom-call(bf16[512,128]{1,0:T(8,128)(2,1)S(1)} %get-tuple-element.20.member_ref, f32[4,20,128]{2,1,0:T(8,128)S(1)} %copy-done, bf16[80,256,128]{2,1,0:T(8,128)(2,1)S(1)} %get-tuple-element.25.blocks_ref, bf16[256,5120]{1,0:T(8,128)(2,1)} %query_hbm.1), custom_call_target="tpu_custom_call" | custom-call | tf_op jit(solution)/shard_map/own_rows/pallas_call | solution.py:333
  162.6 0.0 collective-permute-done.3.far_ref
  162.6 1.1 place.1
Async XLA Ops:
  0.0 23.3 %collective-permute-start = (bf16[256,5120]{1,0:T(8,128)(2,1)}, bf16[256,5120]{1,0:T(8,128)(2,1)S(1)}, u32[]{:S(2)}, u32[]{:S(2)}) collective-permute-start(bf16[256,5120]{1,0:T(8,128)(2,1)} %key_own.1), channel_id=1, source_target_pairs={{0,64},{64,0},{1,65},{65,1},{2,66},{66,2},{3,67},{67,3},{4,68},{68... | collective-permute-start | bytes 7864328 | tf_op jit(solution)/shard_map/ppermute | solution.py:280
  1.4 21.9 %collective-permute-start.1 = (bf16[256,5120]{1,0:T(8,128)(2,1)}, bf16[256,5120]{1,0:T(8,128)(2,1)}, u32[]{:S(2)}, u32[]{:S(2)}) collective-permute-start(bf16[256,5120]{1,0:T(8,128)(2,1)} %value_own.1), channel_id=1, source_target_pairs={{0,64},{64,0},{1,65},{65,1},{2,66},{66,2},{3,67},{67,3},{4,68},{68... | collective-permute-start | bytes 7864328 | tf_op jit(solution)/shard_map/ppermute | solution.py:280
  1.4 34.1 %collective-permute-start.2 = (bf16[256,5120]{1,0:T(8,128)(2,1)}, bf16[256,5120]{1,0:T(8,128)(2,1)}, u32[]{:S(2)}, u32[]{:S(2)}) collective-permute-start(bf16[256,5120]{1,0:T(8,128)(2,1)} %query_hbm.1), channel_id=1, source_target_pairs={{0,64},{64,0},{1,65},{65,1},{2,66},{66,2},{3,67},{67,3},{4,68},{68... | collective-permute-start | bytes 7864328 | tf_op jit(solution)/shard_map/ppermute | solution.py:280
  3.7 19.6 %all-to-all-start = ((s32[64,1,128]{2,1,0:T(1,128)}), s32[64,1,128]{2,1,0:T(1,128)S(1)}, u32[]{:S(2)}, u32[]{:S(2)}) async-start(s32[64,1,128]{2,1,0:T(1,128)} %bitcast.5), calls=%async_computation | async-start | bytes 65536 | tf_op jit(solution)/shard_map/all_to_all | solution.py:275
  23.3 0.8 copy-start.1
  35.5 105.9 %copy-start = (f32[4,20,128]{2,1,0:T(8,128)S(1)}, f32[4,20,128]{2,1,0:T(8,128)}, u32[]{:S(2)}) copy-start(f32[4,20,128]{2,1,0:T(8,128)} %get-tuple-element.21.bias_ref) | copy-start | bytes 122884
  35.5 105.8 %copy-start.2 = (s32[20,128]{1,0:T(8,128)S(1)}, s32[20,128]{1,0:T(8,128)}, u32[]{:S(2)}) copy-start(s32[20,128]{1,0:T(8,128)} %get-tuple-element.22.position_ref) | copy-start | bytes 30724
  152.4 10.2 %collective-permute-start.3 = (bf16[256,2560]{1,0:T(8,128)(2,1)S(1)}, bf16[256,2560]{1,0:T(8,128)(2,1)S(1)}, u32[]{:S(2)}, u32[]{:S(2)}) collective-permute-start(bf16[256,2560]{1,0:T(8,128)(2,1)S(1)} %get-tuple-element.26), channel_id=1, source_target_pairs={{0,64},{64,0},{1,65},{65,1},{2,66},{66,2},{3,67},{67,3},{4,68},{68... | collective-permute-start | bytes 3932168 | tf_op jit(solution)/shard_map/ppermute | solution.py:280

commit v5 on v4

--- a/solution.py
+++ b/solution.py
@@ -12,7 +12,13 @@
 CAPACITY = 2
 PICKS = 4
 HEADS_STEP = 4
+SORT_STEP = 10
+GATHERS = 1
 MASKED = -1e30
+
+
+def shift_of(count):
+    return count.bit_length() - 1
 
 
 def slot_lows(needed, shard_blocks):
@@ -20,9 +26,9 @@
     shards = blocks // shard_blocks
     key_block = lax.broadcasted_iota(jnp.int32, (heads, blocks), 1)
     head = lax.broadcasted_iota(jnp.int32, (heads, blocks), 0)
-    pair = head * shard_blocks + lax.rem(key_block, shard_blocks)
+    pair = head * shard_blocks + jnp.bitwise_and(key_block, shard_blocks - 1)
     low = jnp.min(jnp.where(needed > 0, pair, heads * shard_blocks), axis=0, keepdims=True)
-    owner = lax.broadcasted_iota(jnp.int32, (shards, blocks), 1) // shard_blocks
+    owner = lax.broadcasted_iota(jnp.int32, (shards, blocks), 1) >> shift_of(shard_blocks)
     mine = owner == lax.broadcasted_iota(jnp.int32, (shards, blocks), 0)
     low_col = jnp.min(jnp.where(mine, low, heads * shard_blocks), axis=1, keepdims=True)
     return pair, mine, low_col
@@ -34,8 +40,8 @@
     pair, mine, low_col = slot_lows(needed, shard_blocks)
     high = jnp.max(jnp.where(needed > 0, pair, -1), axis=0, keepdims=True)
     high_col = jnp.max(jnp.where(mine, high, -1), axis=1, keepdims=True)
-    low_col = jnp.minimum(low_col, heads * shard_blocks - 1)
-    high_col = jnp.maximum(high_col, 0)
+    high_col = jnp.where(high_col == low_col, -1, high_col)
+    low_col = jnp.where(low_col == heads * shard_blocks, -1, low_col)
     lane = lax.broadcasted_iota(jnp.int32, table_ref.shape, 1)
     table_ref[...] = jnp.where(lane == 0, low_col, high_col)
 
@@ -51,7 +57,7 @@
     pair, mine, low_col = slot_lows(needed, shard_blocks)
     low_own = jnp.min(jnp.where(mine, low_col, heads * shard_blocks), axis=0, keepdims=True)
     key_block = lax.broadcasted_iota(jnp.int32, (heads, blocks), 1)
-    slot = (key_block // shard_blocks) * CAPACITY + (pair != low_own).astype(jnp.int32)
+    slot = (key_block >> shift_of(shard_blocks)) * CAPACITY + (pair != low_own).astype(jnp.int32)
     upper = (
         lax.broadcasted_iota(jnp.int32, (blocks, blocks), 0)
         < lax.broadcasted_iota(jnp.int32, (blocks, blocks), 1)
@@ -77,11 +83,12 @@
 
 
 def sort_kernel(
-    request_ref, perm_ref, key_own, key_far, value_own, value_far,
-    send_ref, member_ref, perm_pad, member_pad, buf, out_ref, sem, send_sem,
+    request_ref, perm_hbm, key_own, key_far, value_own, value_far,
+    send_ref, member_ref, perm_raw, perm_pad, member_pad, buf, out_ref, sem, perm_sem, send_sem,
 ):
-    heads, rows = perm_ref.shape
+    heads, rows = perm_hbm.shape
     steps, _, half, step_width = buf.shape
+    step_heads = step_width // HEAD_DIM
     shard_blocks = rows // BLOCK
     base = lax.axis_index("head") * (heads * HEAD_DIM)
 
@@ -92,45 +99,78 @@
             for n, ref in enumerate((key_own, value_own, key_far, value_far))
         ]
 
+    perm_copy = pltpu.make_async_copy(perm_hbm, perm_raw, perm_sem)
+    perm_copy.start()
     for g in range(steps):
         for copy in copies(g):
             copy.start()
-    perm_pad[0:heads, :] = local_tokens(perm_ref[...], rows)
-    column = jnp.transpose(perm_pad[...])
-    token = lax.broadcasted_iota(jnp.int32, (rows, rows), 1)
-    member_pad[heads * shard_blocks :, :] = jnp.zeros(
-        (member_pad.shape[0] - heads * shard_blocks, rows), jnp.float32
-    )
-    for g in range(steps):
-        for copy in copies(g):
-            copy.wait()
-        for k in range(HEADS_STEP):
-            h = g * HEADS_STEP + k
-            cut = slice(k * HEAD_DIM, (k + 1) * HEAD_DIM)
-            order = jnp.where(column[:, h : h + 1] == token, 1.0, 0.0)
-            own = jnp.concatenate([buf[g, 0, :, cut], buf[g, 1, :, cut]], axis=1)
-            far = jnp.concatenate([buf[g, 2, :, cut], buf[g, 3, :, cut]], axis=1)
-            both = jnp.concatenate([own, far], axis=0)
-            ordered = jnp.dot(
-                order.astype(jnp.bfloat16), both, preferred_element_type=jnp.float32
-            ).astype(jnp.bfloat16)
-            for b in range(shard_blocks):
-                part = slice(b * BLOCK, (b + 1) * BLOCK)
-                row = h * shard_blocks + b
-                member_pad[row : row + 1, :] = jnp.sum(order[part], axis=0, keepdims=True)
-                out_ref[row, 0:BLOCK] = ordered[part, :HEAD_DIM]
-                out_ref[row, BLOCK : 2 * BLOCK] = ordered[part, HEAD_DIM:]
-
-    def start(d, carry):
+    pairs = heads * shard_blocks
+    member_pad[pairs:, :] = jnp.zeros((member_pad.shape[0] - pairs, rows), jnp.float32)
+    token = lax.broadcasted_iota(jnp.int32, (rows, half), 1)
+    token = token.astype(jnp.float32).astype(jnp.bfloat16)
+    perm_copy.wait()
+    perm_pad[0:heads, :] = perm_raw[...]
+    column = jnp.transpose(local_tokens(perm_pad[...], rows))
+    own_column = jnp.where(column < half, column, -1).astype(jnp.float32)
+    far_column = jnp.where(column < half, -1, column - half).astype(jnp.float32)
+
+    def order_of(h):
+        parts = []
+        for table in (own_column, far_column):
+            wide = jnp.broadcast_to(table[:, h : h + 1], (rows, 128)).astype(jnp.bfloat16)
+            wide = jnp.tile(wide, (1, half // 128))
+            parts.append(jnp.where(wide == token, jnp.bfloat16(1.0), jnp.bfloat16(0.0)))
+        return jnp.concatenate(parts, axis=1)
+
+    def block_sum(part):
+        while part.shape[0] > 16:
+            middle = part.shape[0] // 2
+            part = part[:middle] + part[middle:]
+        return jnp.sum(part.astype(jnp.float32), axis=0, keepdims=True)
+
+    following = order_of(0)
+    for h in range(heads):
+        order = following
+        if h + 1 < heads:
+            following = order_of(h + 1)
+        g, k = divmod(h, step_heads)
+        if k == 0:
+            for copy in copies(g):
+                copy.wait()
+        cut = slice(k * HEAD_DIM, (k + 1) * HEAD_DIM)
+        own = jnp.concatenate([buf[g, 0, :, cut], buf[g, 1, :, cut]], axis=1)
+        far = jnp.concatenate([buf[g, 2, :, cut], buf[g, 3, :, cut]], axis=1)
+        ordered = jnp.dot(
+            order, jnp.concatenate([own, far], axis=0), preferred_element_type=jnp.float32
+        ).astype(jnp.bfloat16)
+        for b in range(shard_blocks):
+            part = slice(b * BLOCK, (b + 1) * BLOCK)
+            row = h * shard_blocks + b
+            member_pad[row : row + 1, :] = block_sum(order[part])
+            out_ref[row, 0:BLOCK] = ordered[part, :HEAD_DIM]
+            out_ref[row, BLOCK : 2 * BLOCK] = ordered[part, HEAD_DIM:]
+
+    def start(d, count):
         for j in range(CAPACITY):
-            pltpu.make_async_copy(
-                out_ref.at[request_ref[d, j]], send_ref.at[d * CAPACITY + j], send_sem
-            ).start()
+            asked = request_ref[d, j]
+
+            @pl.when(asked >= 0)
+            def _():
+                pltpu.make_async_copy(
+                    out_ref.at[asked], send_ref.at[d * CAPACITY + j], send_sem
+                ).start()
+
+            count = count + (asked >= 0).astype(jnp.int32)
+        return count
+
+    started = lax.fori_loop(0, request_ref.shape[0], start, jnp.int32(0), unroll=8)
+    member_ref[...] = jnp.transpose(member_pad[...]).astype(jnp.bfloat16)
+
+    def finish(n, carry):
+        pltpu.make_async_copy(out_ref.at[0], send_ref.at[0], send_sem).wait()
         return carry
 
-    lax.fori_loop(0, request_ref.shape[0], start, 0, unroll=8)
-    member_ref[...] = jnp.transpose(member_pad[...]).astype(jnp.bfloat16)
-    pltpu.make_async_copy(send_ref, send_ref, send_sem).wait()
+    lax.fori_loop(0, started, finish, 0)
 
 
 def score(h, query, member, bias_ref, blocks_ref):
@@ -150,12 +190,15 @@
 def mix(h, scores, blocks_ref):
     top = jnp.max(scores, axis=1, keepdims=True)
     exponent = jnp.exp2((scores - top) * (math.log2(math.e) / math.sqrt(HEAD_DIM)))
-    total = jnp.sum(exponent, axis=1, keepdims=True)
-    weights = (exponent * (1.0 / total)).astype(jnp.bfloat16)
+    weights = exponent.astype(jnp.bfloat16)
     values = jnp.concatenate(
         [blocks_ref[h * PICKS + j, BLOCK : 2 * BLOCK] for j in range(PICKS)], axis=0
     )
-    return jnp.dot(weights, values, preferred_element_type=jnp.float32).astype(jnp.bfloat16)
+    ones = jnp.ones((PICKS * BLOCK, HEAD_DIM), jnp.bfloat16)
+    mixed = jnp.dot(
+        weights, jnp.concatenate([values, ones], axis=1), preferred_element_type=jnp.float32
+    )
+    return (mixed[:, :HEAD_DIM] / mixed[:, HEAD_DIM:]).astype(jnp.bfloat16)
 
 
 def attend(heads, ready, query_ref, member, bias_ref, blocks_ref, finish):
@@ -172,33 +215,50 @@
         finish(h, mix(h, scores, blocks_ref))
 
 
-def query_copy(query_hbm, query_ref, sem):
+def query_copies(query_hbm, query_ref, sem):
     width = query_ref.shape[1]
-    cut = pl.ds(pl.multiple_of(lax.axis_index("head") * width, 128), width)
-    return pltpu.make_async_copy(query_hbm.at[:, cut], query_ref, sem)
+    count = sem.shape[0]
+    base = lax.axis_index("head") * width
+    step_width = width // count
+    return [
+        pltpu.make_async_copy(
+            query_hbm.at[:, pl.ds(pl.multiple_of(base + g * step_width, 128), step_width)],
+            query_ref.at[:, g * step_width : (g + 1) * step_width],
+            sem.at[g],
+        )
+        for g in range(count)
+    ]
 
 
 def far_kernel(
-    position_ref, member_ref, bias_ref, query_hbm, got_ref, out_ref, blocks_ref, query_ref, sem
+    position_ref, member_ref, bias_ref, query_hbm, got_ref,
+    out_ref, blocks_ref, query_ref, sem, query_sem,
 ):
     heads = position_ref.shape[0]
     half = out_ref.shape[0]
-    load = query_copy(query_hbm, query_ref, sem.at[heads])
-    load.start()
+    group = heads // sem.shape[0]
+    loads = query_copies(query_hbm, query_ref, query_sem)
 
     def start(h, carry):
         for j in range(PICKS):
             pltpu.make_async_copy(
-                got_ref.at[position_ref[h, j]], blocks_ref.at[h * PICKS + j], sem.at[h]
+                got_ref.at[position_ref[h, j]], blocks_ref.at[h * PICKS + j], sem.at[h // group]
             ).start()
         return carry
 
-    lax.fori_loop(0, heads, start, 0, unroll=4)
-    load.wait()
+    for h in range(group):
+        start(h, 0)
+    for load in loads:
+        load.start()
+    for h in range(group, heads):
+        start(h, 0)
+    for load in loads:
+        load.wait()
 
     def ready(h):
-        part = blocks_ref.at[h * PICKS : (h + 1) * PICKS]
-        pltpu.make_async_copy(part, part, sem.at[h]).wait()
+        if h % group == 0:
+            part = blocks_ref.at[h * PICKS : (h + group) * PICKS]
+            pltpu.make_async_copy(part, part, sem.at[h // group]).wait()
 
     def finish(h, mixed):
         out_ref[:, h * HEAD_DIM : (h + 1) * HEAD_DIM] = mixed
@@ -213,8 +273,9 @@
     heads = width // HEAD_DIM
     step_width = HEADS_STEP * HEAD_DIM
     base = lax.axis_index("head") * width
-    load = query_copy(query_hbm, query_ref, query_sem)
-    load.start()
+    loads = query_copies(query_hbm, query_ref, query_sem)
+    for load in loads:
+        load.start()
 
     def copy(g):
         return pltpu.make_async_copy(
@@ -228,10 +289,12 @@
         if h % HEADS_STEP == HEADS_STEP - 1:
             copy(h // HEADS_STEP).start()
 
-    load.wait()
-    attend(
-        heads, lambda h: None, query_ref, member_ref[:half, :], bias_ref, blocks_ref, finish
-    )
+    def ready(h):
+        if h == 0:
+            for load in loads:
+                load.wait()
+
+    attend(heads, ready, query_ref, member_ref[:half, :], bias_ref, blocks_ref, finish)
     for g in range(heads // HEADS_STEP):
         copy(g).wait()
 
@@ -299,19 +362,21 @@
             hbm_out((slots, 2 * BLOCK, HEAD_DIM), bf16),
             held_out((rows, 128), bf16),
         ],
-        in_specs=[smem, vmem, hbm, hbm, hbm, hbm],
+        in_specs=[smem, hbm, hbm, hbm, hbm, hbm],
         out_specs=[hbm, vmem],
         scratch_shapes=[
+            pltpu.VMEM((heads, rows), jnp.int32),
             pltpu.VMEM((128, rows), jnp.int32),
             pltpu.VMEM((128, rows), jnp.float32),
-            pltpu.VMEM((steps, 4, half, HEADS_STEP * HEAD_DIM), bf16),
+            pltpu.VMEM((heads // SORT_STEP, 4, half, SORT_STEP * HEAD_DIM), bf16),
             pltpu.VMEM((pairs, 2 * BLOCK, HEAD_DIM), bf16),
-            dma((steps, 4)),
+            dma((heads // SORT_STEP, 4)),
+            dma,
             dma,
         ],
         compiler_params=limit(32),
         name="sort",
-    )(requested, cluster_perm, far(key_states), key_far, far(value_states), value_far)
+    )(requested, far(cluster_perm), far(key_states), key_far, far(value_states), value_far)
     send, member, position, bias, query_far = lax.optimization_barrier(
         (send, member, position, bias, query_far)
     )
@@ -325,7 +390,7 @@
         ],
         in_specs=[smem, vmem, vmem, hbm, hbm],
         out_specs=[vmem, vmem],
-        scratch_shapes=[pltpu.VMEM((half, width), bf16), dma((heads + 1,))],
+        scratch_shapes=[pltpu.VMEM((half, width), bf16), dma((GATHERS,)), dma((1,))],
         compiler_params=limit(32),
         name="far_rows",
     )(position, held(member), bias, query_far, far(got))
@@ -339,7 +404,7 @@
             pltpu.VMEM((half, width), bf16),
             pltpu.VMEM((half, width), bf16),
             dma((steps,)),
-            dma,
+            dma((1,)),
         ],
         compiler_params=limit(32),
         name="own_rows",

time: 164 us -> 154 us (0.939)
  Pallas kernels: 34.4 us -> 25.5 us
    pallas_call x1, Pallas kernels: 11 us -> 7.12 us  [shards(): pl.pallas_call(far_kernel, out_shape=[held_out((half, width), bf16), held...]
    pallas_call x1, Pallas kernels: 11.4 us -> 8.1 us  [shards(): pl.pallas_call(sort_kernel, out_shape=[hbm_out((slots, 2 * BLOCK, HEAD_DI...]
    pallas_call x1, Pallas kernels: 7.18 us -> 5.39 us  [shards(): pl.pallas_call(own_kernel, out_shape=hbm_out((half, columns), bf16), in_s...]
  transfers between devices with their start and end apart: 5 -> 5, of which waited for: 1 -> 1; matrix products, arithmetic and copies ran while one was open for 0% -> 0% of each run, Pallas kernels for 14% -> 11%
where the time goes in v5:
time: 154 us
  blocking collectives  106 us (69%)
  Pallas kernels  25.5 us (17%)
  starting transfers between devices  16.3 us (11%)
  waiting for transfers between devices  6.37 us (4%)
    all_to_all x1, blocking collectives, shards(): got = lax.all_to_all(send, 'seq', split_axis=0, concat_axis=0, tiled=True)  106 us
    all_to_all x1, starting transfers between devices, shards(): lax.all_to_all(table.reshape(seq_count, 1, 128), 'seq', split_axis=0, con...  11.2 us
    pallas_call x1, Pallas kernels, shards(): pl.pallas_call(sort_kernel, out_shape=[hbm_out((slots, 2 * BLOCK, HEAD_DI...  8.1 us
    pallas_call x1, Pallas kernels, shards(): pl.pallas_call(far_kernel, out_shape=[held_out((half, width), bf16), held...  7.12 us
    all_to_all x1, waiting for transfers between devices, shards(): lax.all_to_all(table.reshape(seq_count, 1, 128), 'seq', split_axis=0, con...  6.36 us
    pallas_call x1, Pallas kernels, shards(): pl.pallas_call(own_kernel, out_shape=hbm_out((half, columns), bf16), in_s...  5.39 us
    ppermute x4, starting transfers between devices, swap(): return lax.ppermute(x, 'head', [(0, 1), (1, 0)])  5.12 us
  transfers between devices with their start and end apart: 5, of which 1 were waited for; matrix products, arithmetic and copies ran while one was open for 0% of the time, Pallas kernels for 11%

profile of v5, /device:TPU:1, one launch (start us, length us, event | category | flops | bytes accessed | tf_op | source)
XLA Modules:
  0.0 153.9 jit_solution(9999696204170818308)
XLA Ops:
  0.0 1.4 collective-permute-start
  1.4 0.0 collective-permute-start.1
  1.4 0.5 collective-permute-start.2
  1.9 1.8 %request.1 = s32[64,128]{1,0:T(8,128)} custom-call(s32[20,4,256]{2,1,0:T(4,128)} %mask_ref.3), custom_call_target="tpu_custom_call" | custom-call | tf_op jit(solution)/shard_map/request/pallas_call | solution.py:331
  3.7 11.2 %all-to-all-start = ((s32[64,1,128]{2,1,0:T(1,128)}), s32[64,1,128]{2,1,0:T(1,128)S(1)}, u32[]{:S(2)}, u32[]{:S(2)}) async-start(s32[64,1,128]{2,1,0:T(1,128)} %bitcast.5), calls=%async_computation | async-start | bytes 65536 | tf_op jit(solution)/shard_map/all_to_all | solution.py:338
  14.9 2.0 %plan.1 = (s32[20,128]{1,0:T(8,128)}, f32[4,20,128]{2,1,0:T(8,128)}) custom-call(s32[20,4,256]{2,1,0:T(4,128)} %mask_ref.3), custom_call_target="tpu_custom_call" | custom-call | tf_op jit(solution)/shard_map/plan/pallas_call | solution.py:349
  16.9 6.4 %all-to-all-done = s32[64,1,128]{2,1,0:T(1,128)S(1)} async-done(((s32[64,1,128]{2,1,0:T(1,128)}), s32[64,1,128]{2,1,0:T(1,128)S(1)}, u32[]{:S(2)}, u32[]{:S(2)}) %all-to-all-start) | async-done | bytes 32800 | tf_op jit(solution)/shard_map/all_to_all | solution.py:338
  23.3 0.0 collective-permute-done.key_far
  23.3 0.0 collective-permute-done.1.value_far
  23.3 8.1 %sort.1 = (bf16[128,256,128]{2,1,0:T(8,128)(2,1)}, bf16[512,128]{1,0:T(8,128)(2,1)S(1)}) custom-call(s32[64,128]{1,0:T(8,128)S(1)} %bitcast.4, s32[20,512]{1,0:T(8,128)} %perm_hbm.1, bf16[256,5120]{1,0:T(8,128)(2,1)} %key_own.1, bf16[256,5120]{1,0:T(8,128)(2,1)S(1)} %collective-permute-done.key_far, bf16[256,5120]{1,0:T(8,128)(2,1)} %value_own.1, ...), custom_call_target="tpu_custom_call" | custom-call | tf_op jit(solution)/shard_map/sort/pallas_call | solution.py:359
  31.4 0.0 collective-permute-done.2.query_hbm
  31.4 0.0 copy-start
  31.4 0.0 copy-start.1
  31.4 105.5 %all_to_all.10.got_ref = bf16[128,256,128]{2,1,0:T(8,128)(2,1)} all-to-all(bf16[128,256,128]{2,1,0:T(8,128)(2,1)} %get-tuple-element.24), channel_id=1, replica_groups=mesh['head'=2,'seq'=64] {'seq'}, dimensions={0} | all-to-all | bytes 16777216 | tf_op jit(solution)/shard_map/all_to_all | solution.py:383
  137.0 0.0 copy-done
  137.0 0.0 copy-done.1
  137.0 7.1 %far_rows.1 = (bf16[256,2560]{1,0:T(8,128)(2,1)S(1)}, bf16[80,256,128]{2,1,0:T(8,128)(2,1)S(1)}) custom-call(s32[20,128]{1,0:T(8,128)S(1)} %copy-done.1, bf16[512,128]{1,0:T(8,128)(2,1)S(1)} %get-tuple-element.20.member_ref, f32[4,20,128]{2,1,0:T(8,128)S(1)} %copy-done, bf16[256,5120]{1,0:T(8,128)(2,1)} %collective-permute-done.2.query_hbm, ...), custom_call_target="tpu_custom_call" | custom-call | tf_op jit(solution)/shard_map/far_rows/pallas_call | solution.py:385
  144.1 3.2 %collective-permute-start.3 = (bf16[256,2560]{1,0:T(8,128)(2,1)S(1)}, bf16[256,2560]{1,0:T(8,128)(2,1)S(1)}, u32[]{:S(2)}, u32[]{:S(2)}) collective-permute-start(bf16[256,2560]{1,0:T(8,128)(2,1)S(1)} %get-tuple-element.26), channel_id=1, source_target_pairs={{0,64},{64,0},{1,65},{65,1},{2,66},{66,2},{3,67},{67,3},{4,68},{68... | collective-permute-start | bytes 3932168 | tf_op jit(solution)/shard_map/ppermute | solution.py:343
  147.3 5.4 %own_rows.1.out_in = bf16[256,5120]{1,0:T(8,128)(2,1)} custom-call(bf16[512,128]{1,0:T(8,128)(2,1)S(1)} %get-tuple-element.20.member_ref, f32[4,20,128]{2,1,0:T(8,128)S(1)} %copy-done, bf16[80,256,128]{2,1,0:T(8,128)(2,1)S(1)} %get-tuple-element.25.blocks_ref, bf16[256,5120]{1,0:T(8,128)(2,1)} %query_hbm.1), custom_call_target="tpu_custom_call" | custom-call | tf_op jit(solution)/shard_map/own_rows/pallas_call | solution.py:398
  152.7 0.0 collective-permute-done.3.far_ref
  152.7 1.1 place.1
Async XLA Ops:
  0.0 23.3 %collective-permute-start = (bf16[256,5120]{1,0:T(8,128)(2,1)}, bf16[256,5120]{1,0:T(8,128)(2,1)S(1)}, u32[]{:S(2)}, u32[]{:S(2)}) collective-permute-start(bf16[256,5120]{1,0:T(8,128)(2,1)} %key_own.1), channel_id=1, source_target_pairs={{0,64},{64,0},{1,65},{65,1},{2,66},{66,2},{3,67},{67,3},{4,68},{68... | collective-permute-start | bytes 7864328 | tf_op jit(solution)/shard_map/ppermute | solution.py:343
  1.4 21.9 %collective-permute-start.1 = (bf16[256,5120]{1,0:T(8,128)(2,1)}, bf16[256,5120]{1,0:T(8,128)(2,1)}, u32[]{:S(2)}, u32[]{:S(2)}) collective-permute-start(bf16[256,5120]{1,0:T(8,128)(2,1)} %value_own.1), channel_id=1, source_target_pairs={{0,64},{64,0},{1,65},{65,1},{2,66},{66,2},{3,67},{67,3},{4,68},{68... | collective-permute-start | bytes 7864328 | tf_op jit(solution)/shard_map/ppermute | solution.py:343
  1.4 30.0 %collective-permute-start.2 = (bf16[256,5120]{1,0:T(8,128)(2,1)}, bf16[256,5120]{1,0:T(8,128)(2,1)}, u32[]{:S(2)}, u32[]{:S(2)}) collective-permute-start(bf16[256,5120]{1,0:T(8,128)(2,1)} %query_hbm.1), channel_id=1, source_target_pairs={{0,64},{64,0},{1,65},{65,1},{2,66},{66,2},{3,67},{67,3},{4,68},{68... | collective-permute-start | bytes 7864328 | tf_op jit(solution)/shard_map/ppermute | solution.py:343
  3.7 19.6 %all-to-all-start = ((s32[64,1,128]{2,1,0:T(1,128)}), s32[64,1,128]{2,1,0:T(1,128)S(1)}, u32[]{:S(2)}, u32[]{:S(2)}) async-start(s32[64,1,128]{2,1,0:T(1,128)} %bitcast.5), calls=%async_computation | async-start | bytes 65536 | tf_op jit(solution)/shard_map/all_to_all | solution.py:338
  31.4 105.6 %copy-start = (f32[4,20,128]{2,1,0:T(8,128)S(1)}, f32[4,20,128]{2,1,0:T(8,128)}, u32[]{:S(2)}) copy-start(f32[4,20,128]{2,1,0:T(8,128)} %get-tuple-element.21.bias_ref) | copy-start | bytes 122884
  31.4 105.5 %copy-start.1 = (s32[20,128]{1,0:T(8,128)S(1)}, s32[20,128]{1,0:T(8,128)}, u32[]{:S(2)}) copy-start(s32[20,128]{1,0:T(8,128)} %get-tuple-element.22.position_ref) | copy-start | bytes 30724
  144.1 8.6 %collective-permute-start.3 = (bf16[256,2560]{1,0:T(8,128)(2,1)S(1)}, bf16[256,2560]{1,0:T(8,128)(2,1)S(1)}, u32[]{:S(2)}, u32[]{:S(2)}) collective-permute-start(bf16[256,2560]{1,0:T(8,128)(2,1)S(1)} %get-tuple-element.26), channel_id=1, source_target_pairs={{0,64},{64,0},{1,65},{65,1},{2,66},{66,2},{3,67},{67,3},{4,68},{68... | collective-permute-start | bytes 3932168 | tf_op jit(solution)/shard_map/ppermute | solution.py:343

commit v6 on v5

v6 whole, which is shorter than its diff:
```python
import functools
import math

import jax
import jax.numpy as jnp
from jax import lax
from jax.experimental import pallas as pl
from jax.experimental.pallas import tpu as pltpu
from jax.sharding import PartitionSpec as P

HEAD_DIM = 128
BLOCK = 128
CAPACITY = 2
PICKS = 4
EARLY = 8
SORT_STEP = 6
LAST = 6
MASKED = -1e30


def shift_of(count):
    return count.bit_length() - 1


def slot_lows(needed, shard_blocks):
    heads, blocks = needed.shape
    shards = blocks // shard_blocks
    key_block = lax.broadcasted_iota(jnp.int32, (heads, blocks), 1)
    head = lax.broadcasted_iota(jnp.int32, (heads, blocks), 0)
    pair = head * shard_blocks + jnp.bitwise_and(key_block, shard_blocks - 1)
    low = jnp.min(jnp.where(needed > 0, pair, heads * shard_blocks), axis=0, keepdims=True)
    owner = lax.broadcasted_iota(jnp.int32, (shards, blocks), 1) >> shift_of(shard_blocks)
    mine = owner == lax.broadcasted_iota(jnp.int32, (shards, blocks), 0)
    low_col = jnp.min(jnp.where(mine, low, heads * shard_blocks), axis=1, keepdims=True)
    return pair, mine, low_col


def request_kernel(mask_ref, table_ref):
    heads, shard_blocks, _ = mask_ref.shape
    needed = jnp.max(mask_ref[...], axis=1)
    pair, mine, low_col = slot_lows(needed, shard_blocks)
    high = jnp.max(jnp.where(needed > 0, pair, -1), axis=0, keepdims=True)
    high_col = jnp.max(jnp.where(mine, high, -1), axis=1, keepdims=True)
    high_col = jnp.where(high_col == low_col, -1, high_col)
    low_col = jnp.where(low_col == heads * shard_blocks, -1, low_col)
    lane = lax.broadcasted_iota(jnp.int32, table_ref.shape, 1)
    table_ref[...] = jnp.where(lane == 0, low_col, high_col)


def local_tokens(perm, rows):
    return jnp.bitwise_and(perm + lax.axis_index("head") * (rows // 2), rows - 1)


def plan_kernel(mask_ref, position_ref, bias_ref):
    heads, shard_blocks, blocks = mask_ref.shape
    mask = mask_ref[...]
    needed = jnp.max(mask, axis=1)
    pair, mine, low_col = slot_lows(needed, shard_blocks)
    low_own = jnp.min(jnp.where(mine, low_col, heads * shard_blocks), axis=0, keepdims=True)
    key_block = lax.broadcasted_iota(jnp.int32, (heads, blocks), 1)
    slot = (key_block >> shift_of(shard_blocks)) * CAPACITY + (pair != low_own).astype(jnp.int32)
    upper = (
        lax.broadcasted_iota(jnp.int32, (blocks, blocks), 0)
        < lax.broadcasted_iota(jnp.int32, (blocks, blocks), 1)
    )
    prefix = jnp.dot(
        needed.astype(jnp.float32).astype(jnp.bfloat16),
        jnp.where(upper, 1.0, 0.0).astype(jnp.bfloat16),
        preferred_element_type=jnp.float32,
    )
    lane = lax.broadcasted_iota(jnp.int32, (heads, 128), 1)
    row = lax.broadcasted_iota(jnp.int32, (heads, 128), 0)
    position = jnp.zeros((heads, 128), jnp.int32)
    for j in range(PICKS):
        chosen = (needed > 0) & (prefix == float(j))
        slot_j = jnp.sum(jnp.where(chosen, slot, 0), axis=1, keepdims=True)
        position = jnp.where(lane == j, slot_j, position)
        bias = jnp.zeros((heads, 128), jnp.float32)
        for q in range(shard_blocks):
            live = jnp.max(jnp.where(chosen, mask[:, q, :], 0), axis=1, keepdims=True)
            bias = jnp.where((lane == row * shard_blocks + q) & (live == 0), MASKED, bias)
        bias_ref[j] = bias
    position_ref[...] = position


def sort_heads(
    first, perm_hbm, sources, out_ref, member_pad, perm_raw, perm_pad, buf, sem, perm_sem
):
    heads, rows = perm_hbm.shape
    steps, _, half, step_width = buf.shape
    step_heads = step_width // HEAD_DIM
    count = steps * step_heads
    shard_blocks = rows // BLOCK
    base = (lax.axis_index("head") * heads + first) * HEAD_DIM

    def copies(g):
        cut = pl.ds(pl.multiple_of(base + g * step_width, 128), step_width)
        return [
            pltpu.make_async_copy(ref.at[:, cut], buf.at[g, n], sem.at[g, n])
            for n, ref in enumerate(sources)
        ]

    perm_copy = pltpu.make_async_copy(perm_hbm, perm_raw, perm_sem)
    perm_copy.start()
    for g in range(steps):
        for copy in copies(g):
            copy.start()
    member_pad[...] = jnp.zeros(member_pad.shape, jnp.float32)
    token = lax.broadcasted_iota(jnp.int32, (rows, half), 1)
    token = token.astype(jnp.float32).astype(jnp.bfloat16)
    perm_copy.wait()
    perm_pad[0:heads, :] = perm_raw[...]
    column = jnp.transpose(local_tokens(perm_pad[...], rows))
    own_column = jnp.where(column < half, column, -1).astype(jnp.float32)
    far_column = jnp.where(column < half, -1, column - half).astype(jnp.float32)

    def order_of(h):
        parts = []
        for table in (own_column, far_column):
            wide = jnp.broadcast_to(table[:, h : h + 1], (rows, 128)).astype(jnp.bfloat16)
            wide = jnp.tile(wide, (1, half // 128))
            parts.append(jnp.where(wide == token, jnp.bfloat16(1.0), jnp.bfloat16(0.0)))
        return jnp.concatenate(parts, axis=1)

    def block_sum(part):
        while part.shape[0] > 16:
            middle = part.shape[0] // 2
            part = part[:middle] + part[middle:]
        return jnp.sum(part.astype(jnp.float32), axis=0, keepdims=True)

    following = order_of(first)
    for n in range(count):
        order = following
        if n + 1 < count:
            following = order_of(first + n + 1)
        g, k = divmod(n, step_heads)
        if k == 0:
            for copy in copies(g):
                copy.wait()
        cut = slice(k * HEAD_DIM, (k + 1) * HEAD_DIM)
        own = jnp.concatenate([buf[g, 0, :, cut], buf[g, 1, :, cut]], axis=1)
        far = jnp.concatenate([buf[g, 2, :, cut], buf[g, 3, :, cut]], axis=1)
        ordered = jnp.dot(
            order, jnp.concatenate([own, far], axis=0), preferred_element_type=jnp.float32
        ).astype(jnp.bfloat16)
        for b in range(shard_blocks):
            part = slice(b * BLOCK, (b + 1) * BLOCK)
            row = (first + n) * shard_blocks + b
            member_pad[row : row + 1, :] = block_sum(order[part])
            slot = n * shard_blocks + b
            out_ref[slot, 0:BLOCK] = ordered[part, :HEAD_DIM]
            out_ref[slot, BLOCK : 2 * BLOCK] = ordered[part, HEAD_DIM:]
    return jnp.transpose(member_pad[...])


def early_kernel(
    perm_hbm, key_own, key_far, value_own, value_far,
    early_ref, member_ref, perm_raw, perm_pad, member_pad, buf, blocks, sem, perm_sem, out_sem,
):
    sources = (key_own, value_own, key_far, value_far)
    member = sort_heads(
        0, perm_hbm, sources, blocks, member_pad, perm_raw, perm_pad, buf, sem, perm_sem
    )
    copy = pltpu.make_async_copy(blocks, early_ref, out_sem)
    copy.start()
    member_ref[...] = member.astype(jnp.bfloat16)
    copy.wait()


def sort_kernel(
    request_ref, perm_hbm, key_own, key_far, value_own, value_far, early_ref, early_member,
    send_ref, member_ref, perm_raw, perm_pad, member_pad, buf, blocks,
    sem, perm_sem, early_sem, send_sem,
):
    early_count = early_ref.shape[0]
    early_copy = pltpu.make_async_copy(early_ref, blocks.at[0:early_count], early_sem)
    early_copy.start()
    sources = (key_own, value_own, key_far, value_far)
    member = sort_heads(
        EARLY, perm_hbm, sources, blocks.at[early_count:], member_pad, perm_raw, perm_pad,
        buf, sem, perm_sem,
    )
    early_copy.wait()

    def start(d, count):
        for j in range(CAPACITY):
            asked = request_ref[d, j]

            @pl.when(asked >= 0)
            def _():
                pltpu.make_async_copy(
                    blocks.at[asked], send_ref.at[d * CAPACITY + j], send_sem
                ).start()

            count = count + (asked >= 0).astype(jnp.int32)
        return count

    started = lax.fori_loop(0, request_ref.shape[0], start, jnp.int32(0), unroll=8)
    member_ref[...] = (member + early_member[...].astype(jnp.float32)).astype(jnp.bfloat16)

    def finish(n, carry):
        pltpu.make_async_copy(blocks.at[0], send_ref.at[0], send_sem).wait()
        return carry

    lax.fori_loop(0, started, finish, 0)


def score(h, query, member, bias_ref, blocks):
    keys = []
    for j in range(PICKS):
        bias = jnp.broadcast_to(bias_ref[j, h : h + 1, :].astype(jnp.bfloat16), (BLOCK, 128))
        keys.append(jnp.concatenate([blocks[j, 0:BLOCK], bias], axis=1))
    return lax.dot_general(
        jnp.concatenate([query, member], axis=1),
        jnp.concatenate(keys, axis=0),
        (((1,), (1,)), ((), ())),
        preferred_element_type=jnp.float32,
    )


def mix(scores, blocks):
    top = jnp.max(scores, axis=1, keepdims=True)
    exponent = jnp.exp2((scores - top) * (math.log2(math.e) / math.sqrt(HEAD_DIM)))
    weights = exponent.astype(jnp.bfloat16)
    values = jnp.concatenate([blocks[j, BLOCK : 2 * BLOCK] for j in range(PICKS)], axis=0)
    ones = jnp.ones((PICKS * BLOCK, HEAD_DIM), jnp.bfloat16)
    mixed = jnp.dot(
        weights, jnp.concatenate([values, ones], axis=1), preferred_element_type=jnp.float32
    )
    return (mixed[:, :HEAD_DIM] / mixed[:, HEAD_DIM:]).astype(jnp.bfloat16)


def attend(first, count, query_ref, member, bias_ref, blocks_ref, far_ref, stage, send_own):
    half = stage.shape[0]
    blocks_of = lambda n: blocks_ref.at[n * PICKS : (n + 1) * PICKS]

    def score_of(n):
        cut = slice(n * HEAD_DIM, (n + 1) * HEAD_DIM)
        return score(first + n, query_ref[:, cut], member, bias_ref, blocks_of(n))

    following = score_of(0)
    for n in range(count):
        scores = following
        if n + 1 < count:
            following = score_of(n + 1)
        mixed = mix(scores, blocks_of(n))
        cut = slice(n * HEAD_DIM, (n + 1) * HEAD_DIM)
        stage[:, cut] = mixed[:half]
        far_ref[:, cut] = mixed[half:]
        send_own(n)


def own_copies(first, stage, out_ref, sem):
    pieces = sem.shape[0]
    step = stage.shape[1] // pieces
    base = lax.axis_index("head") * (out_ref.shape[1] // 2) + first * HEAD_DIM
    copies = [
        pltpu.make_async_copy(
            stage.at[:, g * step : (g + 1) * step],
            out_ref.at[:, pl.ds(pl.multiple_of(base + g * step, 128), step)],
            sem.at[g],
        )
        for g in range(pieces)
    ]

    def send_own(n):
        g, rest = divmod((n + 1) * HEAD_DIM, step)
        if rest == 0:
            copies[g - 1].start()

    return copies, send_own


def first_kernel(
    position_ref, member_ref, bias_ref, query_own, query_far, got_ref,
    out_ref, far_ref, later_blocks, later_query,
    blocks, query, stage, block_sem, query_sem, out_sem,
):
    heads = position_ref.shape[0]
    half = stage.shape[0]
    count = stage.shape[1] // HEAD_DIM
    width = heads * HEAD_DIM
    base = lax.axis_index("head") * width

    def query_copies(first, target, n):
        cut = pl.ds(pl.multiple_of(base + first * HEAD_DIM, 128), target.shape[1])
        return [
            pltpu.make_async_copy(
                source.at[:, cut], target.at[r * half : (r + 1) * half], query_sem.at[n, r]
            )
            for r, source in enumerate((query_own, query_far))
        ]

    def block_copy(h, j):
        target = blocks.at[h * PICKS + j] if h < count else later_blocks.at[(h - count) * PICKS + j]
        return pltpu.make_async_copy(
            got_ref.at[position_ref[h, j]], target, block_sem.at[0 if h < count else 1]
        )

    now, later = query_copies(0, query, 0), query_copies(count, later_query, 1)
    for copy in now:
        copy.start()
    for h in range(count):
        for j in range(PICKS):
            block_copy(h, j).start()
    for copy in later:
        copy.start()
    for h in range(count, heads):
        for j in range(PICKS):
            block_copy(h, j).start()
    for copy in now:
        copy.wait()
    pltpu.make_async_copy(blocks, blocks, block_sem.at[0]).wait()
    copies, send_own = own_copies(0, stage, out_ref, out_sem)
    attend(0, count, query, member_ref[...], bias_ref, blocks, far_ref, stage, send_own)
    for copy in later:
        copy.wait()
    pltpu.make_async_copy(later_blocks, later_blocks, block_sem.at[1]).wait()
    for copy in copies:
        copy.wait()


def last_kernel(
    member_ref, bias_ref, blocks, query, out_in, out_ref, far_ref, stage, out_sem
):
    del out_in
    count = stage.shape[1] // HEAD_DIM
    first = bias_ref.shape[1] - count
    copies, send_own = own_copies(first, stage, out_ref, out_sem)
    attend(first, count, query, member_ref[...], bias_ref, blocks, far_ref, stage, send_own)
    for copy in copies:
        copy.wait()


def place_kernel(first, out_in, far_ref, out_ref, sem):
    del out_in
    width = far_ref.shape[1]
    start = (1 - lax.axis_index("head")) * (out_ref.shape[1] // 2) + first * HEAD_DIM
    copy = pltpu.make_async_copy(
        far_ref, out_ref.at[:, pl.ds(pl.multiple_of(start, 128), width)], sem
    )
    copy.start()
    copy.wait()


def shards(queries, key_states, value_states, cluster_perm, block_mask):
    heads, rows = cluster_perm.shape
    half, columns = queries.shape
    width = heads * HEAD_DIM
    shard_blocks = rows // BLOCK
    seq_count = lax.axis_size("seq")
    pairs = heads * shard_blocks
    slots = seq_count * CAPACITY
    vmem = pl.BlockSpec(memory_space=pltpu.VMEM)
    smem = pl.BlockSpec(memory_space=pltpu.SMEM)
    hbm = pl.BlockSpec(memory_space=pltpu.HBM)
    limit = lambda mib: pltpu.CompilerParams(vmem_limit_bytes=mib << 20)
    held = lambda x: pltpu.with_memory_space_constraint(x, pltpu.VMEM)
    far = lambda x: pltpu.with_memory_space_constraint(x, pltpu.HBM)
    held_out = lambda shape, dtype: pltpu.VMEM(shape, dtype)
    hbm_out = lambda shape, dtype: pltpu.HBM(shape, dtype)
    dma = pltpu.SemaphoreType.DMA
    bf16 = jnp.bfloat16

    table = pl.pallas_call(
        request_kernel,
        out_shape=jax.ShapeDtypeStruct((seq_count, 128), jnp.int32),
        in_specs=[vmem],
        out_specs=vmem,
        name="request",
    )(block_mask)
    requested = lax.all_to_all(
        table.reshape(seq_count, 1, 128), "seq", split_axis=0, concat_axis=0, tiled=True
    ).reshape(seq_count, 128)

    def swap(x):
        return lax.ppermute(x, "head", [(0, 1), (1, 0)])

    key_far = swap(key_states)
    value_far = swap(value_states)

    query_far = swap(queries)
    position, bias = pl.pallas_call(
        plan_kernel,
        out_shape=[
            jax.ShapeDtypeStruct((heads, 128), jnp.int32),
            jax.ShapeDtypeStruct((PICKS, heads, 128), jnp.float32),
        ],
        in_specs=[vmem],
        out_specs=[vmem] * 2,
        name="plan",
    )(block_mask)
    key_args = (far(cluster_perm), far(key_states), key_far, far(value_states), value_far)

    def sort_scratch(count, step, kept):
        return [
            pltpu.VMEM((heads, rows), jnp.int32),
            pltpu.VMEM((128, rows), jnp.int32),
            pltpu.VMEM((128, rows), jnp.float32),
            pltpu.VMEM((count // step, 4, half, step * HEAD_DIM), bf16),
            pltpu.VMEM((kept, 2 * BLOCK, HEAD_DIM), bf16),
            dma((count // step, 4)),
            dma,
        ]

    early, early_member = pl.pallas_call(
        early_kernel,
        out_shape=[
            hbm_out((EARLY * shard_blocks, 2 * BLOCK, HEAD_DIM), bf16),
            jax.ShapeDtypeStruct((rows, 128), bf16),
        ],
        in_specs=[hbm] * 5,
        out_specs=[hbm, vmem],
        scratch_shapes=sort_scratch(EARLY, EARLY, EARLY * shard_blocks) + [dma],
        compiler_params=limit(24),
        name="early_sort",
    )(*key_args)
    send, member = pl.pallas_call(
        sort_kernel,
        out_shape=[
            hbm_out((slots, 2 * BLOCK, HEAD_DIM), bf16),
            held_out((rows, 128), bf16),
        ],
        in_specs=[smem] + [hbm] * 6 + [vmem],
        out_specs=[hbm, vmem],
        scratch_shapes=sort_scratch(heads - EARLY, SORT_STEP, pairs) + [dma, dma],
        compiler_params=limit(32),
        name="sort",
    )(requested, *key_args, far(early), early_member)
    send, member, position, bias, query_far = lax.optimization_barrier(
        (send, member, position, bias, query_far)
    )
    got = lax.all_to_all(send, "seq", split_axis=0, concat_axis=0, tiled=True)

    first, last = heads - LAST, LAST
    out, far_first, later_blocks, later_query = pl.pallas_call(
        first_kernel,
        out_shape=[
            hbm_out((half, columns), bf16),
            held_out((half, first * HEAD_DIM), bf16),
            held_out((last * PICKS, 2 * BLOCK, HEAD_DIM), bf16),
            held_out((rows, last * HEAD_DIM), bf16),
        ],
        in_specs=[smem, vmem, vmem, hbm, hbm, hbm],
        out_specs=[hbm, vmem, vmem, vmem],
        scratch_shapes=[
            pltpu.VMEM((first * PICKS, 2 * BLOCK, HEAD_DIM), bf16),
            pltpu.VMEM((rows, first * HEAD_DIM), bf16),
            pltpu.VMEM((half, first * HEAD_DIM), bf16),
            dma((2,)),
            dma((2, 2)),
            dma((2,)),
        ],
        compiler_params=limit(32),
        name="first_heads",
    )(position, held(member), bias, far(queries), query_far, far(got))
    far_first = swap(far_first)
    out, far_last = pl.pallas_call(
        last_kernel,
        out_shape=[
            hbm_out((half, columns), bf16),
            held_out((half, last * HEAD_DIM), bf16),
        ],
        in_specs=[vmem, vmem, vmem, vmem, hbm],
        out_specs=[hbm, vmem],
        scratch_shapes=[pltpu.VMEM((half, last * HEAD_DIM), bf16), dma((1,))],
        input_output_aliases={4: 0},
        compiler_params=limit(32),
        name="last_heads",
    )(held(member), bias, held(later_blocks), held(later_query), out)
    far_last = swap(far_last)

    def place(out, part, at):
        return pl.pallas_call(
            functools.partial(place_kernel, at),
            out_shape=hbm_out((half, columns), bf16),
            in_specs=[hbm, vmem],
            out_specs=hbm,
            scratch_shapes=[dma],
            input_output_aliases={0: 0},
            compiler_params=limit(8),
            name="place",
        )(out, held(part))

    return place(place(out, far_first, 0), far_last, first)


def solution(mesh):
    placed = (
        P(("seq", "head"), None),
        P(("seq", "head"), None),
        P(("seq", "head"), None),
        P("head", "seq"),
        P("head", "seq", None),
    )
    return jax.shard_map(
        shards, mesh=mesh, in_specs=placed, out_specs=P(("seq", "head"), None), check_vma=False
    )
```

time: 154 us -> 157 us (1.019)
  waiting for transfers between devices: 6.37 us -> 2.79 us
  Pallas kernels: 25.5 us -> 29 us
  blocking collectives: 106 us -> 109 us
    all_to_all x1, waiting for transfers between devices: 6.36 us -> 2.03 us  [shards(): lax.all_to_all(table.reshape(seq_count, 1, 128), 'seq', split_axis=0, con...]
    pallas_call x3 -> x5, Pallas kernels: 13.6 us -> 17.8 us  [the longest x1 8.93 us: shards(): pl.pallas_call(first_kernel, out_shape=[hbm_out((half, columns), bf16), h...]
    all_to_all x1, blocking collectives: 106 us -> 109 us  [shards(): got = lax.all_to_all(send, 'seq', split_axis=0, concat_axis=0, tiled=True)]
    ppermute x4 -> x5, starting transfers between devices: 5.12 us -> 4.58 us  [swap(): return lax.ppermute(x, 'head', [(0, 1), (1, 0)])]
  transfers between devices with their start and end apart: 5 -> 6, of which waited for: 1 -> 2; matrix products, arithmetic and copies ran while one was open for 0% -> 0% of each run, Pallas kernels for 11% -> 12%
where the time goes in v6:
time: 157 us
  blocking collectives  109 us (69%)
  Pallas kernels  29 us (18%)
  starting transfers between devices  15.8 us (10%)
  waiting for transfers between devices  2.79 us (2%)
    all_to_all x1, blocking collectives, shards(): got = lax.all_to_all(send, 'seq', split_axis=0, concat_axis=0, tiled=True)  109 us
    all_to_all x1, starting transfers between devices, shards(): lax.all_to_all(table.reshape(seq_count, 1, 128), 'seq', split_axis=0, con...  11.2 us
    pallas_call x1, Pallas kernels, shards(): pl.pallas_call(first_kernel, out_shape=[hbm_out((half, columns), bf16), h...  8.93 us
    pallas_call x1, Pallas kernels, shards(): pl.pallas_call(sort_kernel, out_shape=[hbm_out((slots, 2 * BLOCK, HEAD_DI...  7.48 us
    ppermute x5, starting transfers between devices, swap(): return lax.ppermute(x, 'head', [(0, 1), (1, 0)])  4.58 us
    pallas_call x1, Pallas kernels, shards(): pl.pallas_call(early_kernel, out_shape=[hbm_out((EARLY * shard_blocks, 2...  4.34 us
  transfers between devices with their start and end apart: 6, of which 2 were waited for; matrix products, arithmetic and copies ran while one was open for 0% of the time, Pallas kernels for 12%

profile of v6, /device:TPU:1, one launch (start us, length us, event | category | flops | bytes accessed | tf_op | source)
XLA Modules:
  0.0 157.1 jit_solution(4636123659359073020)
XLA Ops:
  0.0 1.4 collective-permute-start
  1.4 0.0 collective-permute-start.1
  1.4 0.5 collective-permute-start.2
  1.9 1.8 %request.1 = s32[64,128]{1,0:T(8,128)} custom-call(s32[20,4,256]{2,1,0:T(4,128)} %mask_ref.3), custom_call_target="tpu_custom_call" | custom-call | tf_op jit(solution)/shard_map/request/pallas_call | solution.py:365
  3.7 11.2 %all-to-all-start = ((s32[64,1,128]{2,1,0:T(1,128)}), s32[64,1,128]{2,1,0:T(1,128)S(1)}, u32[]{:S(2)}, u32[]{:S(2)}) async-start(s32[64,1,128]{2,1,0:T(1,128)} %bitcast.5), calls=%async_computation | async-start | bytes 65536 | tf_op jit(solution)/shard_map/all_to_all | solution.py:372
  14.9 2.0 %plan.1 = (s32[20,128]{1,0:T(8,128)}, f32[4,20,128]{2,1,0:T(8,128)}) custom-call(s32[20,4,256]{2,1,0:T(4,128)} %mask_ref.3), custom_call_target="tpu_custom_call" | custom-call | tf_op jit(solution)/shard_map/plan/pallas_call | solution.py:383
  16.9 0.0 collective-permute-done.key_far
  16.9 0.0 collective-permute-done.1.value_far
  16.9 4.3 %early_sort.1 = (bf16[32,256,128]{2,1,0:T(8,128)(2,1)}, bf16[512,128]{1,0:T(8,128)(2,1)S(1)}) custom-call(s32[20,512]{1,0:T(8,128)} %perm_hbm.3, bf16[256,5120]{1,0:T(8,128)(2,1)} %key_own.3, bf16[256,5120]{1,0:T(8,128)(2,1)S(1)} %collective-permute-done.key_far, bf16[256,5120]{1,0:T(8,128)(2,1)} %value_own.3, bf16[256,5120]{1,0:T(8,128)(2,1)} %collective-permute-done.1.value_far), custom_call_target="tpu_custom_call" | custom-call | tf_op jit(solution)/shard_map/early_sort/pallas_call | solution.py:406
  21.3 2.0 %all-to-all-done = s32[64,1,128]{2,1,0:T(1,128)S(1)} async-done(((s32[64,1,128]{2,1,0:T(1,128)}), s32[64,1,128]{2,1,0:T(1,128)S(1)}, u32[]{:S(2)}, u32[]{:S(2)}) %all-to-all-start) | async-done | bytes 32800 | tf_op jit(solution)/shard_map/all_to_all | solution.py:372
  23.3 7.5 %sort.1 = (bf16[128,256,128]{2,1,0:T(8,128)(2,1)}, bf16[512,128]{1,0:T(8,128)(2,1)S(1)}) custom-call(s32[64,128]{1,0:T(8,128)S(1)} %bitcast.4, s32[20,512]{1,0:T(8,128)} %perm_hbm.3, bf16[256,5120]{1,0:T(8,128)(2,1)} %key_own.3, bf16[256,5120]{1,0:T(8,128)(2,1)S(1)} %collective-permute-done.key_far, bf16[256,5120]{1,0:T(8,128)(2,1)} %value_own.3, ...), custom_call_target="tpu_custom_call" | custom-call | tf_op jit(solution)/shard_map/sort/pallas_call | solution.py:418
  30.8 0.0 collective-permute-done.2.query_far
  30.8 0.0 copy-start
  30.8 0.0 copy-start.1
  30.8 109.2 %all_to_all.10.got_ref = bf16[128,256,128]{2,1,0:T(8,128)(2,1)} all-to-all(bf16[128,256,128]{2,1,0:T(8,128)(2,1)} %get-tuple-element.32), channel_id=1, replica_groups=mesh['head'=2,'seq'=64] {'seq'}, dimensions={0} | all-to-all | bytes 16777216 | tf_op jit(solution)/shard_map/all_to_all | solution.py:433
  140.0 0.0 copy-done
  140.1 8.9 %first_heads.1 = (bf16[256,5120]{1,0:T(8,128)(2,1)}, bf16[256,1792]{1,0:T(8,128)(2,1)S(1)}, bf16[24,256,128]{2,1,0:T(8,128)(2,1)S(1)}, bf16[512,768]{1,0:T(8,128)(2,1)S(1)}) custom-call(s32[20,128]{1,0:T(8,128)S(1)} %copy-done.1, bf16[512,128]{1,0:T(8,128)(2,1)S(1)} %get-tuple-element.28.member_ref, f32[4,20,128]{2,1,0:T(8,128)S(1)} %copy-done, ...), custom_call_target="tpu_custom_call" | custom-call | tf_op jit(solution)/shard_map/first_heads/pallas_call | solution.py:436
  149.0 2.6 %collective-permute-start.3 = (bf16[256,1792]{1,0:T(8,128)(2,1)S(1)}, bf16[256,1792]{1,0:T(8,128)(2,1)S(1)}, u32[]{:S(2)}, u32[]{:S(2)}) collective-permute-start(bf16[256,1792]{1,0:T(8,128)(2,1)S(1)} %get-tuple-element.37), channel_id=1, source_target_pairs={{0,64},{64,0},{1,65},{65,1},{2,66},{66,2},{3,67},{67,3},{4,68},{68... | collective-permute-start | bytes 2752520 | tf_op jit(solution)/shard_map/ppermute | solution.py:377
  151.6 2.8 %last_heads.1 = (bf16[256,5120]{1,0:T(8,128)(2,1)}, bf16[256,768]{1,0:T(8,128)(2,1)S(1)}) custom-call(bf16[512,128]{1,0:T(8,128)(2,1)S(1)} %get-tuple-element.28.member_ref, f32[4,20,128]{2,1,0:T(8,128)S(1)} %copy-done, bf16[24,256,128]{2,1,0:T(8,128)(2,1)S(1)} %get-tuple-element.33.blocks, ...), custom_call_target="tpu_custom_call", output_to_operand_aliasing={{0}: (4, {})} | custom-call | tf_op jit(solution)/shard_map/last_heads/pallas_call | solution.py:458
  154.3 0.1 collective-permute-start.4
  154.4 0.0 collective-permute-done.3.far_ref
  154.4 0.9 place.2.out_in
  155.4 0.7 collective-permute-done.4.far_ref
  156.1 0.8 place.3
  (1 shorter events, 0.0 us)
Async XLA Ops:
  0.0 16.9 %collective-permute-start = (bf16[256,5120]{1,0:T(8,128)(2,1)}, bf16[256,5120]{1,0:T(8,128)(2,1)S(1)}, u32[]{:S(2)}, u32[]{:S(2)}) collective-permute-start(bf16[256,5120]{1,0:T(8,128)(2,1)} %key_own.3), channel_id=1, source_target_pairs={{0,64},{64,0},{1,65},{65,1},{2,66},{66,2},{3,67},{67,3},{4,68},{68... | collective-permute-start | bytes 7864328 | tf_op jit(solution)/shard_map/ppermute | solution.py:377
  1.4 15.5 %collective-permute-start.1 = (bf16[256,5120]{1,0:T(8,128)(2,1)}, bf16[256,5120]{1,0:T(8,128)(2,1)}, u32[]{:S(2)}, u32[]{:S(2)}) collective-permute-start(bf16[256,5120]{1,0:T(8,128)(2,1)} %value_own.3), channel_id=1, source_target_pairs={{0,64},{64,0},{1,65},{65,1},{2,66},{66,2},{3,67},{67,3},{4,68},{68... | collective-permute-start | bytes 7864328 | tf_op jit(solution)/shard_map/ppermute | solution.py:377
  1.4 29.4 %collective-permute-start.2 = (bf16[256,5120]{1,0:T(8,128)(2,1)}, bf16[256,5120]{1,0:T(8,128)(2,1)}, u32[]{:S(2)}, u32[]{:S(2)}) collective-permute-start(bf16[256,5120]{1,0:T(8,128)(2,1)} %query_own.1), channel_id=1, source_target_pairs={{0,64},{64,0},{1,65},{65,1},{2,66},{66,2},{3,67},{67,3},{4,68},{68... | collective-permute-start | bytes 7864328 | tf_op jit(solution)/shard_map/ppermute | solution.py:377
  3.7 19.6 %all-to-all-start = ((s32[64,1,128]{2,1,0:T(1,128)}), s32[64,1,128]{2,1,0:T(1,128)S(1)}, u32[]{:S(2)}, u32[]{:S(2)}) async-start(s32[64,1,128]{2,1,0:T(1,128)} %bitcast.5), calls=%async_computation | async-start | bytes 65536 | tf_op jit(solution)/shard_map/all_to_all | solution.py:372
  30.8 109.3 %copy-start = (f32[4,20,128]{2,1,0:T(8,128)S(1)}, f32[4,20,128]{2,1,0:T(8,128)}, u32[]{:S(2)}) copy-start(f32[4,20,128]{2,1,0:T(8,128)} %get-tuple-element.29.bias_ref) | copy-start | bytes 122884
  30.8 109.2 %copy-start.1 = (s32[20,128]{1,0:T(8,128)S(1)}, s32[20,128]{1,0:T(8,128)}, u32[]{:S(2)}) copy-start(s32[20,128]{1,0:T(8,128)} %get-tuple-element.30.position_ref) | copy-start | bytes 30724
  149.0 5.5 %collective-permute-start.3 = (bf16[256,1792]{1,0:T(8,128)(2,1)S(1)}, bf16[256,1792]{1,0:T(8,128)(2,1)S(1)}, u32[]{:S(2)}, u32[]{:S(2)}) collective-permute-start(bf16[256,1792]{1,0:T(8,128)(2,1)S(1)} %get-tuple-element.37), channel_id=1, source_target_pairs={{0,64},{64,0},{1,65},{65,1},{2,66},{66,2},{3,67},{67,3},{4,68},{68... | collective-permute-start | bytes 2752520 | tf_op jit(solution)/shard_map/ppermute | solution.py:377
  154.3 1.8 %collective-permute-start.4 = (bf16[256,768]{1,0:T(8,128)(2,1)S(1)}, bf16[256,768]{1,0:T(8,128)(2,1)S(1)}, u32[]{:S(2)}, u32[]{:S(2)}) collective-permute-start(bf16[256,768]{1,0:T(8,128)(2,1)S(1)} %get-tuple-element.38), channel_id=1, source_target_pairs={{0,64},{64,0},{1,65},{65,1},{2,66},{66,2},{3,67},{67,3},{4,68},{68... | collective-permute-start | bytes 1179656 | tf_op jit(solution)/shard_map/ppermute | solution.py:377

commit v7 on v6

--- a/solution.py
+++ b/solution.py
@@ -1,4 +1,3 @@
-import functools
 import math
 
 import jax
@@ -36,13 +35,23 @@
 
 
 def request_kernel(mask_ref, table_ref):
-    heads, shard_blocks, _ = mask_ref.shape
-    needed = jnp.max(mask_ref[...], axis=1)
-    pair, mine, low_col = slot_lows(needed, shard_blocks)
-    high = jnp.max(jnp.where(needed > 0, pair, -1), axis=0, keepdims=True)
+    heads, shard_blocks, blocks = mask_ref.shape
+    shards = blocks >> shift_of(shard_blocks)
+    count = heads * shard_blocks
+    mask = mask_ref[...]
+    head = lax.broadcasted_iota(jnp.int32, mask.shape, 0)
+    key_block = lax.broadcasted_iota(jnp.int32, mask.shape, 2)
+    pair = head * shard_blocks + jnp.bitwise_and(key_block, shard_blocks - 1)
+    low = jnp.min(jnp.where(mask > 0, pair, count), axis=0)
+    high = jnp.max(jnp.where(mask > 0, pair, -1), axis=0)
+    low = jnp.min(low, axis=0, keepdims=True)
+    high = jnp.max(high, axis=0, keepdims=True)
+    owner = lax.broadcasted_iota(jnp.int32, (shards, blocks), 1) >> shift_of(shard_blocks)
+    mine = owner == lax.broadcasted_iota(jnp.int32, (shards, blocks), 0)
+    low_col = jnp.min(jnp.where(mine, low, count), axis=1, keepdims=True)
     high_col = jnp.max(jnp.where(mine, high, -1), axis=1, keepdims=True)
     high_col = jnp.where(high_col == low_col, -1, high_col)
-    low_col = jnp.where(low_col == heads * shard_blocks, -1, low_col)
+    low_col = jnp.where(low_col == count, -1, low_col)
     lane = lax.broadcasted_iota(jnp.int32, table_ref.shape, 1)
     table_ref[...] = jnp.where(lane == 0, low_col, high_col)
 
@@ -83,11 +92,9 @@
     position_ref[...] = position
 
 
-def sort_heads(
-    first, perm_hbm, sources, out_ref, member_pad, perm_raw, perm_pad, buf, sem, perm_sem
-):
-    heads, rows = perm_hbm.shape
+def sort_heads(first, heads, sources, column_of, out_ref, member_pad, buf, sem):
     steps, _, half, step_width = buf.shape
+    rows = 2 * half
     step_heads = step_width // HEAD_DIM
     count = steps * step_heads
     shard_blocks = rows // BLOCK
@@ -100,17 +107,13 @@
             for n, ref in enumerate(sources)
         ]
 
-    perm_copy = pltpu.make_async_copy(perm_hbm, perm_raw, perm_sem)
-    perm_copy.start()
     for g in range(steps):
         for copy in copies(g):
             copy.start()
     member_pad[...] = jnp.zeros(member_pad.shape, jnp.float32)
     token = lax.broadcasted_iota(jnp.int32, (rows, half), 1)
     token = token.astype(jnp.float32).astype(jnp.bfloat16)
-    perm_copy.wait()
-    perm_pad[0:heads, :] = perm_raw[...]
-    column = jnp.transpose(local_tokens(perm_pad[...], rows))
+    column = column_of()
     own_column = jnp.where(column < half, column, -1).astype(jnp.float32)
     far_column = jnp.where(column < half, -1, column - half).astype(jnp.float32)
 
@@ -155,12 +158,22 @@
 
 def early_kernel(
     perm_hbm, key_own, key_far, value_own, value_far,
-    early_ref, member_ref, perm_raw, perm_pad, member_pad, buf, blocks, sem, perm_sem, out_sem,
+    early_ref, member_ref, column_ref, perm_raw, perm_pad, member_pad, buf, blocks,
+    sem, perm_sem, out_sem,
 ):
+    heads, rows = perm_hbm.shape
+    perm_copy = pltpu.make_async_copy(perm_hbm, perm_raw, perm_sem)
+    perm_copy.start()
+
+    def column_of():
+        perm_copy.wait()
+        perm_pad[0:heads, :] = perm_raw[...]
+        column = jnp.transpose(local_tokens(perm_pad[...], rows))
+        column_ref[...] = column
+        return column
+
     sources = (key_own, value_own, key_far, value_far)
-    member = sort_heads(
-        0, perm_hbm, sources, blocks, member_pad, perm_raw, perm_pad, buf, sem, perm_sem
-    )
+    member = sort_heads(0, heads, sources, column_of, blocks, member_pad, buf, sem)
     copy = pltpu.make_async_copy(blocks, early_ref, out_sem)
     copy.start()
     member_ref[...] = member.astype(jnp.bfloat16)
@@ -168,17 +181,20 @@
 
 
 def sort_kernel(
-    request_ref, perm_hbm, key_own, key_far, value_own, value_far, early_ref, early_member,
-    send_ref, member_ref, perm_raw, perm_pad, member_pad, buf, blocks,
-    sem, perm_sem, early_sem, send_sem,
+    request_ref, column_ref, key_own, key_far, value_own, value_far, early_ref, early_member,
+    send_ref, member_ref, member_pad, buf, blocks, sem, early_sem, send_sem,
 ):
     early_count = early_ref.shape[0]
+    heads = blocks.shape[0] * BLOCK // column_ref.shape[0]
+    sources = (key_own, value_own, key_far, value_far)
     early_copy = pltpu.make_async_copy(early_ref, blocks.at[0:early_count], early_sem)
-    early_copy.start()
-    sources = (key_own, value_own, key_far, value_far)
+
+    def column_of():
+        early_copy.start()
+        return column_ref[...]
+
     member = sort_heads(
-        EARLY, perm_hbm, sources, blocks.at[early_count:], member_pad, perm_raw, perm_pad,
-        buf, sem, perm_sem,
+        EARLY, heads, sources, column_of, blocks.at[early_count:], member_pad, buf, sem
     )
     early_copy.wait()
 
@@ -230,8 +246,9 @@
     return (mixed[:, :HEAD_DIM] / mixed[:, HEAD_DIM:]).astype(jnp.bfloat16)
 
 
-def attend(first, count, query_ref, member, bias_ref, blocks_ref, far_ref, stage, send_own):
-    half = stage.shape[0]
+def attend(first, query_ref, member, bias_ref, blocks_ref, own_ref, far_ref):
+    half, width = own_ref.shape
+    count = width // HEAD_DIM
     blocks_of = lambda n: blocks_ref.at[n * PICKS : (n + 1) * PICKS]
 
     def score_of(n):
@@ -245,40 +262,17 @@
             following = score_of(n + 1)
         mixed = mix(scores, blocks_of(n))
         cut = slice(n * HEAD_DIM, (n + 1) * HEAD_DIM)
-        stage[:, cut] = mixed[:half]
+        own_ref[:, cut] = mixed[:half]
         far_ref[:, cut] = mixed[half:]
-        send_own(n)
-
-
-def own_copies(first, stage, out_ref, sem):
-    pieces = sem.shape[0]
-    step = stage.shape[1] // pieces
-    base = lax.axis_index("head") * (out_ref.shape[1] // 2) + first * HEAD_DIM
-    copies = [
-        pltpu.make_async_copy(
-            stage.at[:, g * step : (g + 1) * step],
-            out_ref.at[:, pl.ds(pl.multiple_of(base + g * step, 128), step)],
-            sem.at[g],
-        )
-        for g in range(pieces)
-    ]
-
-    def send_own(n):
-        g, rest = divmod((n + 1) * HEAD_DIM, step)
-        if rest == 0:
-            copies[g - 1].start()
-
-    return copies, send_own
 
 
 def first_kernel(
     position_ref, member_ref, bias_ref, query_own, query_far, got_ref,
-    out_ref, far_ref, later_blocks, later_query,
-    blocks, query, stage, block_sem, query_sem, out_sem,
+    own_ref, far_ref, later_blocks, later_query, blocks, query, block_sem, query_sem,
 ):
     heads = position_ref.shape[0]
-    half = stage.shape[0]
-    count = stage.shape[1] // HEAD_DIM
+    half = own_ref.shape[0]
+    count = own_ref.shape[1] // HEAD_DIM
     width = heads * HEAD_DIM
     base = lax.axis_index("head") * width
 
@@ -311,34 +305,42 @@
     for copy in now:
         copy.wait()
     pltpu.make_async_copy(blocks, blocks, block_sem.at[0]).wait()
-    copies, send_own = own_copies(0, stage, out_ref, out_sem)
-    attend(0, count, query, member_ref[...], bias_ref, blocks, far_ref, stage, send_own)
+    attend(0, query, member_ref[...], bias_ref, blocks, own_ref, far_ref)
     for copy in later:
         copy.wait()
     pltpu.make_async_copy(later_blocks, later_blocks, block_sem.at[1]).wait()
+
+
+def last_kernel(member_ref, bias_ref, blocks, query, own_ref, far_ref):
+    first = bias_ref.shape[1] - own_ref.shape[1] // HEAD_DIM
+    attend(first, query, member_ref[...], bias_ref, blocks, own_ref, far_ref)
+
+
+def columns_of(out_ref, side, part_ref, first):
+    start = side * (out_ref.shape[1] // 2) + first * HEAD_DIM
+    return out_ref.at[:, pl.ds(pl.multiple_of(start, 128), part_ref.shape[1])]
+
+
+def place_kernel(own_first, own_last, far_first, out_ref, sem):
+    core = lax.axis_index("head")
+    first = own_first.shape[1] // HEAD_DIM
+    copies = [
+        pltpu.make_async_copy(part, columns_of(out_ref, side, part, at), sem.at[n])
+        for n, (part, side, at) in enumerate(
+            ((own_first, core, 0), (own_last, core, first), (far_first, 1 - core, 0))
+        )
+    ]
+    for copy in copies:
+        copy.start()
     for copy in copies:
         copy.wait()
 
 
-def last_kernel(
-    member_ref, bias_ref, blocks, query, out_in, out_ref, far_ref, stage, out_sem
-):
+def place_last_kernel(out_in, far_last, out_ref, sem):
     del out_in
-    count = stage.shape[1] // HEAD_DIM
-    first = bias_ref.shape[1] - count
-    copies, send_own = own_copies(first, stage, out_ref, out_sem)
-    attend(first, count, query, member_ref[...], bias_ref, blocks, far_ref, stage, send_own)
-    for copy in copies:
-        copy.wait()
-
-
-def place_kernel(first, out_in, far_ref, out_ref, sem):
-    del out_in
-    width = far_ref.shape[1]
-    start = (1 - lax.axis_index("head")) * (out_ref.shape[1] // 2) + first * HEAD_DIM
-    copy = pltpu.make_async_copy(
-        far_ref, out_ref.at[:, pl.ds(pl.multiple_of(start, 128), width)], sem
-    )
+    first = (out_ref.shape[1] // 2 - far_last.shape[1]) // HEAD_DIM
+    side = 1 - lax.axis_index("head")
+    copy = pltpu.make_async_copy(far_last, columns_of(out_ref, side, far_last, first), sem)
     copy.start()
     copy.wait()
 
@@ -390,99 +392,99 @@
         out_specs=[vmem] * 2,
         name="plan",
     )(block_mask)
-    key_args = (far(cluster_perm), far(key_states), key_far, far(value_states), value_far)
+    key_args = (far(key_states), key_far, far(value_states), value_far)
 
     def sort_scratch(count, step, kept):
         return [
-            pltpu.VMEM((heads, rows), jnp.int32),
-            pltpu.VMEM((128, rows), jnp.int32),
             pltpu.VMEM((128, rows), jnp.float32),
             pltpu.VMEM((count // step, 4, half, step * HEAD_DIM), bf16),
             pltpu.VMEM((kept, 2 * BLOCK, HEAD_DIM), bf16),
             dma((count // step, 4)),
             dma,
+            dma,
         ]
 
-    early, early_member = pl.pallas_call(
+    early, early_member, column = pl.pallas_call(
         early_kernel,
         out_shape=[
             hbm_out((EARLY * shard_blocks, 2 * BLOCK, HEAD_DIM), bf16),
             jax.ShapeDtypeStruct((rows, 128), bf16),
+            held_out((rows, 128), jnp.int32),
         ],
         in_specs=[hbm] * 5,
-        out_specs=[hbm, vmem],
-        scratch_shapes=sort_scratch(EARLY, EARLY, EARLY * shard_blocks) + [dma],
+        out_specs=[hbm, vmem, vmem],
+        scratch_shapes=[pltpu.VMEM((heads, rows), jnp.int32), pltpu.VMEM((128, rows), jnp.int32)]
+        + sort_scratch(EARLY, EARLY, EARLY * shard_blocks),
         compiler_params=limit(24),
         name="early_sort",
-    )(*key_args)
+    )(far(cluster_perm), *key_args)
     send, member = pl.pallas_call(
         sort_kernel,
         out_shape=[
             hbm_out((slots, 2 * BLOCK, HEAD_DIM), bf16),
             held_out((rows, 128), bf16),
         ],
-        in_specs=[smem] + [hbm] * 6 + [vmem],
+        in_specs=[smem, vmem] + [hbm] * 5 + [vmem],
         out_specs=[hbm, vmem],
-        scratch_shapes=sort_scratch(heads - EARLY, SORT_STEP, pairs) + [dma, dma],
+        scratch_shapes=sort_scratch(heads - EARLY, SORT_STEP, pairs),
         compiler_params=limit(32),
         name="sort",
-    )(requested, *key_args, far(early), early_member)
+    )(requested, held(column), *key_args, far(early), early_member)
     send, member, position, bias, query_far = lax.optimization_barrier(
         (send, member, position, bias, query_far)
     )
     got = lax.all_to_all(send, "seq", split_axis=0, concat_axis=0, tiled=True)
 
     first, last = heads - LAST, LAST
-    out, far_first, later_blocks, later_query = pl.pallas_call(
+    part = lambda count: held_out((half, count * HEAD_DIM), bf16)
+    own_first, far_first, later_blocks, later_query = pl.pallas_call(
         first_kernel,
         out_shape=[
-            hbm_out((half, columns), bf16),
-            held_out((half, first * HEAD_DIM), bf16),
+            part(first),
+            part(first),
             held_out((last * PICKS, 2 * BLOCK, HEAD_DIM), bf16),
             held_out((rows, last * HEAD_DIM), bf16),
         ],
         in_specs=[smem, vmem, vmem, hbm, hbm, hbm],
-        out_specs=[hbm, vmem, vmem, vmem],
+        out_specs=[vmem] * 4,
         scratch_shapes=[
             pltpu.VMEM((first * PICKS, 2 * BLOCK, HEAD_DIM), bf16),
             pltpu.VMEM((rows, first * HEAD_DIM), bf16),
-            pltpu.VMEM((half, first * HEAD_DIM), bf16),
             dma((2,)),
             dma((2, 2)),
-            dma((2,)),
         ],
-        compiler_params=limit(32),
+        compiler_params=limit(24),
         name="first_heads",
     )(position, held(member), bias, far(queries), query_far, far(got))
     far_first = swap(far_first)
-    out, far_last = pl.pallas_call(
+    own_last, far_last = pl.pallas_call(
         last_kernel,
-        out_shape=[
-            hbm_out((half, columns), bf16),
-            held_out((half, last * HEAD_DIM), bf16),
-        ],
-        in_specs=[vmem, vmem, vmem, vmem, hbm],
-        out_specs=[hbm, vmem],
-        scratch_shapes=[pltpu.VMEM((half, last * HEAD_DIM), bf16), dma((1,))],
-        input_output_aliases={4: 0},
-        compiler_params=limit(32),
+        out_shape=[part(last), part(last)],
+        in_specs=[vmem] * 4,
+        out_specs=[vmem] * 2,
+        compiler_params=limit(24),
         name="last_heads",
-    )(held(member), bias, held(later_blocks), held(later_query), out)
+    )(held(member), bias, held(later_blocks), held(later_query))
     far_last = swap(far_last)
-
-    def place(out, part, at):
-        return pl.pallas_call(
-            functools.partial(place_kernel, at),
-            out_shape=hbm_out((half, columns), bf16),
-            in_specs=[hbm, vmem],
-            out_specs=hbm,
-            scratch_shapes=[dma],
-            input_output_aliases={0: 0},
-            compiler_params=limit(8),
-            name="place",
-        )(out, held(part))
-
-    return place(place(out, far_first, 0), far_last, first)
+    out = pl.pallas_call(
+        place_kernel,
+        out_shape=hbm_out((half, columns), bf16),
+        in_specs=[vmem] * 3,
+        out_specs=hbm,
+        scratch_shapes=[dma((3,))],
+        compiler_params=limit(8),
+        name="place",
+    )(held(own_first), held(own_last), held(far_first))
+    return pl.pallas_call(
+        place_last_kernel,
+        out_shape=hbm_out((half, columns), bf16),
+        in_specs=[hbm, vmem],
+        out_specs=hbm,
+        scratch_shapes=[dma],
+        input_output_aliases={0: 0},
+        compiler_params=limit(8),
+        name="place_last",
+    )(out, held(far_last))
 
 
 def solution(mesh):

time: 157 us -> 154 us (0.981)
  no operation moved by 1% of the time
where the time goes in v7:
time: 154 us; the launch traced here: 155 us
  blocking collectives  109 us (71%)
  Pallas kernels  27.6 us (18%)
  starting transfers between devices  15.9 us (10%)
  waiting for transfers between devices  2.35 us (2%)
    all_to_all x1, blocking collectives, shards(): got = lax.all_to_all(send, 'seq', split_axis=0, concat_axis=0, tiled=True)  109 us
    all_to_all x1, starting transfers between devices, shards(): lax.all_to_all(table.reshape(seq_count, 1, 128), 'seq', split_axis=0, con...  11.2 us
    pallas_call x1, Pallas kernels, shards(): pl.pallas_call(first_kernel, out_shape=[part(first), part(first), held_ou...  8.22 us
    pallas_call x1, Pallas kernels, shards(): pl.pallas_call(sort_kernel, out_shape=[hbm_out((slots, 2 * BLOCK, HEAD_DI...  7.12 us
    ppermute x5, starting transfers between devices, swap(): return lax.ppermute(x, 'head', [(0, 1), (1, 0)])  4.68 us
    pallas_call x1, Pallas kernels, shards(): pl.pallas_call(early_kernel, out_shape=[hbm_out((EARLY * shard_blocks, 2...  4.33 us
  transfers between devices with their start and end apart: 6, of which 2 were waited for; matrix products, arithmetic and copies ran while one was open for 0% of the time, Pallas kernels for 12%

profile of v7, /device:TPU:1, one launch (start us, length us, event | category | flops | bytes accessed | tf_op | source)
XLA Modules:
  0.0 154.8 jit_solution(14695083038840725715)
XLA Ops:
  0.0 1.4 collective-permute-start
  1.4 0.0 collective-permute-start.1
  1.4 0.5 collective-permute-start.2
  1.9 1.7 %request.1 = s32[64,128]{1,0:T(8,128)} custom-call(s32[20,4,256]{2,1,0:T(4,128)} %mask_ref.3), custom_call_target="tpu_custom_call" | custom-call | tf_op jit(solution)/shard_map/request/pallas_call | solution.py:367
  3.6 11.2 %all-to-all-start = ((s32[64,1,128]{2,1,0:T(1,128)}), s32[64,1,128]{2,1,0:T(1,128)S(1)}, u32[]{:S(2)}, u32[]{:S(2)}) async-start(s32[64,1,128]{2,1,0:T(1,128)} %bitcast.5), calls=%async_computation | async-start | bytes 65536 | tf_op jit(solution)/shard_map/all_to_all | solution.py:374
  14.9 2.0 %plan.1 = (s32[20,128]{1,0:T(8,128)}, f32[4,20,128]{2,1,0:T(8,128)}) custom-call(s32[20,4,256]{2,1,0:T(4,128)} %mask_ref.3), custom_call_target="tpu_custom_call" | custom-call | tf_op jit(solution)/shard_map/plan/pallas_call | solution.py:385
  16.9 0.0 collective-permute-done.key_far
  16.9 0.0 collective-permute-done.1.value_far
  16.9 4.3 %early_sort.1 = (bf16[32,256,128]{2,1,0:T(8,128)(2,1)}, bf16[512,128]{1,0:T(8,128)(2,1)S(1)}, s32[512,128]{1,0:T(8,128)S(1)}) custom-call(s32[20,512]{1,0:T(8,128)} %perm_hbm.1, bf16[256,5120]{1,0:T(8,128)(2,1)} %key_own.3, bf16[256,5120]{1,0:T(8,128)(2,1)S(1)} %collective-permute-done.key_far, bf16[256,5120]{1,0:T(8,128)(2,1)} %value_own.3, ...), custom_call_target="tpu_custom_call" | custom-call | tf_op jit(solution)/shard_map/early_sort/pallas_call | solution.py:407
  21.2 2.0 %all-to-all-done = s32[64,1,128]{2,1,0:T(1,128)S(1)} async-done(((s32[64,1,128]{2,1,0:T(1,128)}), s32[64,1,128]{2,1,0:T(1,128)S(1)}, u32[]{:S(2)}, u32[]{:S(2)}) %all-to-all-start) | async-done | bytes 32800 | tf_op jit(solution)/shard_map/all_to_all | solution.py:374
  23.2 7.1 %sort.1 = (bf16[128,256,128]{2,1,0:T(8,128)(2,1)}, bf16[512,128]{1,0:T(8,128)(2,1)S(1)}) custom-call(s32[64,128]{1,0:T(8,128)S(1)} %bitcast.4, s32[512,128]{1,0:T(8,128)S(1)} %get-tuple-element.23.column_ref, bf16[256,5120]{1,0:T(8,128)(2,1)} %key_own.3, bf16[256,5120]{1,0:T(8,128)(2,1)S(1)} %collective-permute-done.key_far, bf16[256,5120]{1,0:T(8,128)(2,1)} %value_own.3, ...), custom_call_target="tpu_custom_call" | custom-call | tf_op jit(solution)/shard_map/sort/pallas_call | solution.py:421
  30.4 0.0 collective-permute-done.2.query_far
  30.4 0.0 copy-start
  30.4 0.0 copy-start.1
  30.4 108.7 %all_to_all.10.got_ref = bf16[128,256,128]{2,1,0:T(8,128)(2,1)} all-to-all(bf16[128,256,128]{2,1,0:T(8,128)(2,1)} %get-tuple-element.34), channel_id=1, replica_groups=mesh['head'=2,'seq'=64] {'seq'}, dimensions={0} | all-to-all | bytes 16777216 | tf_op jit(solution)/shard_map/all_to_all | solution.py:436
  139.1 0.0 copy-done
  139.1 8.2 %first_heads.1 = (bf16[256,1792]{1,0:T(8,128)(2,1)S(1)}, bf16[256,1792]{1,0:T(8,128)(2,1)S(1)}, bf16[24,256,128]{2,1,0:T(8,128)(2,1)S(1)}, bf16[512,768]{1,0:T(8,128)(2,1)S(1)}) custom-call(s32[20,128]{1,0:T(8,128)S(1)} %copy-done.1, bf16[512,128]{1,0:T(8,128)(2,1)S(1)} %get-tuple-element.31.member_ref, f32[4,20,128]{2,1,0:T(8,128)S(1)} %copy-done, ...), custom_call_target="tpu_custom_call" | custom-call | tf_op jit(solution)/shard_map/first_heads/pallas_call | solution.py:440
  147.4 2.6 %collective-permute-start.3 = (bf16[256,1792]{1,0:T(8,128)(2,1)S(1)}, bf16[256,1792]{1,0:T(8,128)(2,1)S(1)}, u32[]{:S(2)}, u32[]{:S(2)}) collective-permute-start(bf16[256,1792]{1,0:T(8,128)(2,1)S(1)} %get-tuple-element.39), channel_id=1, source_target_pairs={{0,64},{64,0},{1,65},{65,1},{2,66},{66,2},{3,67},{67,3},{4,68},{68... | collective-permute-start | bytes 2752520 | tf_op jit(solution)/shard_map/ppermute | solution.py:379
  150.0 2.1 %last_heads.1 = (bf16[256,768]{1,0:T(8,128)(2,1)S(1)}, bf16[256,768]{1,0:T(8,128)(2,1)S(1)}) custom-call(bf16[512,128]{1,0:T(8,128)(2,1)S(1)} %get-tuple-element.31.member_ref, f32[4,20,128]{2,1,0:T(8,128)S(1)} %copy-done, bf16[24,256,128]{2,1,0:T(8,128)(2,1)S(1)} %get-tuple-element.36.blocks, bf16[512,768]{1,0:T(8,128)(2,1)S(1)} %get-tuple-element.37.query), custom_call_target="tpu_custom_call" | custom-call | tf_op jit(solution)/shard_map/last_heads/pallas_call | solution.py:460
  152.1 0.1 collective-permute-start.4
  152.2 0.0 collective-permute-done.3.far_first
  152.2 1.4 place.1.out_in
  153.6 0.3 collective-permute-done.4.far_last
  153.9 0.8 place_last.1
  (1 shorter events, 0.0 us)
Async XLA Ops:
  0.0 16.9 %collective-permute-start = (bf16[256,5120]{1,0:T(8,128)(2,1)}, bf16[256,5120]{1,0:T(8,128)(2,1)S(1)}, u32[]{:S(2)}, u32[]{:S(2)}) collective-permute-start(bf16[256,5120]{1,0:T(8,128)(2,1)} %key_own.3), channel_id=1, source_target_pairs={{0,64},{64,0},{1,65},{65,1},{2,66},{66,2},{3,67},{67,3},{4,68},{68... | collective-permute-start | bytes 7864328 | tf_op jit(solution)/shard_map/ppermute | solution.py:379
  1.4 15.4 %collective-permute-start.1 = (bf16[256,5120]{1,0:T(8,128)(2,1)}, bf16[256,5120]{1,0:T(8,128)(2,1)}, u32[]{:S(2)}, u32[]{:S(2)}) collective-permute-start(bf16[256,5120]{1,0:T(8,128)(2,1)} %value_own.3), channel_id=1, source_target_pairs={{0,64},{64,0},{1,65},{65,1},{2,66},{66,2},{3,67},{67,3},{4,68},{68... | collective-permute-start | bytes 7864328 | tf_op jit(solution)/shard_map/ppermute | solution.py:379
  1.4 29.0 %collective-permute-start.2 = (bf16[256,5120]{1,0:T(8,128)(2,1)}, bf16[256,5120]{1,0:T(8,128)(2,1)}, u32[]{:S(2)}, u32[]{:S(2)}) collective-permute-start(bf16[256,5120]{1,0:T(8,128)(2,1)} %query_own.1), channel_id=1, source_target_pairs={{0,64},{64,0},{1,65},{65,1},{2,66},{66,2},{3,67},{67,3},{4,68},{68... | collective-permute-start | bytes 7864328 | tf_op jit(solution)/shard_map/ppermute | solution.py:379
  3.6 19.6 %all-to-all-start = ((s32[64,1,128]{2,1,0:T(1,128)}), s32[64,1,128]{2,1,0:T(1,128)S(1)}, u32[]{:S(2)}, u32[]{:S(2)}) async-start(s32[64,1,128]{2,1,0:T(1,128)} %bitcast.5), calls=%async_computation | async-start | bytes 65536 | tf_op jit(solution)/shard_map/all_to_all | solution.py:374
  30.4 108.7 %copy-start = (f32[4,20,128]{2,1,0:T(8,128)S(1)}, f32[4,20,128]{2,1,0:T(8,128)}, u32[]{:S(2)}) copy-start(f32[4,20,128]{2,1,0:T(8,128)} %get-tuple-element.32.bias_ref) | copy-start | bytes 122884
  30.4 108.7 %copy-start.1 = (s32[20,128]{1,0:T(8,128)S(1)}, s32[20,128]{1,0:T(8,128)}, u32[]{:S(2)}) copy-start(s32[20,128]{1,0:T(8,128)} %get-tuple-element.30.position_ref) | copy-start | bytes 30724
  147.4 4.8 %collective-permute-start.3 = (bf16[256,1792]{1,0:T(8,128)(2,1)S(1)}, bf16[256,1792]{1,0:T(8,128)(2,1)S(1)}, u32[]{:S(2)}, u32[]{:S(2)}) collective-permute-start(bf16[256,1792]{1,0:T(8,128)(2,1)S(1)} %get-tuple-element.39), channel_id=1, source_target_pairs={{0,64},{64,0},{1,65},{65,1},{2,66},{66,2},{3,67},{67,3},{4,68},{68... | collective-permute-start | bytes 2752520 | tf_op jit(solution)/shard_map/ppermute | solution.py:379
  152.1 1.8 %collective-permute-start.4 = (bf16[256,768]{1,0:T(8,128)(2,1)S(1)}, bf16[256,768]{1,0:T(8,128)(2,1)S(1)}, u32[]{:S(2)}, u32[]{:S(2)}) collective-permute-start(bf16[256,768]{1,0:T(8,128)(2,1)S(1)} %get-tuple-element.40), channel_id=1, source_target_pairs={{0,64},{64,0},{1,65},{65,1},{2,66},{66,2},{3,67},{67,3},{4,68},{68... | collective-permute-start | bytes 1179656 | tf_op jit(solution)/shard_map/ppermute | solution.py:379

commit v8 on v7

--- a/solution.py
+++ b/solution.py
@@ -11,8 +11,8 @@
 BLOCK = 128
 CAPACITY = 2
 PICKS = 4
-EARLY = 8
-SORT_STEP = 6
+EARLY = 10
+SORT_STEP = 5
 LAST = 6
 MASKED = -1e30
 
@@ -60,7 +60,7 @@
     return jnp.bitwise_and(perm + lax.axis_index("head") * (rows // 2), rows - 1)
 
 
-def plan_kernel(mask_ref, position_ref, bias_ref):
+def plan(mask_ref, position_ref, bias_ref):
     heads, shard_blocks, blocks = mask_ref.shape
     mask = mask_ref[...]
     needed = jnp.max(mask, axis=1)
@@ -157,8 +157,8 @@
 
 
 def early_kernel(
-    perm_hbm, key_own, key_far, value_own, value_far,
-    early_ref, member_ref, column_ref, perm_raw, perm_pad, member_pad, buf, blocks,
+    mask_ref, perm_hbm, key_own, key_far, value_own, value_far,
+    early_ref, member_ref, column_ref, position_ref, bias_ref, perm_raw, perm_pad, member_pad, buf, blocks,
     sem, perm_sem, out_sem,
 ):
     heads, rows = perm_hbm.shape
@@ -166,6 +166,7 @@
     perm_copy.start()
 
     def column_of():
+        plan(mask_ref, position_ref, bias_ref)
         perm_copy.wait()
         perm_pad[0:heads, :] = perm_raw[...]
         column = jnp.transpose(local_tokens(perm_pad[...], rows))
@@ -382,16 +383,6 @@
     value_far = swap(value_states)
 
     query_far = swap(queries)
-    position, bias = pl.pallas_call(
-        plan_kernel,
-        out_shape=[
-            jax.ShapeDtypeStruct((heads, 128), jnp.int32),
-            jax.ShapeDtypeStruct((PICKS, heads, 128), jnp.float32),
-        ],
-        in_specs=[vmem],
-        out_specs=[vmem] * 2,
-        name="plan",
-    )(block_mask)
     key_args = (far(key_states), key_far, far(value_states), value_far)
 
     def sort_scratch(count, step, kept):
@@ -404,20 +395,22 @@
             dma,
         ]
 
-    early, early_member, column = pl.pallas_call(
+    early, early_member, column, position, bias = pl.pallas_call(
         early_kernel,
         out_shape=[
             hbm_out((EARLY * shard_blocks, 2 * BLOCK, HEAD_DIM), bf16),
             jax.ShapeDtypeStruct((rows, 128), bf16),
             held_out((rows, 128), jnp.int32),
+            jax.ShapeDtypeStruct((heads, 128), jnp.int32),
+            jax.ShapeDtypeStruct((PICKS, heads, 128), jnp.float32),
         ],
-        in_specs=[hbm] * 5,
-        out_specs=[hbm, vmem, vmem],
+        in_specs=[vmem] + [hbm] * 5,
+        out_specs=[hbm] + [vmem] * 4,
         scratch_shapes=[pltpu.VMEM((heads, rows), jnp.int32), pltpu.VMEM((128, rows), jnp.int32)]
         + sort_scratch(EARLY, EARLY, EARLY * shard_blocks),
         compiler_params=limit(24),
         name="early_sort",
-    )(far(cluster_perm), *key_args)
+    )(block_mask, far(cluster_perm), *key_args)
     send, member = pl.pallas_call(
         sort_kernel,
         out_shape=[

time: 154 us -> 152 us (0.987); the launches traced: 155 us -> 149 us
  blocking collectives: 109 us -> 104 us
  Pallas kernels: 27.6 us -> 26 us
    all_to_all x1, blocking collectives: 109 us -> 104 us  [shards(): got = lax.all_to_all(send, 'seq', split_axis=0, concat_axis=0, tiled=True)]
    pallas_call x1 -> x0, Pallas kernels: 1.99 us -> none  [shards(): pl.pallas_call(plan_kernel, out_shape=[jax.ShapeDtypeStruct((heads, 128),...]
  transfers between devices with their start and end apart: 6 -> 6, of which waited for: 2 -> 2; matrix products, arithmetic and copies ran while one was open for 0% -> 0% of each run, Pallas kernels for 12% -> 11%
where the time goes in v8:
time: 152 us; the launch traced here: 149 us
  blocking collectives  104 us (68%)
  Pallas kernels  26 us (17%)
  starting transfers between devices  15.3 us (10%)
  waiting for transfers between devices  2.75 us (2%)
    all_to_all x1, blocking collectives, shards(): got = lax.all_to_all(send, 'seq', split_axis=0, concat_axis=0, tiled=True)  104 us
    all_to_all x1, starting transfers between devices, shards(): lax.all_to_all(table.reshape(seq_count, 1, 128), 'seq', split_axis=0, con...  11.2 us
    pallas_call x1, Pallas kernels, shards(): pl.pallas_call(first_kernel, out_shape=[part(first), part(first), held_ou...  8.21 us
    pallas_call x1, Pallas kernels, shards(): pl.pallas_call(sort_kernel, out_shape=[hbm_out((slots, 2 * BLOCK, HEAD_DI...  6.79 us
    pallas_call x1, Pallas kernels, shards(): pl.pallas_call(early_kernel, out_shape=[hbm_out((EARLY * shard_blocks, 2...  5.03 us
    ppermute x5, starting transfers between devices, swap(): return lax.ppermute(x, 'head', [(0, 1), (1, 0)])  4.07 us
  transfers between devices with their start and end apart: 6, of which 2 were waited for; matrix products, arithmetic and copies ran while one was open for 0% of the time, Pallas kernels for 11%

profile of v8, /device:TPU:1, one launch (start us, length us, event | category | flops | bytes accessed | tf_op | source)
XLA Modules:
  0.0 149.4 jit_solution(2520557040569259070)
XLA Ops:
  0.0 1.4 collective-permute-start
  1.4 0.0 collective-permute-start.1
  1.4 0.5 collective-permute-start.2
  1.9 1.7 %request.1 = s32[64,128]{1,0:T(8,128)} custom-call(s32[20,4,256]{2,1,0:T(4,128)} %mask_ref.3), custom_call_target="tpu_custom_call" | custom-call | tf_op jit(solution)/shard_map/request/pallas_call | solution.py:368
  3.7 11.2 %all-to-all-start = ((s32[64,1,128]{2,1,0:T(1,128)}), s32[64,1,128]{2,1,0:T(1,128)S(1)}, u32[]{:S(2)}, u32[]{:S(2)}) async-start(s32[64,1,128]{2,1,0:T(1,128)} %bitcast.5), calls=%async_computation | async-start | bytes 65536 | tf_op jit(solution)/shard_map/all_to_all | solution.py:375
  14.9 0.0 collective-permute-done.key_far
  14.9 0.0 collective-permute-done.1.value_far
  14.9 0.0 copy-start
  14.9 0.9 copy-done
  15.8 5.0 %early_sort.1 = (bf16[40,256,128]{2,1,0:T(8,128)(2,1)}, bf16[512,128]{1,0:T(8,128)(2,1)S(1)}, s32[512,128]{1,0:T(8,128)S(1)}, s32[20,128]{1,0:T(8,128)S(1)}, f32[4,20,128]{2,1,0:T(8,128)S(1)}) custom-call(s32[20,4,256]{2,1,0:T(4,128)S(1)} %copy-done, s32[20,512]{1,0:T(8,128)} %perm_hbm.1, bf16[256,5120]{1,0:T(8,128)(2,1)} %key_own.3, ...), custom_call_target="tpu_custom_call" | custom-call | tf_op jit(solution)/shard_map/early_sort/pallas_call | solution.py:398
  20.8 2.4 %all-to-all-done = s32[64,1,128]{2,1,0:T(1,128)S(1)} async-done(((s32[64,1,128]{2,1,0:T(1,128)}), s32[64,1,128]{2,1,0:T(1,128)S(1)}, u32[]{:S(2)}, u32[]{:S(2)}) %all-to-all-start) | async-done | bytes 32800 | tf_op jit(solution)/shard_map/all_to_all | solution.py:375
  23.3 6.8 %sort.1 = (bf16[128,256,128]{2,1,0:T(8,128)(2,1)}, bf16[512,128]{1,0:T(8,128)(2,1)S(1)}) custom-call(s32[64,128]{1,0:T(8,128)S(1)} %bitcast.4, s32[512,128]{1,0:T(8,128)S(1)} %get-tuple-element.23.column_ref, bf16[256,5120]{1,0:T(8,128)(2,1)} %key_own.3, bf16[256,5120]{1,0:T(8,128)(2,1)S(1)} %collective-permute-done.key_far, bf16[256,5120]{1,0:T(8,128)(2,1)} %value_own.3, ...), custom_call_target="tpu_custom_call" | custom-call | tf_op jit(solution)/shard_map/sort/pallas_call | solution.py:414
  30.1 0.0 collective-permute-done.2.query_far
  30.1 104.2 %all_to_all.10.got_ref = bf16[128,256,128]{2,1,0:T(8,128)(2,1)} all-to-all(bf16[128,256,128]{2,1,0:T(8,128)(2,1)} %get-tuple-element.34), channel_id=1, replica_groups=mesh['head'=2,'seq'=64] {'seq'}, dimensions={0} | all-to-all | bytes 16777216 | tf_op jit(solution)/shard_map/all_to_all | solution.py:429
  134.3 8.2 %first_heads.1 = (bf16[256,1792]{1,0:T(8,128)(2,1)S(1)}, bf16[256,1792]{1,0:T(8,128)(2,1)S(1)}, bf16[24,256,128]{2,1,0:T(8,128)(2,1)S(1)}, bf16[512,768]{1,0:T(8,128)(2,1)S(1)}) custom-call(s32[20,128]{1,0:T(8,128)S(1)} %get-tuple-element.30.position_ref, bf16[512,128]{1,0:T(8,128)(2,1)S(1)} %get-tuple-element.31.member_ref, ...), custom_call_target="tpu_custom_call" | custom-call | tf_op jit(solution)/shard_map/first_heads/pallas_call | solution.py:433
  142.5 2.0 %collective-permute-start.3 = (bf16[256,1792]{1,0:T(8,128)(2,1)S(1)}, bf16[256,1792]{1,0:T(8,128)(2,1)S(1)}, u32[]{:S(2)}, u32[]{:S(2)}) collective-permute-start(bf16[256,1792]{1,0:T(8,128)(2,1)S(1)} %get-tuple-element.39), channel_id=1, source_target_pairs={{0,64},{64,0},{1,65},{65,1},{2,66},{66,2},{3,67},{67,3},{4,68},{68... | collective-permute-start | bytes 2752520 | tf_op jit(solution)/shard_map/ppermute | solution.py:380
  144.6 2.1 %last_heads.1 = (bf16[256,768]{1,0:T(8,128)(2,1)S(1)}, bf16[256,768]{1,0:T(8,128)(2,1)S(1)}) custom-call(bf16[512,128]{1,0:T(8,128)(2,1)S(1)} %get-tuple-element.31.member_ref, f32[4,20,128]{2,1,0:T(8,128)S(1)} %get-tuple-element.32.bias_ref, bf16[24,256,128]{2,1,0:T(8,128)(2,1)S(1)} %get-tuple-element.36.blocks, bf16[512,768]{1,0:T(8,128)(2,1)S(1)} %get-tuple-element.37.query), custom_call_target="tpu_custom_call" | custom-call | tf_op jit(solution)/shard_map/last_heads/pallas_call | solution.py:453
  146.7 0.1 collective-permute-start.4
  146.7 0.0 collective-permute-done.3.far_first
  146.8 1.4 place.1.out_in
  148.2 0.3 collective-permute-done.4.far_last
  148.5 0.8 place_last.1
Async XLA Ops:
  0.0 14.9 %collective-permute-start = (bf16[256,5120]{1,0:T(8,128)(2,1)}, bf16[256,5120]{1,0:T(8,128)(2,1)S(1)}, u32[]{:S(2)}, u32[]{:S(2)}) collective-permute-start(bf16[256,5120]{1,0:T(8,128)(2,1)} %key_own.3), channel_id=1, source_target_pairs={{0,64},{64,0},{1,65},{65,1},{2,66},{66,2},{3,67},{67,3},{4,68},{68... | collective-permute-start | bytes 7864328 | tf_op jit(solution)/shard_map/ppermute | solution.py:380
  1.4 13.5 %collective-permute-start.1 = (bf16[256,5120]{1,0:T(8,128)(2,1)}, bf16[256,5120]{1,0:T(8,128)(2,1)}, u32[]{:S(2)}, u32[]{:S(2)}) collective-permute-start(bf16[256,5120]{1,0:T(8,128)(2,1)} %value_own.3), channel_id=1, source_target_pairs={{0,64},{64,0},{1,65},{65,1},{2,66},{66,2},{3,67},{67,3},{4,68},{68... | collective-permute-start | bytes 7864328 | tf_op jit(solution)/shard_map/ppermute | solution.py:380
  1.4 28.6 %collective-permute-start.2 = (bf16[256,5120]{1,0:T(8,128)(2,1)}, bf16[256,5120]{1,0:T(8,128)(2,1)}, u32[]{:S(2)}, u32[]{:S(2)}) collective-permute-start(bf16[256,5120]{1,0:T(8,128)(2,1)} %query_own.1), channel_id=1, source_target_pairs={{0,64},{64,0},{1,65},{65,1},{2,66},{66,2},{3,67},{67,3},{4,68},{68... | collective-permute-start | bytes 7864328 | tf_op jit(solution)/shard_map/ppermute | solution.py:380
  3.7 19.6 %all-to-all-start = ((s32[64,1,128]{2,1,0:T(1,128)}), s32[64,1,128]{2,1,0:T(1,128)S(1)}, u32[]{:S(2)}, u32[]{:S(2)}) async-start(s32[64,1,128]{2,1,0:T(1,128)} %bitcast.5), calls=%async_computation | async-start | bytes 65536 | tf_op jit(solution)/shard_map/all_to_all | solution.py:375
  14.9 0.9 copy-start
  142.5 4.2 %collective-permute-start.3 = (bf16[256,1792]{1,0:T(8,128)(2,1)S(1)}, bf16[256,1792]{1,0:T(8,128)(2,1)S(1)}, u32[]{:S(2)}, u32[]{:S(2)}) collective-permute-start(bf16[256,1792]{1,0:T(8,128)(2,1)S(1)} %get-tuple-element.39), channel_id=1, source_target_pairs={{0,64},{64,0},{1,65},{65,1},{2,66},{66,2},{3,67},{67,3},{4,68},{68... | collective-permute-start | bytes 2752520 | tf_op jit(solution)/shard_map/ppermute | solution.py:380
  146.7 1.8 %collective-permute-start.4 = (bf16[256,768]{1,0:T(8,128)(2,1)S(1)}, bf16[256,768]{1,0:T(8,128)(2,1)S(1)}, u32[]{:S(2)}, u32[]{:S(2)}) collective-permute-start(bf16[256,768]{1,0:T(8,128)(2,1)S(1)} %get-tuple-element.40), channel_id=1, source_target_pairs={{0,64},{64,0},{1,65},{65,1},{2,66},{66,2},{3,67},{67,3},{4,68},{68... | collective-permute-start | bytes 1179656 | tf_op jit(solution)/shard_map/ppermute | solution.py:380
